TPU v7x, 128 devices: a whole 4x4x4 slice. The times are simulated.
128 devices in a mesh: body: 2 (over core), dom: 64 (over z, x, y).
Axes of the slice: x: 4, y: 4, z: 4, core: 2. Of those that a mesh axis runs over, the one named last changes fastest.
Arguments:
- displacement: float32 [2, 3, 262144], P('body', None, 'dom'), may hold values from -6 to 6
- connectivity: int32 [2, 8, 262144], P('body', None, 'dom'), may hold values from 0 to 4096
- plastic_strain: float32 [2, 6, 262144], P('body', None, 'dom'), may hold values from -4 to 4
- element_size: float32 [2, 262144], P('body', 'dom'), may hold values from 0.5 to 2
- yield_stress: float32 [2, 262144], P('body', 'dom'), may hold values from 0.3 to 3
- external_force: float32 [2, 3, 262144], P('body', None, 'dom'), may hold values from -12 to 12
- slave_disp: bfloat16 [2, 8192, 3, 128], P('body', 'dom'), may hold values from -6 to 6
- pair_owner: int32 [2, 8192, 2], P('body', 'dom'), may hold values from 0 to 63, all different within a row; in each aligned block of 128 rows (0 to 127, 128 to 255, ..., all dimensions but the last counted through in order) at most 8 rows name the same one
- pair_local: int32 [2, 8192, 2], P('body', 'dom'), may hold values from 0 to 127
- active: int32 [2, 8192], P('body', 'dom'), may hold values 0 or 1
- master_gap: float32 [2, 8192, 128], P('body', 'dom'), may hold values from -6 to 6
- master_normal: float32 [2, 8192, 3, 128], P('body', 'dom'), may hold values from -4 to 4
- master_disp: bfloat16 [2, 8192, 3, 128], P('body', 'dom'), may hold values from -6 to 6
- coupling: bfloat16 [128, 128], replicated, may hold values from -0.25 to 0.25
- quad_weight: float32 [128], replicated, may hold values from 0.1 to 1.9
Outputs:
- residual: float32 [2, 3, 262144], P('body', None, 'dom')
- slave_force: float32 [2, 8192, 3, 128], P('body', 'dom')
- master_force: float32 [2, 8192, 3, 128], P('body', 'dom')
Inputs may be any that keep to these rules, and one draw needn't show every extreme that they name: `pair_owner`: among the rows of one device, at most 8 pairings name the same owner, a bound that some block reaches; a segment's two pairings name different owners.
All inputs are finite; a program needn't handle non-finite values. No bound on the sum of `active` on one device may be relied on, other than what follows from the above.
Results may differ from a plain program's by a relative error of at most 0.0055.
Values may be sent and summed in bfloat16 or wider, within the bound.
No kernel may reach another device: no remote copies, remote signals or barrier semaphores. Data moves between devices by JAX's collectives and lax.ppermute only.
A program may use at most 128 MiB of HBM per device.

v0:
```python
import jax
import jax.numpy as jnp
import numpy as np
from jax import lax
from jax.sharding import PartitionSpec as P

GHOST = 2048


LAME_A = 1.0
LAME_B = 0.5
PENALTY = 2.0


def padded(block, sides, width):
    for axis, dim in sides:
        count = lax.axis_size(axis)
        forward = [(i, i + 1) for i in range(count - 1)]
        backward = [(target, source) for source, target in forward]
        low = lax.ppermute(
            lax.slice_in_dim(block, block.shape[dim] - width, None, axis=dim), axis, forward
        )
        high = lax.ppermute(lax.slice_in_dim(block, 0, width, axis=dim), axis, backward)
        block = jnp.concatenate([low, block, high], axis=dim)
    return block


def shifted(block, axis, distance):
    devices = range(lax.axis_size(axis))
    route = [(i - distance, i) for i in devices if i - distance in devices]
    return lax.ppermute(block, axis, route)


def corner_table():
    rows = [[(2.0 * (a >> j & 1) - 1.0) / 4.0 for j in range(3)] for a in range(8)]
    return jnp.asarray(np.array(rows, dtype=np.float32))


def element_forces(nodal, strain_old, edge, yield_val):
    table = corner_table().astype(nodal.dtype)
    grad = jnp.einsum("iae,aj->ije", nodal, table, precision=lax.Precision.HIGHEST) / edge
    exx = grad[0, 0] - strain_old[0]
    eyy = grad[1, 1] - strain_old[1]
    ezz = grad[2, 2] - strain_old[2]
    exy = 0.5 * (grad[0, 1] + grad[1, 0]) - strain_old[3]
    eyz = 0.5 * (grad[1, 2] + grad[2, 1]) - strain_old[4]
    ezx = 0.5 * (grad[2, 0] + grad[0, 2]) - strain_old[5]
    trace = exx + eyy + ezz
    sxx = LAME_A * trace + 2.0 * LAME_B * exx
    syy = LAME_A * trace + 2.0 * LAME_B * eyy
    szz = LAME_A * trace + 2.0 * LAME_B * ezz
    sxy = 2.0 * LAME_B * exy
    syz = 2.0 * LAME_B * eyz
    szx = 2.0 * LAME_B * ezx
    mean = (sxx + syy + szz) / 3.0
    dxx, dyy, dzz = (sxx - mean, syy - mean, szz - mean)
    norm_dev = jnp.sqrt(
        dxx * dxx + dyy * dyy + dzz * dzz + 2.0 * (sxy * sxy + syz * syz + szx * szx)
    )
    radius = jnp.sqrt(2.0 / 3.0) * yield_val
    factor = radius / jnp.maximum(norm_dev, radius)
    row_x = jnp.stack([mean + factor * dxx, factor * sxy, factor * szx])
    row_y = jnp.stack([factor * sxy, mean + factor * dyy, factor * syz])
    row_z = jnp.stack([factor * szx, factor * syz, mean + factor * dzz])
    stress = jnp.stack([row_x, row_y, row_z])
    return edge * edge * jnp.einsum("ije,aj->iae", stress, table, precision=lax.Precision.HIGHEST)


def at_masters(got_disp, got_meta, gap_rows, normal_rows, mdisp_rows, mortar, weights):
    blocks, slots = (got_disp.shape[0], got_disp.shape[1])
    points = got_disp.shape[3]
    disp = got_disp.reshape(blocks * slots, 3, points)
    where = got_meta[:, :, 0].reshape(-1)
    flag = got_meta[:, :, 1].reshape(-1).astype(jnp.float32)
    proj = jnp.einsum("scp,pq->scq", disp, mortar, preferred_element_type=jnp.float32)
    normal = normal_rows[where]
    gap = gap_rows[where] - jnp.sum(normal * (proj - mdisp_rows[where].astype(jnp.float32)), axis=1)
    press = PENALTY * jnp.maximum(gap, 0.0) * flag[:, None]
    traction = weights * press[:, None, :] * normal
    master_sum = jnp.zeros(normal_rows.shape, jnp.float32).at[where].add(-traction)
    return (traction.reshape(blocks, slots, 3, points), master_sum)


def local(
    displacement,
    connectivity,
    plastic_strain,
    element_size,
    yield_stress,
    external_force,
    slave_disp,
    pair_owner,
    pair_local,
    active,
    master_gap,
    master_normal,
    master_disp,
    coupling,
    quad_weight,
):
    node_count = displacement.shape[2]
    extended = padded(displacement[0], (("dom", 1),), GHOST)
    links = connectivity[0] + jnp.arange(node_count, dtype=jnp.int32)[None, :]
    nodal = extended[:, links]
    forces = element_forces(nodal, plastic_strain[0], element_size[0], yield_stress[0])
    assembled = jnp.zeros(extended.shape, jnp.float32).at[:, links].add(forces)
    own = assembled[:, GHOST : GHOST + node_count]
    from_next = shifted(assembled[:, :GHOST], "dom", -1)
    from_prev = shifted(assembled[:, GHOST + node_count :], "dom", 1)
    own = own.at[:, node_count - GHOST :].add(from_next)
    own = own.at[:, :GHOST].add(from_prev)
    residual = own - external_force[0]
    points = slave_disp.shape[3]
    seg = slave_disp.shape[1]
    peers = lax.axis_size("dom")
    slots = max(2, 4 * seg // peers)
    mortar = (jnp.eye(points, dtype=jnp.float32) + coupling.astype(jnp.float32)).astype(
        jnp.bfloat16
    )
    owner_rows = pair_owner[0].reshape(-1)
    local_rows = pair_local[0].reshape(-1)
    flag_rows = jnp.repeat(active[0], 2)
    disp_rows = jnp.repeat(slave_disp[0], 2, axis=0)
    meta_rows = jnp.stack([local_rows, flag_rows], axis=1)
    onehot = (owner_rows[:, None] == jnp.arange(peers, dtype=jnp.int32)[None, :]).astype(jnp.int32)
    before = jnp.cumsum(onehot, axis=0) - onehot
    rank = jnp.sum(before * onehot, axis=1)
    gap_rows, normal_rows, mdisp_rows = (master_gap[0], master_normal[0], master_disp[0])
    side = lax.axis_index("body")
    start = (1 - side) * peers
    target = start + owner_rows
    send_disp = (
        jnp.zeros((2 * peers, slots, 3, points), jnp.bfloat16).at[target, rank].set(disp_rows)
    )
    send_meta = jnp.zeros((2 * peers, slots, 2), jnp.int32).at[target, rank].set(meta_rows)
    got_disp, got_meta = (
        lax.all_to_all(send_disp, ("body", "dom"), split_axis=0, concat_axis=0, tiled=True),
        lax.all_to_all(send_meta, ("body", "dom"), split_axis=0, concat_axis=0, tiled=True),
    )
    got_disp = lax.dynamic_slice_in_dim(got_disp, start, peers, 0)
    got_meta = lax.dynamic_slice_in_dim(got_meta, start, peers, 0)
    traction, master_sum = at_masters(
        got_disp, got_meta, gap_rows, normal_rows, mdisp_rows, mortar, quad_weight
    )
    outgoing = jnp.zeros((2 * peers, slots, 3, points), jnp.float32)
    outgoing = lax.dynamic_update_slice_in_dim(outgoing, traction, start, 0)
    returned = lax.all_to_all(outgoing, ("body", "dom"), split_axis=0, concat_axis=0, tiled=True)
    returned = lax.dynamic_slice_in_dim(returned, start, peers, 0)
    pair_rows = returned[owner_rows, rank]
    pair_sum = jnp.sum(pair_rows.reshape(seg, 2, 3, points), axis=1).astype(jnp.bfloat16)
    slave_force = jnp.einsum("scq,pq->scp", pair_sum, mortar, preferred_element_type=jnp.float32)
    return (residual[None], slave_force[None], master_sum[None])


def solution(mesh):
    return jax.shard_map(
        local,
        mesh=mesh,
        in_specs=(
            P("body", None, "dom"),
            P("body", None, "dom"),
            P("body", None, "dom"),
            P("body", "dom"),
            P("body", "dom"),
            P("body", None, "dom"),
            P("body", "dom", None, None),
            P("body", "dom", None),
            P("body", "dom", None),
            P("body", "dom"),
            P("body", "dom", None),
            P("body", "dom", None, None),
            P("body", "dom", None, None),
            P(),
            P(),
        ),
        out_specs=(
            P("body", None, "dom"),
            P("body", "dom", None, None),
            P("body", "dom", None, None),
        ),
        check_vma=False,
    )
```

profile of v0, /device:TPU:30, one launch (start us, length us, event | category | flops | bytes accessed | tf_op | source)
XLA Modules:
  0.0 439.8 jit_solution(2160516460994864321)
XLA Ops:
  0.6 0.9 copy.182
  1.5 3.4 collective-permute-start
  4.9 2.4 collective-permute-start.1
  7.4 0.8 copy.133
  8.6 0.6 reduce-window.6
  9.5 0.7 broadcast_in_dim.24
  10.4 0.8 copy.137
  11.6 11.5 %scatter_fusion = s32[128,8,2]{2,1,0:T(8,128)S(1)} fusion(s32[128,8,2]{2,1,0:T(8,128)S(1)} %broadcast_in_dim.23, s32[256]{0:T(256)S(1)} %bitcast.172, s32[256,2]{1,0:T(8,128)S(1)} %copy.138), kind=kCustom, calls=%fused_computation.6 | custom fusion | bytes 8192 | tf_op jit(solution)/shard_map/scatter | solution.py:135
  23.2 1.5 copy.139
  24.6 10.2 %all-to-all-start = ((s32[128,8,2]{1,2,0:T(2,128)}), s32[128,8,2]{1,2,0:T(2,128)S(1)}, u32[]{:S(2)}, u32[]{:S(2)}) async-start(s32[128,8,2]{1,2,0:T(2,128)} %copy.139), calls=%async_computation | async-start | bytes 262144 | tf_op jit(solution)/shard_map/all_to_all | solution.py:138
  35.0 2.0 copy.132
  37.7 9.8 %scatter_fusion.1 = bf16[128,8,3,128]{3,2,1,0:T(4,128)(2,1)S(1)} fusion(bf16[128,8,3,128]{3,2,1,0:T(4,128)(2,1)S(1)} %broadcast_in_dim.25, s32[256]{0:T(256)S(1)} %bitcast.173, bf16[256,3,128]{2,1,0:T(4,128)(2,1)S(1)} %bitcast.181), kind=kCustom, calls=%fused_computation.7 | custom fusion | bytes 591872 | tf_op jit(solution)/shard_map/scatter | solution.py:133
  47.5 1.0 copy.144
  48.5 0.6 compare_reduce_fusion
  49.1 10.2 %all-to-all-start.1 = ((bf16[128,8,3,128]{3,1,2,0:T(8,128)(2,1)}), bf16[128,8,3,128]{3,1,2,0:T(8,128)(2,1)}, u32[]{:S(2)}, u32[]{:S(2)}) async-start(bf16[128,8,3,128]{3,1,2,0:T(8,128)(2,1)} %copy.144), calls=%async_computation.1 | async-start | bytes 1572864 | tf_op jit(solution)/shard_map/all_to_all | solution.py:137
  59.7 2.6 copy.118
  62.3 111.2 %gather_fusion = f32[32768,3]{1,0:T(8,128)} fusion(f32[3,8192]{0,1:T(8,128)} %copy.118, s32[32768]{0:T(1024)S(1)} %broadcast_clamp_fusion), kind=kCustom, calls=%fused_computation | custom fusion | bytes 917504 | tf_op jit(solution)/shard_map/gather | solution.py:104
  173.5 9.8 %copy.119 = f32[8,4096,3]{1,0,2:T(8,128)S(1)} copy(f32[8,4096,3]{2,1,0:T(8,128)} %bitcast.174) | data formatting | bytes 786432 | tf_op jit(solution)/shard_map/gather | solution.py:104
  183.3 0.5 fusion.1
  184.3 0.5 fusion
  184.8 8.6 %copy.156 = f32[8,4096,3]{2,1,0:T(8,128)} copy(f32[8,4096,3]{1,0,2:T(8,128)S(1)} %fusion) | data formatting | bytes 786432 | tf_op jit(solution)/shard_map/mul | solution.py:66
  193.4 176.4 %scatter_custom_fusion = f32[3,8192]{0,1:T(8,128)} fusion(s32[32768]{0:T(1024)S(1)} %bitcast.185, f32[32768,3]{1,0:T(8,128)} %bitcast.176, f32[]{:T(128)} %constant.88.clone.1), kind=kCustom, calls=%fused_computation.15 | custom fusion | flops 98304 | bytes 98816 | tf_op jit(solution)/shard_map/scatter-add | solution.py:106
  369.8 3.0 fusion.54
  372.9 0.3 copy.127
  373.2 2.7 collective-permute-start.2
  375.9 0.3 copy.130
  376.2 7.5 %collective-permute-start.3 = (f32[3,2048]{1,0:T(4,128)S(1)}, f32[3,2048]{1,0:T(4,128)S(1)}, u32[]{:S(2)}, u32[]{:S(2)}) collective-permute-start(f32[3,2048]{1,0:T(4,128)S(1)} %copy.130), channel_id=1, source_target_pairs={{0,1},{1,2},{2,3},{3,4},{4,5},{5,6},{6,7},{7,8},{8,9},{9,10},{10,1... | collective-permute-start | bytes 73736 | tf_op jit(solution)/shard_map/ppermute | solution.py:31
  383.8 2.1 gather_fusion.2
  385.9 2.6 gather_fusion.3
  388.4 1.6 gather_fusion.1
  390.3 1.7 copy.128
  392.1 1.4 copy.129
  393.4 1.4 copy.131
  394.8 1.4 constant_dynamic-update-slice_fusion
  396.4 1.0 fusion.7
  397.4 1.5 fusion.6
  398.9 1.1 fusion.12
  400.0 1.3 broadcast_in_dim.22
  401.3 1.0 fusion.8
  402.3 9.7 %all-to-all-start.2 = ((f32[128,8,3,128]{3,1,2,0:T(8,128)}), f32[128,8,3,128]{3,1,2,0:T(8,128)}, u32[]{:S(2)}, u32[]{:S(2)}) async-start(f32[128,8,3,128]{3,1,2,0:T(8,128)} %fusion.8), calls=%async_computation.2 | async-start | bytes 3145728 | tf_op jit(solution)/shard_map/all_to_all | solution.py:147
  411.9 3.1 fusion.2
  415.1 2.9 copy.154
  418.1 0.4 multiply_negate_fusion
  418.5 16.9 %scatter_fusion.2 = f32[128,3,128]{2,1,0:T(4,128)S(1)} fusion(f32[128,3,128]{2,1,0:T(4,128)S(1)} %broadcast_in_dim.56, s32[512]{0:T(512)S(1)} %bitcast.191, f32[512,3,128]{2,1,0:T(4,128)S(1)} %multiply_negate_fusion), kind=kCustom, calls=%fused_computation.8 | custom fusion | flops 196608 | bytes 2361344 | tf_op jit(solution)/shard_map/scatter-add | solution.py:80
  435.4 0.7 copy.155
  436.1 1.2 constant_dynamic-slice_fusion
  437.6 1.3 gather_fusion.4
  439.0 0.9 convolution_bitcast_fusion
  (79 shorter events, 3.9 us)
Async XLA Ops:
  0.6 387.8 %copy-start = (f32[1,128,128]{2,1,0:T(8,128)S(1)}, f32[1,128,128]{2,1,0:T(8,128)}, u32[]{:S(2)}) copy-start(f32[1,128,128]{2,1,0:T(8,128)} %param.30) | copy-start | bytes 196612
  1.5 58.1 %collective-permute-start = (f32[3,2048]{1,0:T(4,128)S(1)}, f32[3,2048]{1,0:T(4,128)S(1)}, u32[]{:S(2)}, u32[]{:S(2)}) collective-permute-start(f32[3,2048]{1,0:T(4,128)S(1)} %get-tuple-element.57), channel_id=1, source_target_pairs={{0,1},{1,2},{2,3},{3,4},{4,5},{5,6},{6,7},{7,8},{8,9},{9,10},{10,1... | collective-permute-start | bytes 73736 | tf_op jit(solution)/shard_map/ppermute | solution.py:20
  4.9 54.7 %collective-permute-start.1 = (f32[3,2048]{1,0:T(4,128)S(1)}, f32[3,2048]{1,0:T(4,128)S(1)}, u32[]{:S(2)}, u32[]{:S(2)}) collective-permute-start(f32[3,2048]{1,0:T(4,128)S(1)} %get-tuple-element.58), channel_id=1, source_target_pairs={{1,0},{2,1},{3,2},{4,3},{5,4},{6,5},{7,6},{8,7},{9,8},{10,9},{11,1... | collective-permute-start | bytes 73736 | tf_op jit(solution)/shard_map/ppermute | solution.py:23
  10.2 24.7 %copy-start.5 = (s32[1,8,4096]{2,1,0:T(8,128)S(1)}, s32[1,8,4096]{2,1,0:T(8,128)}, u32[]{:S(2)}) copy-start(s32[1,8,4096]{2,1,0:T(8,128)} %param.21) | copy-start | bytes 393220
  11.6 23.4 %copy-start.9 = (f32[1,4096]{1,0:T(1,128)S(1)}, f32[1,4096]{1,0:T(1,128)}, u32[]{:S(2)}) copy-start(f32[1,4096]{1,0:T(1,128)} %param.23) | copy-start | bytes 49156
  11.6 23.4 %copy-start.10 = (f32[1,3,4096]{2,0,1:T(1,128)S(1)}, f32[1,3,4096]{2,0,1:T(1,128)}, u32[]{:S(2)}) copy-start(f32[1,3,4096]{2,0,1:T(1,128)} %param.25) | copy-start | bytes 147460
  23.1 13.9 %copy-start.3 = (f32[1,128,3,128]{3,1,2,0:T(8,128)S(1)}, f32[1,128,3,128]{3,1,2,0:T(8,128)}, u32[]{:S(2)}) copy-start(f32[1,128,3,128]{3,1,2,0:T(8,128)} %param.31) | copy-start | bytes 589828
  23.2 14.0 %copy-start.6 = (bf16[1,128,3,128]{3,1,2,0:T(8,128)(2,1)S(1)}, bf16[1,128,3,128]{3,1,2,0:T(8,128)(2,1)}, u32[]{:S(2)}) copy-start(bf16[1,128,3,128]{3,1,2,0:T(8,128)(2,1)} %param.32) | copy-start | bytes 294916
  24.6 12.6 %copy-start.7 = (bf16[1,128,3,128]{3,1,2,0:T(8,128)(2,1)S(1)}, bf16[1,128,3,128]{3,1,2,0:T(8,128)(2,1)}, u32[]{:S(2)}) copy-start(bf16[1,128,3,128]{3,1,2,0:T(8,128)(2,1)} %param.26) | copy-start | bytes 294916
  24.6 24.5 %all-to-all-start = ((s32[128,8,2]{1,2,0:T(2,128)}), s32[128,8,2]{1,2,0:T(2,128)S(1)}, u32[]{:S(2)}, u32[]{:S(2)}) async-start(s32[128,8,2]{1,2,0:T(2,128)} %copy.139), calls=%async_computation | async-start | bytes 262144 | tf_op jit(solution)/shard_map/all_to_all | solution.py:138
  49.1 348.2 %all-to-all-start.1 = ((bf16[128,8,3,128]{3,1,2,0:T(8,128)(2,1)}), bf16[128,8,3,128]{3,1,2,0:T(8,128)(2,1)}, u32[]{:S(2)}, u32[]{:S(2)}) async-start(bf16[128,8,3,128]{3,1,2,0:T(8,128)(2,1)} %copy.144), calls=%async_computation.1 | async-start | bytes 1572864 | tf_op jit(solution)/shard_map/all_to_all | solution.py:137
  173.5 9.8 %copy-start.12 = (f32[8,3,1]{0,1,2:T(4,128)S(1)}, f32[8,3,1]{0,1,2:T(4,128)}, u32[]{:S(2)}) copy-start(f32[8,3,1]{0,1,2:T(4,128)} %constant.163) | copy-start | bytes 292
  173.5 10.3 %copy-start.8 = (f32[1,6,4096]{2,0,1:T(1,128)S(1)}, f32[1,6,4096]{2,0,1:T(1,128)}, u32[]{:S(2)}) copy-start(f32[1,6,4096]{2,0,1:T(1,128)} %param.22) | copy-start | bytes 294916
  173.5 10.3 %copy-start.11 = (f32[1,4096]{1,0:T(1,128)S(1)}, f32[1,4096]{1,0:T(1,128)}, u32[]{:S(2)}) copy-start(f32[1,4096]{1,0:T(1,128)} %param.24) | copy-start | bytes 49156
  373.2 18.8 %collective-permute-start.2 = (f32[3,2048]{1,0:T(4,128)S(1)}, f32[3,2048]{1,0:T(4,128)S(1)}, u32[]{:S(2)}, u32[]{:S(2)}) collective-permute-start(f32[3,2048]{1,0:T(4,128)S(1)} %copy.127), channel_id=1, source_target_pairs={{1,0},{2,1},{3,2},{4,3},{5,4},{6,5},{7,6},{8,7},{9,8},{10,9},{11,1... | collective-permute-start | bytes 73736 | tf_op jit(solution)/shard_map/ppermute | solution.py:31
  376.2 17.2 %collective-permute-start.3 = (f32[3,2048]{1,0:T(4,128)S(1)}, f32[3,2048]{1,0:T(4,128)S(1)}, u32[]{:S(2)}, u32[]{:S(2)}) collective-permute-start(f32[3,2048]{1,0:T(4,128)S(1)} %copy.130), channel_id=1, source_target_pairs={{0,1},{1,2},{2,3},{3,4},{4,5},{5,6},{6,7},{7,8},{8,9},{9,10},{10,1... | collective-permute-start | bytes 73736 | tf_op jit(solution)/shard_map/ppermute | solution.py:31
  390.3 4.5 %slice-start = ((f32[3,8192]{0,1:T(8,128)}), f32[3,4096]{0,1:T(8,128)S(1)}, s32[]{:S(2)}) async-start(f32[3,8192]{0,1:T(8,128)} %scatter_custom_fusion), calls=%async_computation.3 | async-start | bytes 4194304 | tf_op jit(solution)/shard_map/slice | solution.py:107
  394.8 1.5 copy-start.1
  396.4 1.0 copy-start.4
  396.4 2.5 copy-start.13
  402.3 33.8 %all-to-all-start.2 = ((f32[128,8,3,128]{3,1,2,0:T(8,128)}), f32[128,8,3,128]{3,1,2,0:T(8,128)}, u32[]{:S(2)}, u32[]{:S(2)}) async-start(f32[128,8,3,128]{3,1,2,0:T(8,128)} %fusion.8), calls=%async_computation.2 | async-start | bytes 3145728 | tf_op jit(solution)/shard_map/all_to_all | solution.py:147
  415.1 2.9 copy-start.2
where the time goes:
time: 443 us; the launch traced here: 440 us
  other arithmetic  202 us (46%)
  local copies, waits for them, and re-layouts  187 us (42%)
  starting transfers between devices  46.1 us (10%)
    scatter-add x1, other arithmetic, local(): assembled = jnp.zeros(extended.shape, jnp.float32).at[:, links].add(forces)  176 us
    gather x2, local copies, waits for them, and re-layouts, local(): nodal = extended[:, links]  121 us
    scatter-add x1, other arithmetic, at_masters(): jnp.zeros(normal_rows.shape, jnp.float32).at[where].add(-traction)  16.9 us
    scatter x2, local copies, waits for them, and re-layouts, local(): jnp.zeros((2 * peers, slots, 2), jnp.int32).at[target, rank].set(meta_rows)  13 us
    scatter x2, local copies, waits for them, and re-layouts, local(): jnp.zeros((2 * peers, slots, 3, points), jnp.bfloat16).at[target, rank]  10.8 us
    ppermute x2, starting transfers between devices, shifted(): return lax.ppermute(block, axis, route)  10.2 us
    all_to_all x1, starting transfers between devices, local(): lax.all_to_all(send_meta, ('body', 'dom'), split_axis=0, concat_axis=0, t...  10.2 us
    all_to_all x1, starting transfers between devices, local(): lax.all_to_all(send_disp, ('body', 'dom'), split_axis=0, concat_axis=0, t...  10.2 us
  transfers between devices with their start and end apart: 7, of which 0 were waited for; matrix products, arithmetic and copies ran while one was open for 87% of the time, Pallas kernels for 0%

commit v1 on v0

v1 whole, which is shorter than its diff:
```python
import functools

import jax
import jax.numpy as jnp
import numpy as np
from jax import lax
from jax.experimental import pallas as pl
from jax.experimental.pallas import tpu as pltpu
from jax.sharding import PartitionSpec as P

LANES = 128
WINDOW = 40
HALO = 16
BLOCKS = 32
SLOTS = 8
PEERS = 64
SEG = 128
F32 = jnp.float32
BF16 = jnp.bfloat16
NT = (((1,), (1,)), ((), ()))
TN = (((0,), (0,)), ((), ()))
NN = (((1,), (0,)), ((), ()))


def dot(a, b, dims=NN):
    return lax.dot_general(a, b, dims, preferred_element_type=F32)


def iota(shape, dim, dtype=jnp.int32):
    return lax.broadcasted_iota(jnp.int32, shape, dim).astype(dtype)


def element_kernel(low, own, high, links, strain, edge_ref, yield_ref, ext, prev_out, next_out, own_out,
                   disp, lo_s, hi_s, force_s, acc):
    disp[:, 0:HALO, :] = low[...]
    disp[:, HALO : HALO + BLOCKS, :] = own[...]
    disp[:, HALO + BLOCKS : 2 * HALO + BLOCKS, :] = high[...]
    acc[...] = jnp.zeros_like(acc)
    lane = iota((8, LANES), 1)
    for m in range(BLOCKS // 8):
        nodal = []
        for a in range(8):
            reach = links[pl.ds(64 * m + a, 8, stride=8), :] + lane
            hi = reach >> 7
            lo = reach & 127
            lo_s[a * BLOCKS + 8 * m : a * BLOCKS + 8 * m + 8, :] = lo
            hi_s[a * BLOCKS + 8 * m : a * BLOCKS + 8 * m + 8, :] = hi
            got = [jnp.zeros((8, LANES), F32)] * 3
            for h in range(33):
                here = hi == h
                for i in range(3):
                    rows = disp[i, 8 * m + h : 8 * m + h + 8, :]
                    got[i] = jnp.where(here, jnp.take_along_axis(rows, lo, axis=1), got[i])
            nodal.append(got)
        edge = edge_ref[8 * m : 8 * m + 8, :]
        scale = 0.25 / edge
        grad = [[None] * 3 for _ in range(3)]
        for i in range(3):
            u = [nodal[a][i] for a in range(8)]
            for j in range(3):
                plus = [u[a] for a in range(8) if a >> j & 1]
                minus = [u[a] for a in range(8) if not a >> j & 1]
                total = sum(p - q for p, q in zip(plus, minus))
                grad[i][j] = total * scale
        old = [strain[c, 8 * m : 8 * m + 8, :] for c in range(6)]
        exx = grad[0][0] - old[0]
        eyy = grad[1][1] - old[1]
        ezz = grad[2][2] - old[2]
        exy = 0.5 * (grad[0][1] + grad[1][0]) - old[3]
        eyz = 0.5 * (grad[1][2] + grad[2][1]) - old[4]
        ezx = 0.5 * (grad[2][0] + grad[0][2]) - old[5]
        trace = exx + eyy + ezz
        sxx = trace + exx
        syy = trace + eyy
        szz = trace + ezz
        mean = (sxx + syy + szz) / 3.0
        dxx, dyy, dzz = sxx - mean, syy - mean, szz - mean
        size = jnp.sqrt(dxx * dxx + dyy * dyy + dzz * dzz + 2.0 * (exy * exy + eyz * eyz + ezx * ezx))
        radius = np.float32(np.sqrt(2.0 / 3.0)) * yield_ref[8 * m : 8 * m + 8, :]
        factor = radius / jnp.maximum(size, radius)
        area = 0.25 * edge * edge
        xy, yz, zx = area * factor * exy, area * factor * eyz, area * factor * ezx
        xx = area * (mean + factor * dxx)
        yy = area * (mean + factor * dyy)
        zz = area * (mean + factor * dzz)
        for i, (tx, ty, tz) in enumerate(((xx, xy, zx), (xy, yy, yz), (zx, yz, zz))):
            four = [tx + ty, ty - tx, tx - ty, -tx - ty]
            for a in range(8):
                pick = four[(0 if a & 1 else 1) if a & 2 else (2 if a & 1 else 3)]
                f = pick + tz if a & 4 else pick - tz
                force_s[i, a * BLOCKS + 8 * m : a * BLOCKS + 8 * m + 8, :] = f
    row = iota((WINDOW, LANES), 0)
    row_lane = iota((LANES, LANES), 0)
    for k in range(BLOCKS):
        left, right = [], []
        for a in range(8):
            r = a * BLOCKS + k
            hi = jnp.broadcast_to(hi_s[r : r + 1, :], (WINDOW, LANES))
            lo = jnp.broadcast_to(lo_s[r : r + 1, :], (LANES, LANES))
            here = hi == row
            parts = [
                jnp.where(here, jnp.broadcast_to(force_s[i, r : r + 1, :], (WINDOW, LANES)), 0.0) for i in range(3)
            ]
            left.append(jnp.concatenate(parts, axis=0).astype(BF16))
            right.append(jnp.where(lo == row_lane, 1.0, 0.0).astype(BF16))
        sums = dot(jnp.concatenate(left, axis=1), jnp.concatenate(right, axis=1), NT)
        for i in range(3):
            acc[i, k : k + WINDOW, :] += sums[i * WINDOW : (i + 1) * WINDOW]
    prev_out[...] = acc[:, 0:HALO, :]
    next_out[...] = acc[:, HALO + BLOCKS : 2 * HALO + BLOCKS, :]
    own_out[...] = acc[:, HALO : HALO + BLOCKS, :] - ext[...]


def finish_kernel(own, from_prev, from_next, out):
    out[:, 0:HALO, :] = own[:, 0:HALO, :] + from_prev[...]
    out[:, HALO:BLOCKS, :] = own[:, HALO:BLOCKS, :] + from_next[...]


def pack_kernel(owner, where, active, disp, send, place):
    names = iota((PEERS, SEG), 0)
    earlier = jnp.where(iota((SEG, SEG), 0) < iota((SEG, SEG), 1), 1.0, 0.0).astype(BF16)
    ones = jnp.ones((SEG, SEG), BF16)
    hot = [owner[k : k + 1, :] == names for k in range(2)]
    hot16 = [jnp.where(h, 1.0, 0.0).astype(BF16) for h in hot]
    before = [dot(hot16[0], earlier), dot(hot16[1], earlier) + dot(hot16[0], ones)]
    slots = iota((PEERS * SLOTS, SEG), 0)
    sent = jnp.zeros((PEERS * SLOTS, SEG), F32)
    meta = jnp.zeros((PEERS * SLOTS, SEG), F32)
    for k in range(2):
        rank = jnp.sum(jnp.where(hot[k], before[k], 0.0), axis=0, keepdims=True)
        slot = owner[k : k + 1, :] * SLOTS + rank.astype(jnp.int32)
        mark = ((where[k : k + 1, :] + 1) * active[...]).astype(F32)
        here = slot == slots
        sent = jnp.where(here, 1.0, sent)
        meta = jnp.where(here, mark, meta)
    sent = sent.astype(BF16)
    place[...] = sent
    for c in range(3):
        send[:, c * LANES : (c + 1) * LANES] = dot(sent, disp[c]).astype(BF16)
    send[:, 3 * LANES :] = dot(meta.astype(BF16), ones).astype(BF16)


def rows_kernel(gap, normal, mdisp, out):
    total = gap[...]
    for c in range(3):
        n = normal[c]
        total = total + n * mdisp[c].astype(F32)
        out[1 + c] = n
    out[0] = total


def mortar_of(coupling):
    eye = jnp.where(iota((LANES, LANES), 0) == iota((LANES, LANES), 1), 1.0, 0.0)
    return (eye + coupling[...].astype(F32)).astype(BF16)


def split(x):
    top = x.astype(BF16)
    return top, (x - top.astype(F32)).astype(BF16)


def master_kernel(got, rows, coupling, weight, back, force):
    mortar = mortar_of(coupling)
    table = [split(rows[c]) for c in range(4)]
    name = iota((SEG, LANES), 1, F32) + 1.0
    totals = [jnp.zeros((SEG, LANES), F32)] * 3
    for part in range(PEERS * SLOTS // SEG):
        span = slice(part * SEG, (part + 1) * SEG)
        hot = jnp.where(got[span, 3 * LANES :].astype(F32) == name, 1.0, 0.0).astype(BF16)
        gap, n0, n1, n2 = (dot(hot, t) + dot(hot, b) for t, b in table)
        normal = (n0, n1, n2)
        for c in range(3):
            gap = gap - normal[c] * dot(got[span, c * LANES : (c + 1) * LANES], mortar)
        press = weight[...] * (2.0 * jnp.maximum(gap, 0.0))
        for c in range(3):
            top, low = split(press * normal[c])
            back[span, c * LANES : (c + 1) * LANES] = top
            totals[c] = totals[c] + dot(hot, top, TN) + dot(hot, low, TN)
    for c in range(3):
        force[c] = -totals[c]


def slave_kernel(got, place, coupling, out):
    mortar = mortar_of(coupling)
    for c in range(3):
        pair = dot(place[...], got[:, c * LANES : (c + 1) * LANES], TN).astype(BF16)
        out[c] = dot(pair, mortar, NT)


def shape(*dims, dtype=F32):
    return jax.ShapeDtypeStruct(dims, dtype)


def call(kernel, outs, cost, scratch=()):
    return pl.pallas_call(
        kernel,
        out_shape=outs,
        scratch_shapes=scratch,
        cost_estimate=pl.CostEstimate(flops=cost, bytes_accessed=1 << 20, transcendentals=0),
        name=kernel.__name__,
    )


def shifted(block, distance):
    devices = range(PEERS)
    return lax.ppermute(block, "dom", [(i - distance, i) for i in devices if i - distance in devices])


def swapped(block):
    return lax.ppermute(block, "body", [(0, 1), (1, 0)])


def exchanged(block):
    return lax.all_to_all(block, "dom", split_axis=0, concat_axis=0, tiled=True)


def local(
    displacement,
    connectivity,
    plastic_strain,
    element_size,
    yield_stress,
    external_force,
    slave_disp,
    pair_owner,
    pair_local,
    active,
    master_gap,
    master_normal,
    master_disp,
    coupling,
    quad_weight,
):
    seg_major = lambda x: jnp.transpose(x[0], (1, 0, 2))
    send, place = call(
        pack_kernel,
        (shape(PEERS * SLOTS, 4 * LANES, dtype=BF16), shape(PEERS * SLOTS, SEG, dtype=BF16)),
        1 << 27,
    )(pair_owner[0].T, pair_local[0].T, active, seg_major(slave_disp))
    got = exchanged(send)

    own = displacement[0].reshape(3, BLOCKS, LANES)
    low = shifted(own[:, BLOCKS - HALO :], 1)
    high = shifted(own[:, :HALO], -1)
    rows = call(rows_kernel, shape(4, SEG, LANES), 1 << 20)(
        master_gap[0], seg_major(master_normal), seg_major(master_disp)
    )
    rows = swapped(rows)
    links = jnp.transpose(connectivity[0].reshape(8, BLOCKS, LANES), (1, 0, 2)).reshape(8 * BLOCKS, LANES)
    to_prev, to_next, own_force = call(
        element_kernel,
        (shape(3, HALO, LANES), shape(3, HALO, LANES), shape(3, BLOCKS, LANES)),
        1 << 32,
        (
            pltpu.VMEM((3, 2 * HALO + BLOCKS + 8, LANES), F32),
            pltpu.VMEM((8 * BLOCKS, LANES), jnp.int32),
            pltpu.VMEM((8 * BLOCKS, LANES), jnp.int32),
            pltpu.VMEM((3, 8 * BLOCKS, LANES), F32),
            pltpu.VMEM((3, 2 * HALO + BLOCKS + 8, LANES), F32),
        ),
    )(
        low,
        own,
        high,
        links,
        plastic_strain[0].reshape(6, BLOCKS, LANES),
        element_size.reshape(BLOCKS, LANES),
        yield_stress.reshape(BLOCKS, LANES),
        external_force[0].reshape(3, BLOCKS, LANES),
    )

    back, force = call(
        master_kernel, (shape(PEERS * SLOTS, 3 * LANES, dtype=BF16), shape(3, SEG, LANES)), 1 << 28
    )(got, rows, coupling, quad_weight.reshape(1, LANES))
    returned = exchanged(back)
    master_force = swapped(force)

    residual = call(finish_kernel, shape(3, BLOCKS, LANES), 1 << 20)(
        own_force, shifted(to_next, 1), shifted(to_prev, -1)
    )
    slave_force = call(slave_kernel, shape(3, SEG, LANES), 1 << 27)(returned, place, coupling)
    return (
        residual.reshape(1, 3, BLOCKS * LANES),
        jnp.transpose(slave_force, (1, 0, 2))[None],
        jnp.transpose(master_force, (1, 0, 2))[None],
    )


def solution(mesh):
    return jax.shard_map(
        local,
        mesh=mesh,
        in_specs=(
            P("body", None, "dom"),
            P("body", None, "dom"),
            P("body", None, "dom"),
            P("body", "dom"),
            P("body", "dom"),
            P("body", None, "dom"),
            P("body", "dom", None, None),
            P("body", "dom", None),
            P("body", "dom", None),
            P("body", "dom"),
            P("body", "dom", None),
            P("body", "dom", None, None),
            P("body", "dom", None, None),
            P(),
            P(),
        ),
        out_specs=(
            P("body", None, "dom"),
            P("body", "dom", None, None),
            P("body", "dom", None, None),
        ),
        check_vma=False,
    )
```

time: 443 us -> 68.1 us (0.15)
  other arithmetic: 202 us -> 0 us
  local copies, waits for them, and re-layouts: 187 us -> 3.52 us
  Pallas kernels: 0 us -> 18.6 us
  starting transfers between devices: 46.1 us -> 37 us
  waiting for transfers between devices: 0.02 us -> 7.68 us
    scatter-add x3 -> x0, other arithmetic: 194 us -> none  [the longest x1 176 us: local(): assembled = jnp.zeros(extended.shape, jnp.float32).at[:, links].add(forces)]
    gather x6 -> x0, local copies, waits for them, and re-layouts: 129 us -> none  [the longest x2 121 us: local(): nodal = extended[:, links]]
    scatter x4 -> x0, local copies, waits for them, and re-layouts: 23.8 us -> none  [the longest x2 13 us: local(): jnp.zeros((2 * peers, slots, 2), jnp.int32).at[target, rank].set(meta_rows)]
    pallas_call x0 -> x6, Pallas kernels: none -> 18.6 us  [the longest x1 7.47 us: local(): call(element_kernel, (shape(3, HALO, LANES), shape(3, HALO, LANES), shape...]
    all_to_all x3 -> x2, starting transfers between devices: 30.1 us -> 21 us  [exchanged(): return lax.all_to_all(block, 'dom', split_axis=0, concat_axis=0, tiled=True)]
    mul x4 -> x0, local copies, waits for them, and re-layouts: 8.87 us -> none  [the longest x1 8.62 us: element_forces(): edge * edge]
    ppermute x4 -> x6, waiting for transfers between devices: 0.01 us -> 7.68 us  [the longest x4 7.67 us: shifted(): lax.ppermute(block, 'dom', [(i - distance, i) for i in devices if i - dis...]
    unnamed x39 -> x19, local copies, waits for them, and re-layouts: 8.8 us -> 3.52 us
  transfers between devices with their start and end apart: 7 -> 8, of which waited for: 0 -> 2; matrix products, arithmetic and copies ran while one was open for 87% -> 0% of each run, Pallas kernels for 0% -> 21%
where the time goes in v1:
time: 68.1 us; the launch traced here: 67.6 us
  starting transfers between devices  37 us (54%)
  Pallas kernels  18.6 us (27%)
  waiting for transfers between devices  7.68 us (11%)
  local copies, waits for them, and re-layouts  3.52 us (5%)
  between operations  0.78 us (1%)
    all_to_all x2, starting transfers between devices, exchanged(): return lax.all_to_all(block, 'dom', split_axis=0, concat_axis=0, tiled=True)  21 us
    ppermute x4, starting transfers between devices, shifted(): lax.ppermute(block, 'dom', [(i - distance, i) for i in devices if i - dis...  15.9 us
    ppermute x4, waiting for transfers between devices, shifted(): lax.ppermute(block, 'dom', [(i - distance, i) for i in devices if i - dis...  7.67 us
    pallas_call x1, Pallas kernels, local(): call(element_kernel, (shape(3, HALO, LANES), shape(3, HALO, LANES), shape...  7.47 us
    unnamed x19, local copies, waits for them, and re-layouts  3.52 us
    pallas_call x1, Pallas kernels, local(): call(master_kernel, (shape(PEERS * SLOTS, 3 * LANES, dtype=BF16), shape(3...  3.26 us
    pallas_call x1, Pallas kernels, local(): call(slave_kernel, shape(3, SEG, LANES), 1 << 27)(returned, place, coupling)  2.4 us
    pallas_call x1, Pallas kernels, local(): call(pack_kernel, (shape(PEERS * SLOTS, 4 * LANES, dtype=BF16), shape(PEE...  2.27 us
  transfers between devices with their start and end apart: 8, of which 2 were waited for; matrix products, arithmetic and copies ran while one was open for 0% of the time, Pallas kernels for 21%

profile of v1, /device:TPU:30, one launch (start us, length us, event | category | flops | bytes accessed | tf_op | source)
XLA Modules:
  0.0 67.6 jit_solution(8316901296656522341)
XLA Ops:
  0.6 2.3 %pack_kernel.1 = (bf16[512,512]{1,0:T(8,128)(2,1)}, bf16[512,128]{1,0:T(8,128)(2,1)}) custom-call(s32[2,128]{1,0:T(2,128)} %bitcast.56, s32[2,128]{1,0:T(2,128)} %bitcast.57, s32[1,128]{1,0:T(1,128)} %active.1, bf16[3,128,128]{2,1,0:T(8,128)(2,1)} %bitcast.51), custom_call_target="tpu_custom_call" | custom-call | flops 134217728 | bytes 1048576 | tf_op jit(solution)/shard_map/pack_kernel/pallas_call | solution.py:235
  2.9 11.1 %all-to-all-start = ((bf16[64,8,512]{2,1,0:T(8,128)(2,1)}), bf16[64,8,512]{2,1,0:T(8,128)(2,1)S(1)}, u32[]{:S(2)}, u32[]{:S(2)}) async-start(bf16[64,8,512]{2,1,0:T(8,128)(2,1)} %bitcast.40), calls=%async_computation | async-start | bytes 1048576 | tf_op jit(solution)/shard_map/all_to_all | solution.py:214
  14.0 0.0 copy-start.2
  14.0 1.8 %rows_kernel.1 = f32[4,128,128]{2,1,0:T(8,128)} custom-call(f32[128,128]{1,0:T(8,128)} %bitcast.46, f32[3,128,128]{2,1,0:T(8,128)} %bitcast.42, bf16[3,128,128]{2,1,0:T(8,128)(2,1)} %bitcast.45), custom_call_target="tpu_custom_call" | custom-call | flops 1048576 | bytes 1048576 | tf_op jit(solution)/shard_map/rows_kernel/pallas_call | solution.py:245
  15.8 0.0 collective-permute-start.4
  15.8 0.0 copy-done.2
  15.8 2.8 %collective-permute-start.1 = (f32[3,16,128]{2,1,0:T(8,128)S(1)}, f32[3,16,128]{2,1,0:T(8,128)S(1)}, u32[]{:S(2)}, u32[]{:S(2)}) collective-permute-start(f32[3,16,128]{2,1,0:T(8,128)S(1)} %get-tuple-element.23), channel_id=1, source_target_pairs={{1,0},{2,1},{3,2},{4,3},{5,4},{6,5},{7,6},{8,7},{9,8},{10,9},{11,1... | collective-permute-start | bytes 73736 | tf_op jit(solution)/shard_map/ppermute | solution.py:206
  18.6 7.3 %collective-permute-start = (f32[3,16,128]{2,1,0:T(8,128)S(1)}, f32[3,16,128]{2,1,0:T(8,128)S(1)}, u32[]{:S(2)}, u32[]{:S(2)}) collective-permute-start(f32[3,16,128]{2,1,0:T(8,128)S(1)} %get-tuple-element.24), channel_id=1, source_target_pairs={{0,1},{1,2},{2,3},{3,4},{4,5},{5,6},{6,7},{7,8},{8,9},{9,10},{10,1... | collective-permute-start | bytes 73736 | tf_op jit(solution)/shard_map/ppermute | solution.py:206
  25.9 0.0 collective-permute-done.4.rows
  25.9 0.0 copy-start.5
  25.9 0.0 all-to-all-done
  25.9 0.0 copy-start.1
  25.9 0.7 %copy-done.5 = f32[4,128,128]{2,1,0:T(8,128)} copy-done((f32[4,128,128]{2,1,0:T(8,128)}, f32[4,128,128]{2,1,0:T(8,128)S(1)}, u32[]{:S(2)}) %copy-start.5) | copy-done | bytes 262168
  26.6 0.2 copy-done.1
  26.8 3.3 %master_kernel.1 = (bf16[512,384]{1,0:T(8,128)(2,1)}, f32[3,128,128]{2,1,0:T(8,128)}) custom-call(bf16[512,512]{1,0:T(8,128)(2,1)} %bitcast.39, f32[4,128,128]{2,1,0:T(8,128)} %copy-done.5, bf16[128,128]{1,0:T(8,128)(2,1)} %coupling.3, f32[1,128]{1,0:T(1,128)} %bitcast.58), custom_call_target="tpu_custom_call" | custom-call | flops 268435456 | bytes 1048576 | tf_op jit(solution)/shard_map/master_kernel/pallas_call | solution.py:272
  30.1 0.0 copy-start.6
  30.1 9.9 %all-to-all-start.1 = ((bf16[64,8,384]{2,1,0:T(8,128)(2,1)}), bf16[64,8,384]{2,1,0:T(8,128)(2,1)S(1)}, u32[]{:S(2)}, u32[]{:S(2)}) async-start(bf16[64,8,384]{2,1,0:T(8,128)(2,1)} %bitcast.41), calls=%async_computation.1 | async-start | bytes 786432 | tf_op jit(solution)/shard_map/all_to_all | solution.py:214
  40.0 0.0 copy-done.6
  40.0 0.1 collective-permute-start.5
  40.1 0.0 collective-permute-done.1.high
  40.1 0.0 copy-start.7
  40.1 0.0 collective-permute-done.low
  40.1 0.0 copy-start.8
  40.1 0.6 copy-done.7
  40.7 0.0 copy-done.8
  40.7 7.5 %element_kernel.1 = (f32[3,16,128]{2,1,0:T(8,128)}, f32[3,16,128]{2,1,0:T(8,128)}, f32[3,32,128]{2,1,0:T(8,128)}) custom-call(f32[3,16,128]{2,1,0:T(8,128)} %copy-done.8, f32[3,32,128]{2,1,0:T(8,128)} %bitcast.47, f32[3,16,128]{2,1,0:T(8,128)} %copy-done.7, s32[256,128]{1,0:T(8,128)} %bitcast.50, f32[6,32,128]{2,1,0:T(8,128)} %bitcast.52, ...), custom_call_target="tpu_custom_call" | custom-call | flops 4294967296 | bytes 1048576 | tf_op jit(solution)/shard_map/element_kernel/pallas_call | solution.py:250
  48.2 3.4 %collective-permute-start.2 = (f32[3,16,128]{2,1,0:T(8,128)}, f32[3,16,128]{2,1,0:T(8,128)S(1)}, u32[]{:S(2)}, u32[]{:S(2)}) collective-permute-start(f32[3,16,128]{2,1,0:T(8,128)} %get-tuple-element.11), channel_id=1, source_target_pairs={{0,1},{1,2},{2,3},{3,4},{4,5},{5,6},{6,7},{7,8},{8,9},{9,10},{10,1... | collective-permute-start | bytes 73736 | tf_op jit(solution)/shard_map/ppermute | solution.py:206
  51.6 2.5 %collective-permute-start.3 = (f32[3,16,128]{2,1,0:T(8,128)}, f32[3,16,128]{2,1,0:T(8,128)S(1)}, u32[]{:S(2)}, u32[]{:S(2)}) collective-permute-start(f32[3,16,128]{2,1,0:T(8,128)} %get-tuple-element.12), channel_id=1, source_target_pairs={{1,0},{2,1},{3,2},{4,3},{5,4},{6,5},{7,6},{8,7},{9,8},{10,9},{11,1... | collective-permute-start | bytes 73736 | tf_op jit(solution)/shard_map/ppermute | solution.py:206
  54.0 0.1 collective-permute-done.2.from_prev
  54.1 0.0 copy-start.3
  54.1 7.6 %collective-permute-done.3.from_next = f32[3,16,128]{2,1,0:T(8,128)S(1)} collective-permute-done((f32[3,16,128]{2,1,0:T(8,128)}, f32[3,16,128]{2,1,0:T(8,128)S(1)}, u32[]{:S(2)}, u32[]{:S(2)}) %collective-permute-start.3) | collective-permute-done | bytes 24608 | tf_op jit(solution)/shard_map/ppermute | solution.py:206
  61.7 0.0 copy-start.4
  61.7 0.0 copy-done.3
  61.7 0.6 copy-done.4
  62.3 1.4 %finish_kernel.1 = f32[3,32,128]{2,1,0:T(8,128)} custom-call(f32[3,32,128]{2,1,0:T(8,128)} %get-tuple-element.10.own, f32[3,16,128]{2,1,0:T(8,128)} %copy-done.3, f32[3,16,128]{2,1,0:T(8,128)} %copy-done.4), custom_call_target="tpu_custom_call" | custom-call | flops 1048576 | bytes 1048576 | tf_op jit(solution)/shard_map/finish_kernel/pallas_call | solution.py:278
  63.8 0.0 collective-permute-done.5
  63.8 0.0 all-to-all-done.1
  63.8 0.0 copy-start
  63.8 0.7 %copy-done = bf16[64,8,384]{2,1,0:T(8,128)(2,1)} copy-done((bf16[64,8,384]{2,1,0:T(8,128)(2,1)}, bf16[64,8,384]{2,1,0:T(8,128)(2,1)S(1)}, u32[]{:S(2)}) %copy-start) | copy-done | bytes 393240
  64.5 2.4 %slave_kernel.1 = f32[3,128,128]{2,1,0:T(8,128)} custom-call(bf16[512,384]{1,0:T(8,128)(2,1)} %bitcast.38, bf16[512,128]{1,0:T(8,128)(2,1)} %get-tuple-element.15.place, bf16[128,128]{1,0:T(8,128)(2,1)} %coupling.3), custom_call_target="tpu_custom_call" | custom-call | flops 134217728 | bytes 1048576 | tf_op jit(solution)/shard_map/slave_kernel/pallas_call | solution.py:281
  66.9 0.7 %copy.21 = f32[1,128,3,128]{3,1,2,0:T(8,128)} copy(f32[1,128,3,128]{3,1,2,0:T(8,128)S(1)} %bitcast.43) | data formatting | bytes 393216
  (1 shorter events, 0.0 us)
Async XLA Ops:
  2.9 23.0 %all-to-all-start = ((bf16[64,8,512]{2,1,0:T(8,128)(2,1)}), bf16[64,8,512]{2,1,0:T(8,128)(2,1)S(1)}, u32[]{:S(2)}, u32[]{:S(2)}) async-start(bf16[64,8,512]{2,1,0:T(8,128)(2,1)} %bitcast.40), calls=%async_computation | async-start | bytes 1048576 | tf_op jit(solution)/shard_map/all_to_all | solution.py:214
  14.0 1.8 %copy-start.2 = (f32[1,3,4096]{2,0,1:T(1,128)S(1)}, f32[1,3,4096]{2,0,1:T(1,128)}, u32[]{:S(2)}) copy-start(f32[1,3,4096]{2,0,1:T(1,128)} %param.15) | copy-start | bytes 147460
  15.8 10.1 %collective-permute-start.4 = (f32[4,128,128]{2,1,0:T(8,128)}, f32[4,128,128]{2,1,0:T(8,128)S(1)}, u32[]{:S(2)}, u32[]{:S(2)}) collective-permute-start(f32[4,128,128]{2,1,0:T(8,128)} %rows_kernel.1), channel_id=1, source_target_pairs={{0,64},{64,0},{1,65},{65,1},{2,66},{66,2},{3,67},{67,3},{4,68},{68... | collective-permute-start | bytes 786440 | tf_op jit(solution)/shard_map/ppermute | solution.py:210
  15.8 24.3 %collective-permute-start.1 = (f32[3,16,128]{2,1,0:T(8,128)S(1)}, f32[3,16,128]{2,1,0:T(8,128)S(1)}, u32[]{:S(2)}, u32[]{:S(2)}) collective-permute-start(f32[3,16,128]{2,1,0:T(8,128)S(1)} %get-tuple-element.23), channel_id=1, source_target_pairs={{1,0},{2,1},{3,2},{4,3},{5,4},{6,5},{7,6},{8,7},{9,8},{10,9},{11,1... | collective-permute-start | bytes 73736 | tf_op jit(solution)/shard_map/ppermute | solution.py:206
  18.6 21.5 %collective-permute-start = (f32[3,16,128]{2,1,0:T(8,128)S(1)}, f32[3,16,128]{2,1,0:T(8,128)S(1)}, u32[]{:S(2)}, u32[]{:S(2)}) collective-permute-start(f32[3,16,128]{2,1,0:T(8,128)S(1)} %get-tuple-element.24), channel_id=1, source_target_pairs={{0,1},{1,2},{2,3},{3,4},{4,5},{5,6},{6,7},{7,8},{8,9},{9,10},{10,1... | collective-permute-start | bytes 73736 | tf_op jit(solution)/shard_map/ppermute | solution.py:206
  25.9 0.7 %copy-start.5 = (f32[4,128,128]{2,1,0:T(8,128)}, f32[4,128,128]{2,1,0:T(8,128)S(1)}, u32[]{:S(2)}) copy-start(f32[4,128,128]{2,1,0:T(8,128)S(1)} %collective-permute-done.4.rows) | copy-start | bytes 786436
  25.9 0.9 %copy-start.1 = (bf16[64,8,512]{2,1,0:T(8,128)(2,1)}, bf16[64,8,512]{2,1,0:T(8,128)(2,1)S(1)}, u32[]{:S(2)}) copy-start(bf16[64,8,512]{2,1,0:T(8,128)(2,1)S(1)} %all-to-all-done) | copy-start | bytes 1572868
  30.1 9.9 %copy-start.6 = (f32[3,128,128]{2,1,0:T(8,128)S(1)}, f32[3,128,128]{2,1,0:T(8,128)}, u32[]{:S(2)}) copy-start(f32[3,128,128]{2,1,0:T(8,128)} %get-tuple-element.16) | copy-start | bytes 589828
  30.1 33.7 %all-to-all-start.1 = ((bf16[64,8,384]{2,1,0:T(8,128)(2,1)}), bf16[64,8,384]{2,1,0:T(8,128)(2,1)S(1)}, u32[]{:S(2)}, u32[]{:S(2)}) async-start(bf16[64,8,384]{2,1,0:T(8,128)(2,1)} %bitcast.41), calls=%async_computation.1 | async-start | bytes 786432 | tf_op jit(solution)/shard_map/all_to_all | solution.py:214
  40.0 23.8 %collective-permute-start.5 = (f32[3,128,128]{2,1,0:T(8,128)S(1)}, f32[3,128,128]{2,1,0:T(8,128)S(1)}, u32[]{:S(2)}, u32[]{:S(2)}) collective-permute-start(f32[3,128,128]{2,1,0:T(8,128)S(1)} %copy-done.6), channel_id=1, source_target_pairs={{0,64},{64,0},{1,65},{65,1},{2,66},{66,2},{3,67},{67,3},{4,68},{68... | collective-permute-start | bytes 589832 | tf_op jit(solution)/shard_map/ppermute | solution.py:210
  40.1 0.6 copy-start.7
  40.1 0.6 copy-start.8
  48.2 5.9 %collective-permute-start.2 = (f32[3,16,128]{2,1,0:T(8,128)}, f32[3,16,128]{2,1,0:T(8,128)S(1)}, u32[]{:S(2)}, u32[]{:S(2)}) collective-permute-start(f32[3,16,128]{2,1,0:T(8,128)} %get-tuple-element.11), channel_id=1, source_target_pairs={{0,1},{1,2},{2,3},{3,4},{4,5},{5,6},{6,7},{7,8},{8,9},{9,10},{10,1... | collective-permute-start | bytes 73736 | tf_op jit(solution)/shard_map/ppermute | solution.py:206
  51.6 10.1 %collective-permute-start.3 = (f32[3,16,128]{2,1,0:T(8,128)}, f32[3,16,128]{2,1,0:T(8,128)S(1)}, u32[]{:S(2)}, u32[]{:S(2)}) collective-permute-start(f32[3,16,128]{2,1,0:T(8,128)} %get-tuple-element.12), channel_id=1, source_target_pairs={{1,0},{2,1},{3,2},{4,3},{5,4},{6,5},{7,6},{8,7},{9,8},{10,9},{11,1... | collective-permute-start | bytes 73736 | tf_op jit(solution)/shard_map/ppermute | solution.py:206
  54.1 7.6 %copy-start.3 = (f32[3,16,128]{2,1,0:T(8,128)}, f32[3,16,128]{2,1,0:T(8,128)S(1)}, u32[]{:S(2)}) copy-start(f32[3,16,128]{2,1,0:T(8,128)S(1)} %collective-permute-done.2.from_prev) | copy-start | bytes 73732
  61.7 0.6 copy-start.4
  63.8 0.8 %copy-start = (bf16[64,8,384]{2,1,0:T(8,128)(2,1)}, bf16[64,8,384]{2,1,0:T(8,128)(2,1)S(1)}, u32[]{:S(2)}) copy-start(bf16[64,8,384]{2,1,0:T(8,128)(2,1)S(1)} %all-to-all-done.1) | copy-start | bytes 1179652

commit v2 on v1

--- a/solution.py
+++ b/solution.py
@@ -9,7 +9,7 @@
 from jax.sharding import PartitionSpec as P
 
 LANES = 128
-WINDOW = 40
+WINDOW = 48
 HALO = 16
 BLOCKS = 32
 SLOTS = 8
@@ -37,14 +37,15 @@
     disp[:, HALO + BLOCKS : 2 * HALO + BLOCKS, :] = high[...]
     acc[...] = jnp.zeros_like(acc)
     lane = iota((8, LANES), 1)
+    block = iota((8, LANES), 0)
     for m in range(BLOCKS // 8):
         nodal = []
         for a in range(8):
             reach = links[pl.ds(64 * m + a, 8, stride=8), :] + lane
             hi = reach >> 7
             lo = reach & 127
-            lo_s[a * BLOCKS + 8 * m : a * BLOCKS + 8 * m + 8, :] = lo
-            hi_s[a * BLOCKS + 8 * m : a * BLOCKS + 8 * m + 8, :] = hi
+            lo_s[a * BLOCKS + 8 * m : a * BLOCKS + 8 * m + 8, :] = lo.astype(F32)
+            hi_s[a * BLOCKS + 8 * m : a * BLOCKS + 8 * m + 8, :] = (hi + block).astype(F32)
             got = [jnp.zeros((8, LANES), F32)] * 3
             for h in range(33):
                 here = hi == h
@@ -89,34 +90,44 @@
                 pick = four[(0 if a & 1 else 1) if a & 2 else (2 if a & 1 else 3)]
                 f = pick + tz if a & 4 else pick - tz
                 force_s[i, a * BLOCKS + 8 * m : a * BLOCKS + 8 * m + 8, :] = f
-    row = iota((WINDOW, LANES), 0)
-    row_lane = iota((LANES, LANES), 0)
-    for k in range(BLOCKS):
-        left, right = [], []
-        for a in range(8):
-            r = a * BLOCKS + k
-            hi = jnp.broadcast_to(hi_s[r : r + 1, :], (WINDOW, LANES))
-            lo = jnp.broadcast_to(lo_s[r : r + 1, :], (LANES, LANES))
-            here = hi == row
-            parts = [
-                jnp.where(here, jnp.broadcast_to(force_s[i, r : r + 1, :], (WINDOW, LANES)), 0.0) for i in range(3)
-            ]
-            left.append(jnp.concatenate(parts, axis=0).astype(BF16))
-            right.append(jnp.where(lo == row_lane, 1.0, 0.0).astype(BF16))
-        sums = dot(jnp.concatenate(left, axis=1), jnp.concatenate(right, axis=1), NT)
+    row = iota((16, LANES), 0, F32)
+    rows = [(row + 16.0 * t).astype(BF16) for t in range(8)]
+    zero = jnp.zeros((16, LANES), BF16)
+    one = jnp.ones((16, LANES), BF16)
+
+    def wide(ref, *at):
+        return jnp.broadcast_to(ref[at], (16, LANES)).astype(BF16)
+
+    for m in range(BLOCKS // 8):
+        sums = jnp.zeros((3 * WINDOW, LANES), F32)
+        for s in range(8):
+            left, right = [], []
+            for a in range(8):
+                at = slice(a * BLOCKS + 8 * m + s, a * BLOCKS + 8 * m + s + 1)
+                hi = wide(hi_s, at, slice(None))
+                lo = wide(lo_s, at, slice(None))
+                here = [hi == rows[t] for t in range(WINDOW // 16)]
+                parts = []
+                for i in range(3):
+                    f = wide(force_s, i, at, slice(None))
+                    parts += [jnp.where(h, f, zero) for h in here]
+                left.append(jnp.concatenate(parts, axis=0))
+                right.append(jnp.concatenate([jnp.where(lo == r, one, zero) for r in rows], axis=0))
+            sums = sums + dot(jnp.concatenate(left, axis=1), jnp.concatenate(right, axis=1), NT)
         for i in range(3):
-            acc[i, k : k + WINDOW, :] += sums[i * WINDOW : (i + 1) * WINDOW]
+            acc[i, 8 * m : 8 * m + WINDOW, :] += sums[i * WINDOW : (i + 1) * WINDOW]
     prev_out[...] = acc[:, 0:HALO, :]
     next_out[...] = acc[:, HALO + BLOCKS : 2 * HALO + BLOCKS, :]
     own_out[...] = acc[:, HALO : HALO + BLOCKS, :] - ext[...]
 
 
-def finish_kernel(own, from_prev, from_next, out):
+def finish_kernel(own, from_prev, from_next, force, out, force_out):
+    force_out[...] = force[...]
     out[:, 0:HALO, :] = own[:, 0:HALO, :] + from_prev[...]
     out[:, HALO:BLOCKS, :] = own[:, HALO:BLOCKS, :] + from_next[...]
 
 
-def pack_kernel(owner, where, active, disp, send, place):
+def pack_kernel(owner, where, active, disp, gap, normal, mdisp, send, place, rows):
     names = iota((PEERS, SEG), 0)
     earlier = jnp.where(iota((SEG, SEG), 0) < iota((SEG, SEG), 1), 1.0, 0.0).astype(BF16)
     ones = jnp.ones((SEG, SEG), BF16)
@@ -138,15 +149,12 @@
     for c in range(3):
         send[:, c * LANES : (c + 1) * LANES] = dot(sent, disp[c]).astype(BF16)
     send[:, 3 * LANES :] = dot(meta.astype(BF16), ones).astype(BF16)
-
-
-def rows_kernel(gap, normal, mdisp, out):
     total = gap[...]
     for c in range(3):
         n = normal[c]
         total = total + n * mdisp[c].astype(F32)
-        out[1 + c] = n
-    out[0] = total
+        rows[1 + c] = n
+    rows[0] = total
 
 
 def mortar_of(coupling):
@@ -191,11 +199,17 @@
     return jax.ShapeDtypeStruct(dims, dtype)
 
 
-def call(kernel, outs, cost, scratch=()):
+VMEM = pl.BlockSpec(memory_space=pltpu.VMEM)
+
+
+def call(kernel, ins, outs, cost, scratch=()):
     return pl.pallas_call(
         kernel,
         out_shape=outs,
+        in_specs=[VMEM] * ins,
+        out_specs=jax.tree.map(lambda _: VMEM, outs),
         scratch_shapes=scratch,
+        compiler_params=pltpu.CompilerParams(vmem_limit_bytes=8 << 20),
         cost_estimate=pl.CostEstimate(flops=cost, bytes_accessed=1 << 20, transcendentals=0),
         name=kernel.__name__,
     )
@@ -232,31 +246,42 @@
     quad_weight,
 ):
     seg_major = lambda x: jnp.transpose(x[0], (1, 0, 2))
-    send, place = call(
+    send, place, rows = call(
         pack_kernel,
-        (shape(PEERS * SLOTS, 4 * LANES, dtype=BF16), shape(PEERS * SLOTS, SEG, dtype=BF16)),
+        7,
+        (
+            shape(PEERS * SLOTS, 4 * LANES, dtype=BF16),
+            shape(PEERS * SLOTS, SEG, dtype=BF16),
+            shape(4, SEG, LANES),
+        ),
         1 << 27,
-    )(pair_owner[0].T, pair_local[0].T, active, seg_major(slave_disp))
+    )(
+        pair_owner[0].T,
+        pair_local[0].T,
+        active,
+        seg_major(slave_disp),
+        master_gap[0],
+        seg_major(master_normal),
+        seg_major(master_disp),
+    )
     got = exchanged(send)
 
     own = displacement[0].reshape(3, BLOCKS, LANES)
     low = shifted(own[:, BLOCKS - HALO :], 1)
     high = shifted(own[:, :HALO], -1)
-    rows = call(rows_kernel, shape(4, SEG, LANES), 1 << 20)(
-        master_gap[0], seg_major(master_normal), seg_major(master_disp)
-    )
     rows = swapped(rows)
     links = jnp.transpose(connectivity[0].reshape(8, BLOCKS, LANES), (1, 0, 2)).reshape(8 * BLOCKS, LANES)
     to_prev, to_next, own_force = call(
         element_kernel,
+        8,
         (shape(3, HALO, LANES), shape(3, HALO, LANES), shape(3, BLOCKS, LANES)),
         1 << 32,
         (
-            pltpu.VMEM((3, 2 * HALO + BLOCKS + 8, LANES), F32),
-            pltpu.VMEM((8 * BLOCKS, LANES), jnp.int32),
-            pltpu.VMEM((8 * BLOCKS, LANES), jnp.int32),
+            pltpu.VMEM((3, 2 * HALO + BLOCKS + 16, LANES), F32),
+            pltpu.VMEM((8 * BLOCKS, LANES), F32),
+            pltpu.VMEM((8 * BLOCKS, LANES), F32),
             pltpu.VMEM((3, 8 * BLOCKS, LANES), F32),
-            pltpu.VMEM((3, 2 * HALO + BLOCKS + 8, LANES), F32),
+            pltpu.VMEM((3, 2 * HALO + BLOCKS + 16, LANES), F32),
         ),
     )(
         low,
@@ -269,16 +294,15 @@
         external_force[0].reshape(3, BLOCKS, LANES),
     )
 
+    got, to_prev, to_next = lax.optimization_barrier((got, to_prev, to_next))
     back, force = call(
-        master_kernel, (shape(PEERS * SLOTS, 3 * LANES, dtype=BF16), shape(3, SEG, LANES)), 1 << 28
+        master_kernel, 4, (shape(PEERS * SLOTS, 3 * LANES, dtype=BF16), shape(3, SEG, LANES)), 1 << 28
     )(got, rows, coupling, quad_weight.reshape(1, LANES))
     returned = exchanged(back)
-    master_force = swapped(force)
-
-    residual = call(finish_kernel, shape(3, BLOCKS, LANES), 1 << 20)(
-        own_force, shifted(to_next, 1), shifted(to_prev, -1)
-    )
-    slave_force = call(slave_kernel, shape(3, SEG, LANES), 1 << 27)(returned, place, coupling)
+    residual, master_force = call(finish_kernel, 4, (shape(3, BLOCKS, LANES), shape(3, SEG, LANES)), 1 << 20)(
+        own_force, shifted(to_next, 1), shifted(to_prev, -1), swapped(force)
+    )
+    slave_force = call(slave_kernel, 3, shape(3, SEG, LANES), 1 << 27)(returned, place, coupling)
     return (
         residual.reshape(1, 3, BLOCKS * LANES),
         jnp.transpose(slave_force, (1, 0, 2))[None],

time: 68.1 us -> 64.4 us (0.946)
  Pallas kernels: 18.6 us -> 11.2 us
  local copies, waits for them, and re-layouts: 3.52 us -> 4.89 us
  waiting for transfers between devices: 7.68 us -> 8.86 us
  starting transfers between devices: 37 us -> 38.1 us
    pallas_call x6 -> x5, Pallas kernels: 18.6 us -> 11.2 us  [the longest x1 5.79 us: local(): call(element_kernel, 8, (shape(3, HALO, LANES), shape(3, HALO, LANES), sh...]
    unnamed x19 -> x30, local copies, waits for them, and re-layouts: 3.52 us -> 4.89 us
    ppermute x4, waiting for transfers between devices: 7.67 us -> 8.85 us  [shifted(): lax.ppermute(block, 'dom', [(i - distance, i) for i in devices if i - dis...]
    all_to_all x2, starting transfers between devices: 21 us -> 21.9 us  [exchanged(): return lax.all_to_all(block, 'dom', split_axis=0, concat_axis=0, tiled=True)]
  transfers between devices with their start and end apart: 8 -> 8, of which waited for: 2 -> 2; matrix products, arithmetic and copies ran while one was open for 0% -> 0% of each run, Pallas kernels for 21% -> 10%
where the time goes in v2:
time: 64.4 us; the launch traced here: 63.8 us
  starting transfers between devices  38.1 us (59%)
  Pallas kernels  11.2 us (17%)
  waiting for transfers between devices  8.86 us (14%)
  local copies, waits for them, and re-layouts  4.89 us (8%)
  between operations  0.84 us (1%)
    all_to_all x2, starting transfers between devices, exchanged(): return lax.all_to_all(block, 'dom', split_axis=0, concat_axis=0, tiled=True)  21.9 us
    ppermute x4, starting transfers between devices, shifted(): lax.ppermute(block, 'dom', [(i - distance, i) for i in devices if i - dis...  16 us
    ppermute x4, waiting for transfers between devices, shifted(): lax.ppermute(block, 'dom', [(i - distance, i) for i in devices if i - dis...  8.85 us
    pallas_call x1, Pallas kernels, local(): call(element_kernel, 8, (shape(3, HALO, LANES), shape(3, HALO, LANES), sh...  5.79 us
    unnamed x30, local copies, waits for them, and re-layouts  4.89 us
    pallas_call x1, Pallas kernels, local(): call(master_kernel, 4, (shape(PEERS * SLOTS, 3 * LANES, dtype=BF16), shap...  2.02 us
    pallas_call x1, Pallas kernels, local(): call(pack_kernel, 7, (shape(PEERS * SLOTS, 4 * LANES, dtype=BF16), shape(...  1.33 us
    pallas_call x1, Pallas kernels, local(): call(slave_kernel, 3, shape(3, SEG, LANES), 1 << 27)  1.33 us
  transfers between devices with their start and end apart: 8, of which 2 were waited for; matrix products, arithmetic and copies ran while one was open for 0% of the time, Pallas kernels for 10%

profile of v2, /device:TPU:30, one launch (start us, length us, event | category | flops | bytes accessed | tf_op | source)
XLA Modules:
  0.0 63.8 jit_solution(3147139853087223750)
XLA Ops:
  0.6 0.0 copy-start.12
  0.6 0.0 copy-start.11
  0.7 0.0 copy-start.13
  0.7 0.7 %copy-done.12 = s32[1,128,2]{1,2,0:T(2,128)S(1)} copy-done((s32[1,128,2]{1,2,0:T(2,128)S(1)}, s32[1,128,2]{1,2,0:T(2,128)}, u32[]{:S(2)}) %copy-start.12) | copy-done | bytes 1048
  1.3 0.0 copy-done.11
  1.3 0.0 copy-done.13
  1.3 0.0 copy-start.2
  1.3 0.9 %copy-done.2 = f32[1,128,3,128]{3,1,2,0:T(8,128)S(1)} copy-done((f32[1,128,3,128]{3,1,2,0:T(8,128)S(1)}, f32[1,128,3,128]{3,1,2,0:T(8,128)}, u32[]{:S(2)}) %copy-start.2) | copy-done | bytes 196632
  2.3 0.0 copy-start.4
  2.3 0.9 %copy-done.4 = bf16[1,128,3,128]{3,1,2,0:T(8,128)(2,1)S(1)} copy-done((bf16[1,128,3,128]{3,1,2,0:T(8,128)(2,1)S(1)}, bf16[1,128,3,128]{3,1,2,0:T(8,128)(2,1)}, u32[]{:S(2)}) %copy-start.4) | copy-done | bytes 98328
  3.2 0.0 copy-start.5
  3.2 0.9 %copy-done.5 = bf16[1,128,3,128]{3,1,2,0:T(8,128)(2,1)S(1)} copy-done((bf16[1,128,3,128]{3,1,2,0:T(8,128)(2,1)S(1)}, bf16[1,128,3,128]{3,1,2,0:T(8,128)(2,1)}, u32[]{:S(2)}) %copy-start.5) | copy-done | bytes 98328
  4.0 0.0 copy-start.7
  4.0 0.8 %copy-done.7 = f32[1,128,128]{2,1,0:T(8,128)S(1)} copy-done((f32[1,128,128]{2,1,0:T(8,128)S(1)}, f32[1,128,128]{2,1,0:T(8,128)}, u32[]{:S(2)}) %copy-start.7) | copy-done | bytes 65560
  4.9 1.3 %pack_kernel.1 = (bf16[512,512]{1,0:T(8,128)(2,1)}, bf16[512,128]{1,0:T(8,128)(2,1)S(1)}, f32[4,128,128]{2,1,0:T(8,128)S(1)}) custom-call(s32[2,128]{1,0:T(2,128)S(1)} %bitcast.51, s32[2,128]{1,0:T(2,128)S(1)} %bitcast.52, s32[1,128]{1,0:T(1,128)S(1)} %copy-done.13, bf16[3,128,128]{2,1,0:T(8,128)(2,1)S(1)} %bitcast.44, f32[128,128]{1,0:T(8,128)S(1)} %bitcast.47, ...), custom_call_target="tpu_custom_call" | custom-call | flops 134217728 | bytes 1048576 | tf_op jit(solution)/shard_map/pack_kernel/pallas_call | solution.py:249
  6.2 0.0 copy-start
  6.2 11.2 %all-to-all-start = ((bf16[64,8,512]{2,1,0:T(8,128)(2,1)}), bf16[64,8,512]{2,1,0:T(8,128)(2,1)S(1)}, u32[]{:S(2)}, u32[]{:S(2)}) async-start(bf16[64,8,512]{2,1,0:T(8,128)(2,1)} %bitcast.19), calls=%async_computation | async-start | bytes 1048576 | tf_op jit(solution)/shard_map/all_to_all | solution.py:228
  17.5 0.0 copy-start.6
  17.5 0.0 copy-done
  17.5 0.0 copy-start.9
  17.5 2.9 %collective-permute-start.1 = (f32[3,16,128]{2,1,0:T(8,128)S(1)}, f32[3,16,128]{2,1,0:T(8,128)S(1)}, u32[]{:S(2)}, u32[]{:S(2)}) collective-permute-start(f32[3,16,128]{2,1,0:T(8,128)S(1)} %get-tuple-element.35), channel_id=1, source_target_pairs={{1,0},{2,1},{3,2},{4,3},{5,4},{6,5},{7,6},{8,7},{9,8},{10,9},{11,1... | collective-permute-start | bytes 73736 | tf_op jit(solution)/shard_map/ppermute | solution.py:220
  20.4 7.3 %collective-permute-start = (f32[3,16,128]{2,1,0:T(8,128)S(1)}, f32[3,16,128]{2,1,0:T(8,128)S(1)}, u32[]{:S(2)}, u32[]{:S(2)}) collective-permute-start(f32[3,16,128]{2,1,0:T(8,128)S(1)} %get-tuple-element.36), channel_id=1, source_target_pairs={{0,1},{1,2},{2,3},{3,4},{4,5},{5,6},{6,7},{7,8},{8,9},{9,10},{10,1... | collective-permute-start | bytes 73736 | tf_op jit(solution)/shard_map/ppermute | solution.py:220
  27.7 0.1 collective-permute-start.4
  27.8 0.0 collective-permute-done.1.high
  27.8 1.4 %collective-permute-done.low = f32[3,16,128]{2,1,0:T(8,128)S(1)} collective-permute-done((f32[3,16,128]{2,1,0:T(8,128)S(1)}, f32[3,16,128]{2,1,0:T(8,128)S(1)}, u32[]{:S(2)}, u32[]{:S(2)}) %collective-permute-start) | collective-permute-done | bytes 24608 | tf_op jit(solution)/shard_map/ppermute | solution.py:220
  29.2 0.0 copy-done.3
  29.2 0.0 copy-done.8
  29.2 0.0 copy-done.10
  29.2 0.0 copy-done.6
  29.2 0.0 copy-done.9
  29.3 0.0 copy-start.1
  29.3 5.8 %element_kernel.1 = (f32[3,16,128]{2,1,0:T(8,128)S(1)}, f32[3,16,128]{2,1,0:T(8,128)S(1)}, f32[3,32,128]{2,1,0:T(8,128)S(1)}) custom-call(f32[3,16,128]{2,1,0:T(8,128)S(1)} %collective-permute-done.low, f32[3,32,128]{2,1,0:T(8,128)S(1)} %bitcast.41, f32[3,16,128]{2,1,0:T(8,128)S(1)} %collective-permute-done.1.high, s32[256,128]{1,0:T(8,128)S(1)} %bitcast.43, ...), custom_call_target="tpu_custom_call" | custom-call | flops 4294967296 | bytes 1048576 | tf_op jit(solution)/shard_map/element_kernel/pallas_call | solution.py:274
  35.1 0.0 all-to-all-done
  35.1 0.0 copy-start.14
  35.1 0.0 collective-permute-done.4.rows
  35.1 0.0 copy-done.1
  35.1 0.6 copy-done.14
  35.7 2.0 %master_kernel.1 = (bf16[512,384]{1,0:T(8,128)(2,1)}, f32[3,128,128]{2,1,0:T(8,128)S(1)}) custom-call(bf16[512,512]{1,0:T(8,128)(2,1)S(1)} %bitcast.39, f32[4,128,128]{2,1,0:T(8,128)S(1)} %collective-permute-done.4.rows, bf16[128,128]{1,0:T(8,128)(2,1)S(1)} %copy-done.1, f32[1,128]{1,0:T(1,128)S(1)} %bitcast.53), custom_call_target="tpu_custom_call" | custom-call | flops 268435456 | bytes 1048576 | tf_op jit(solution)/shard_map/master_kernel/pallas_call | solution.py:298
  37.8 10.6 %all-to-all-start.1 = ((bf16[64,8,384]{2,1,0:T(8,128)(2,1)}), bf16[64,8,384]{2,1,0:T(8,128)(2,1)S(1)}, u32[]{:S(2)}, u32[]{:S(2)}) async-start(bf16[64,8,384]{2,1,0:T(8,128)(2,1)} %bitcast.23), calls=%async_computation.1 | async-start | bytes 786432 | tf_op jit(solution)/shard_map/all_to_all | solution.py:228
  48.4 0.1 collective-permute-start.5
  48.5 3.4 %collective-permute-start.2 = (f32[3,16,128]{2,1,0:T(8,128)S(1)}, f32[3,16,128]{2,1,0:T(8,128)S(1)}, u32[]{:S(2)}, u32[]{:S(2)}) collective-permute-start(f32[3,16,128]{2,1,0:T(8,128)S(1)} %get-tuple-element.20), channel_id=1, source_target_pairs={{0,1},{1,2},{2,3},{3,4},{4,5},{5,6},{6,7},{7,8},{8,9},{9,10},{10,1... | collective-permute-start | bytes 73736 | tf_op jit(solution)/shard_map/ppermute | solution.py:220
  51.9 2.5 %collective-permute-start.3 = (f32[3,16,128]{2,1,0:T(8,128)S(1)}, f32[3,16,128]{2,1,0:T(8,128)S(1)}, u32[]{:S(2)}, u32[]{:S(2)}) collective-permute-start(f32[3,16,128]{2,1,0:T(8,128)S(1)} %get-tuple-element.21), channel_id=1, source_target_pairs={{1,0},{2,1},{3,2},{4,3},{5,4},{6,5},{7,6},{8,7},{9,8},{10,9},{11,1... | collective-permute-start | bytes 73736 | tf_op jit(solution)/shard_map/ppermute | solution.py:220
  54.3 0.0 collective-permute-done.2.from_prev
  54.4 7.5 %collective-permute-done.3.from_next = f32[3,16,128]{2,1,0:T(8,128)S(1)} collective-permute-done((f32[3,16,128]{2,1,0:T(8,128)S(1)}, f32[3,16,128]{2,1,0:T(8,128)S(1)}, u32[]{:S(2)}, u32[]{:S(2)}) %collective-permute-start.3) | collective-permute-done | bytes 24608 | tf_op jit(solution)/shard_map/ppermute | solution.py:220
  61.8 0.0 collective-permute-done.5.force
  61.8 0.7 %finish_kernel.1 = (f32[3,32,128]{2,1,0:T(8,128)}, f32[3,128,128]{2,1,0:T(8,128)}) custom-call(f32[3,32,128]{2,1,0:T(8,128)S(1)} %get-tuple-element.16.own, f32[3,16,128]{2,1,0:T(8,128)S(1)} %collective-permute-done.2.from_prev, f32[3,16,128]{2,1,0:T(8,128)S(1)} %collective-permute-done.3.from_next, f32[3,128,128]{2,1,0:T(8,128)S(1)} %collective-permute-done.5.force), custom_call_target="tpu_custom_call" | custom-call | flops 1048576 | bytes 1048576 | tf_op jit(solution)/shard_map/finish_kernel/pallas_call | solution.py:302
  62.5 0.0 all-to-all-done.1
  62.5 1.3 %slave_kernel.1 = f32[3,128,128]{2,1,0:T(8,128)} custom-call(bf16[512,384]{1,0:T(8,128)(2,1)S(1)} %bitcast.38, bf16[512,128]{1,0:T(8,128)(2,1)S(1)} %get-tuple-element.27.place, bf16[128,128]{1,0:T(8,128)(2,1)S(1)} %copy-done.1), custom_call_target="tpu_custom_call" | custom-call | flops 134217728 | bytes 1048576 | tf_op jit(solution)/shard_map/slave_kernel/pallas_call | solution.py:305
  (4 shorter events, 0.0 us)
Async XLA Ops:
  0.6 0.7 %copy-start.12 = (s32[1,128,2]{1,2,0:T(2,128)S(1)}, s32[1,128,2]{1,2,0:T(2,128)}, u32[]{:S(2)}) copy-start(s32[1,128,2]{1,2,0:T(2,128)} %param.23) | copy-start | bytes 3076
  0.6 0.7 %copy-start.11 = (s32[1,128,2]{1,2,0:T(2,128)S(1)}, s32[1,128,2]{1,2,0:T(2,128)}, u32[]{:S(2)}) copy-start(s32[1,128,2]{1,2,0:T(2,128)} %param.22) | copy-start | bytes 3076
  0.7 0.7 %copy-start.13 = (s32[1,128]{1,0:T(1,128)S(1)}, s32[1,128]{1,0:T(1,128)}, u32[]{:S(2)}) copy-start(s32[1,128]{1,0:T(1,128)} %active.1) | copy-start | bytes 1540
  1.3 0.9 %copy-start.2 = (f32[1,128,3,128]{3,1,2,0:T(8,128)S(1)}, f32[1,128,3,128]{3,1,2,0:T(8,128)}, u32[]{:S(2)}) copy-start(f32[1,128,3,128]{3,1,2,0:T(8,128)} %param.26) | copy-start | bytes 589828
  2.3 0.9 %copy-start.4 = (bf16[1,128,3,128]{3,1,2,0:T(8,128)(2,1)S(1)}, bf16[1,128,3,128]{3,1,2,0:T(8,128)(2,1)}, u32[]{:S(2)}) copy-start(bf16[1,128,3,128]{3,1,2,0:T(8,128)(2,1)} %param.21) | copy-start | bytes 294916
  3.2 0.9 %copy-start.5 = (bf16[1,128,3,128]{3,1,2,0:T(8,128)(2,1)S(1)}, bf16[1,128,3,128]{3,1,2,0:T(8,128)(2,1)}, u32[]{:S(2)}) copy-start(bf16[1,128,3,128]{3,1,2,0:T(8,128)(2,1)} %param.27) | copy-start | bytes 294916
  4.0 0.8 %copy-start.7 = (f32[1,128,128]{2,1,0:T(8,128)S(1)}, f32[1,128,128]{2,1,0:T(8,128)}, u32[]{:S(2)}) copy-start(f32[1,128,128]{2,1,0:T(8,128)} %param.25) | copy-start | bytes 196612
  6.2 11.3 %copy-start = (f32[1,3,4096]{2,0,1:T(1,128)S(1)}, f32[1,3,4096]{2,0,1:T(1,128)}, u32[]{:S(2)}) copy-start(f32[1,3,4096]{2,0,1:T(1,128)} %param.15) | copy-start | bytes 147460
  6.2 23.0 %copy-start.3 = (s32[1,8,4096]{2,1,0:T(8,128)S(1)}, s32[1,8,4096]{2,1,0:T(8,128)}, u32[]{:S(2)}) copy-start(s32[1,8,4096]{2,1,0:T(8,128)} %param.16) | copy-start | bytes 393220
  6.2 23.0 %copy-start.8 = (f32[1,3,4096]{2,0,1:T(1,128)S(1)}, f32[1,3,4096]{2,0,1:T(1,128)}, u32[]{:S(2)}) copy-start(f32[1,3,4096]{2,0,1:T(1,128)} %param.20) | copy-start | bytes 147460
  6.2 23.0 %copy-start.10 = (f32[1,4096]{1,0:T(1,128)S(1)}, f32[1,4096]{1,0:T(1,128)}, u32[]{:S(2)}) copy-start(f32[1,4096]{1,0:T(1,128)} %param.19) | copy-start | bytes 49156
  6.2 28.8 %all-to-all-start = ((bf16[64,8,512]{2,1,0:T(8,128)(2,1)}), bf16[64,8,512]{2,1,0:T(8,128)(2,1)S(1)}, u32[]{:S(2)}, u32[]{:S(2)}) async-start(bf16[64,8,512]{2,1,0:T(8,128)(2,1)} %bitcast.19), calls=%async_computation | async-start | bytes 1048576 | tf_op jit(solution)/shard_map/all_to_all | solution.py:228
  17.5 11.8 %copy-start.6 = (f32[1,6,4096]{2,0,1:T(1,128)S(1)}, f32[1,6,4096]{2,0,1:T(1,128)}, u32[]{:S(2)}) copy-start(f32[1,6,4096]{2,0,1:T(1,128)} %param.17) | copy-start | bytes 294916
  17.5 11.7 %copy-start.9 = (f32[1,4096]{1,0:T(1,128)S(1)}, f32[1,4096]{1,0:T(1,128)}, u32[]{:S(2)}) copy-start(f32[1,4096]{1,0:T(1,128)} %param.18) | copy-start | bytes 49156
  17.5 10.3 %collective-permute-start.1 = (f32[3,16,128]{2,1,0:T(8,128)S(1)}, f32[3,16,128]{2,1,0:T(8,128)S(1)}, u32[]{:S(2)}, u32[]{:S(2)}) collective-permute-start(f32[3,16,128]{2,1,0:T(8,128)S(1)} %get-tuple-element.35), channel_id=1, source_target_pairs={{1,0},{2,1},{3,2},{4,3},{5,4},{6,5},{7,6},{8,7},{9,8},{10,9},{11,1... | collective-permute-start | bytes 73736 | tf_op jit(solution)/shard_map/ppermute | solution.py:220
  20.4 8.8 %collective-permute-start = (f32[3,16,128]{2,1,0:T(8,128)S(1)}, f32[3,16,128]{2,1,0:T(8,128)S(1)}, u32[]{:S(2)}, u32[]{:S(2)}) collective-permute-start(f32[3,16,128]{2,1,0:T(8,128)S(1)} %get-tuple-element.36), channel_id=1, source_target_pairs={{0,1},{1,2},{2,3},{3,4},{4,5},{5,6},{6,7},{7,8},{8,9},{9,10},{10,1... | collective-permute-start | bytes 73736 | tf_op jit(solution)/shard_map/ppermute | solution.py:220
  27.7 7.4 %collective-permute-start.4 = (f32[4,128,128]{2,1,0:T(8,128)S(1)}, f32[4,128,128]{2,1,0:T(8,128)S(1)}, u32[]{:S(2)}, u32[]{:S(2)}) collective-permute-start(f32[4,128,128]{2,1,0:T(8,128)S(1)} %get-tuple-element.23), channel_id=1, source_target_pairs={{0,64},{64,0},{1,65},{65,1},{2,66},{66,2},{3,67},{67,3},{4,68},{68... | collective-permute-start | bytes 786440 | tf_op jit(solution)/shard_map/ppermute | solution.py:224
  29.3 5.8 %copy-start.1 = (bf16[128,128]{1,0:T(8,128)(2,1)S(1)}, bf16[128,128]{1,0:T(8,128)(2,1)}, u32[]{:S(2)}) copy-start(bf16[128,128]{1,0:T(8,128)(2,1)} %coupling.3) | copy-start | bytes 98308
  35.1 0.7 %copy-start.14 = (f32[128]{0:T(128)S(1)}, f32[128]{0:T(128)}, u32[]{:S(2)}) copy-start(f32[128]{0:T(128)} %param.29) | copy-start | bytes 1540
  37.8 24.8 %all-to-all-start.1 = ((bf16[64,8,384]{2,1,0:T(8,128)(2,1)}), bf16[64,8,384]{2,1,0:T(8,128)(2,1)S(1)}, u32[]{:S(2)}, u32[]{:S(2)}) async-start(bf16[64,8,384]{2,1,0:T(8,128)(2,1)} %bitcast.23), calls=%async_computation.1 | async-start | bytes 786432 | tf_op jit(solution)/shard_map/all_to_all | solution.py:228
  48.4 13.4 %collective-permute-start.5 = (f32[3,128,128]{2,1,0:T(8,128)S(1)}, f32[3,128,128]{2,1,0:T(8,128)S(1)}, u32[]{:S(2)}, u32[]{:S(2)}) collective-permute-start(f32[3,128,128]{2,1,0:T(8,128)S(1)} %get-tuple-element.24), channel_id=1, source_target_pairs={{0,64},{64,0},{1,65},{65,1},{2,66},{66,2},{3,67},{67,3},{4,68},{68... | collective-permute-start | bytes 589832 | tf_op jit(solution)/shard_map/ppermute | solution.py:224
  48.5 5.9 %collective-permute-start.2 = (f32[3,16,128]{2,1,0:T(8,128)S(1)}, f32[3,16,128]{2,1,0:T(8,128)S(1)}, u32[]{:S(2)}, u32[]{:S(2)}) collective-permute-start(f32[3,16,128]{2,1,0:T(8,128)S(1)} %get-tuple-element.20), channel_id=1, source_target_pairs={{0,1},{1,2},{2,3},{3,4},{4,5},{5,6},{6,7},{7,8},{8,9},{9,10},{10,1... | collective-permute-start | bytes 73736 | tf_op jit(solution)/shard_map/ppermute | solution.py:220
  51.9 9.9 %collective-permute-start.3 = (f32[3,16,128]{2,1,0:T(8,128)S(1)}, f32[3,16,128]{2,1,0:T(8,128)S(1)}, u32[]{:S(2)}, u32[]{:S(2)}) collective-permute-start(f32[3,16,128]{2,1,0:T(8,128)S(1)} %get-tuple-element.21), channel_id=1, source_target_pairs={{1,0},{2,1},{3,2},{4,3},{5,4},{6,5},{7,6},{8,7},{9,8},{10,9},{11,1... | collective-permute-start | bytes 73736 | tf_op jit(solution)/shard_map/ppermute | solution.py:220

commit v3 on v2

--- a/solution.py
+++ b/solution.py
@@ -1,5 +1,3 @@
-import functools
-
 import jax
 import jax.numpy as jnp
 import numpy as np
@@ -7,6 +5,7 @@
 from jax.experimental import pallas as pl
 from jax.experimental.pallas import tpu as pltpu
 from jax.sharding import PartitionSpec as P
+
 
 LANES = 128
 WINDOW = 48
@@ -30,11 +29,12 @@
     return lax.broadcasted_iota(jnp.int32, shape, dim).astype(dtype)
 
 
-def element_kernel(low, own, high, links, strain, edge_ref, yield_ref, ext, prev_out, next_out, own_out,
+def element_kernel(parity, far, near, own, links, strain, edge_ref, yield_ref, ext, far_out, near_out, own_out,
                    disp, lo_s, hi_s, force_s, acc):
-    disp[:, 0:HALO, :] = low[...]
+    odd = parity[0:1, :] == 1
+    disp[:, 0:HALO, :] = jnp.where(odd, near[...], far[...])
     disp[:, HALO : HALO + BLOCKS, :] = own[...]
-    disp[:, HALO + BLOCKS : 2 * HALO + BLOCKS, :] = high[...]
+    disp[:, HALO + BLOCKS : 2 * HALO + BLOCKS, :] = jnp.where(odd, far[...], near[...])
     acc[...] = jnp.zeros_like(acc)
     lane = iota((8, LANES), 1)
     block = iota((8, LANES), 0)
@@ -116,18 +116,20 @@
             sums = sums + dot(jnp.concatenate(left, axis=1), jnp.concatenate(right, axis=1), NT)
         for i in range(3):
             acc[i, 8 * m : 8 * m + WINDOW, :] += sums[i * WINDOW : (i + 1) * WINDOW]
-    prev_out[...] = acc[:, 0:HALO, :]
-    next_out[...] = acc[:, HALO + BLOCKS : 2 * HALO + BLOCKS, :]
+    low, high = acc[:, 0:HALO, :], acc[:, HALO + BLOCKS : 2 * HALO + BLOCKS, :]
+    far_out[...] = jnp.where(odd, high, low)
+    near_out[...] = jnp.where(odd, low, high)
     own_out[...] = acc[:, HALO : HALO + BLOCKS, :] - ext[...]
 
 
-def finish_kernel(own, from_prev, from_next, force, out, force_out):
+def finish_kernel(parity, own, far, near, force, out, force_out):
+    odd = parity[0:1, :] == 1
     force_out[...] = force[...]
-    out[:, 0:HALO, :] = own[:, 0:HALO, :] + from_prev[...]
-    out[:, HALO:BLOCKS, :] = own[:, HALO:BLOCKS, :] + from_next[...]
-
-
-def pack_kernel(owner, where, active, disp, gap, normal, mdisp, send, place, rows):
+    out[:, 0:HALO, :] = own[:, 0:HALO, :] + jnp.where(odd, near[...], far[...])
+    out[:, HALO:BLOCKS, :] = own[:, HALO:BLOCKS, :] + jnp.where(odd, far[...], near[...])
+
+
+def pack_kernel(owner, where, active, disp, send, place):
     names = iota((PEERS, SEG), 0)
     earlier = jnp.where(iota((SEG, SEG), 0) < iota((SEG, SEG), 1), 1.0, 0.0).astype(BF16)
     ones = jnp.ones((SEG, SEG), BF16)
@@ -149,6 +151,9 @@
     for c in range(3):
         send[:, c * LANES : (c + 1) * LANES] = dot(sent, disp[c]).astype(BF16)
     send[:, 3 * LANES :] = dot(meta.astype(BF16), ones).astype(BF16)
+
+
+def rows_kernel(gap, normal, mdisp, rows):
     total = gap[...]
     for c in range(3):
         n = normal[c]
@@ -202,22 +207,21 @@
 VMEM = pl.BlockSpec(memory_space=pltpu.VMEM)
 
 
-def call(kernel, ins, outs, cost, scratch=()):
+def call(kernel, ins, outs, cost, scratch=(), grant=8 << 20):
     return pl.pallas_call(
         kernel,
         out_shape=outs,
-        in_specs=[VMEM] * ins,
-        out_specs=jax.tree.map(lambda _: VMEM, outs),
+        in_specs=[VMEM] * ins if ins > 0 else [pl.BlockSpec()] * -ins,
+        out_specs=jax.tree.map(lambda _: VMEM if ins > 0 else pl.BlockSpec(), outs),
         scratch_shapes=scratch,
-        compiler_params=pltpu.CompilerParams(vmem_limit_bytes=8 << 20),
+        compiler_params=pltpu.CompilerParams(vmem_limit_bytes=grant),
         cost_estimate=pl.CostEstimate(flops=cost, bytes_accessed=1 << 20, transcendentals=0),
-        name=kernel.__name__,
-    )
-
-
-def shifted(block, distance):
-    devices = range(PEERS)
-    return lax.ppermute(block, "dom", [(i - distance, i) for i in devices if i - distance in devices])
+    )
+
+
+def paired(block, first):
+    route = [(i, i + 1) for i in range(first, PEERS - 1, 2)]
+    return lax.ppermute(block, "dom", route + [(j, i) for i, j in route])
 
 
 def swapped(block):
@@ -246,34 +250,29 @@
     quad_weight,
 ):
     seg_major = lambda x: jnp.transpose(x[0], (1, 0, 2))
-    send, place, rows = call(
+    send, place = call(
         pack_kernel,
-        7,
-        (
-            shape(PEERS * SLOTS, 4 * LANES, dtype=BF16),
-            shape(PEERS * SLOTS, SEG, dtype=BF16),
-            shape(4, SEG, LANES),
-        ),
+        -4,
+        (shape(PEERS * SLOTS, 4 * LANES, dtype=BF16), shape(PEERS * SLOTS, SEG, dtype=BF16)),
         1 << 27,
-    )(
-        pair_owner[0].T,
-        pair_local[0].T,
-        active,
-        seg_major(slave_disp),
-        master_gap[0],
-        seg_major(master_normal),
-        seg_major(master_disp),
-    )
+        grant=60 << 20,
+    )(pair_owner[0].T, pair_local[0].T, active, seg_major(slave_disp))
     got = exchanged(send)
 
     own = displacement[0].reshape(3, BLOCKS, LANES)
-    low = shifted(own[:, BLOCKS - HALO :], 1)
-    high = shifted(own[:, :HALO], -1)
+    odd = lax.axis_index("dom") & 1
+    parity = jnp.full((8, LANES), odd, jnp.int32)
+    first, last = own[:, :HALO], own[:, BLOCKS - HALO :]
+    far = paired(jnp.where(odd == 1, last, first), 1)
+    near = paired(jnp.where(odd == 1, first, last), 0)
+    rows = call(rows_kernel, 3, shape(4, SEG, LANES), 1 << 20)(
+        master_gap[0], seg_major(master_normal), seg_major(master_disp)
+    )
     rows = swapped(rows)
     links = jnp.transpose(connectivity[0].reshape(8, BLOCKS, LANES), (1, 0, 2)).reshape(8 * BLOCKS, LANES)
-    to_prev, to_next, own_force = call(
+    far_force, near_force, own_force = call(
         element_kernel,
-        8,
+        9,
         (shape(3, HALO, LANES), shape(3, HALO, LANES), shape(3, BLOCKS, LANES)),
         1 << 32,
         (
@@ -284,9 +283,10 @@
             pltpu.VMEM((3, 2 * HALO + BLOCKS + 16, LANES), F32),
         ),
     )(
-        low,
+        parity,
+        far,
+        near,
         own,
-        high,
         links,
         plastic_strain[0].reshape(6, BLOCKS, LANES),
         element_size.reshape(BLOCKS, LANES),
@@ -294,13 +294,13 @@
         external_force[0].reshape(3, BLOCKS, LANES),
     )
 
-    got, to_prev, to_next = lax.optimization_barrier((got, to_prev, to_next))
+    got, far_force, near_force = lax.optimization_barrier((got, far_force, near_force))
     back, force = call(
         master_kernel, 4, (shape(PEERS * SLOTS, 3 * LANES, dtype=BF16), shape(3, SEG, LANES)), 1 << 28
     )(got, rows, coupling, quad_weight.reshape(1, LANES))
     returned = exchanged(back)
-    residual, master_force = call(finish_kernel, 4, (shape(3, BLOCKS, LANES), shape(3, SEG, LANES)), 1 << 20)(
-        own_force, shifted(to_next, 1), shifted(to_prev, -1), swapped(force)
+    residual, master_force = call(finish_kernel, 5, (shape(3, BLOCKS, LANES), shape(3, SEG, LANES)), 1 << 20)(
+        parity, own_force, paired(far_force, 1), paired(near_force, 0), swapped(force)
     )
     slave_force = call(slave_kernel, 3, shape(3, SEG, LANES), 1 << 27)(returned, place, coupling)
     return (

time: 64.4 us -> 56.7 us (0.88)
  starting transfers between devices: 38.1 us -> 29.5 us
  local copies, waits for them, and re-layouts: 4.89 us -> 0.93 us
  waiting for transfers between devices: 8.86 us -> 12.2 us
  Pallas kernels: 11.2 us -> 12.2 us
    ppermute x4, starting transfers between devices: 16 us -> 8.36 us  [paired(): return lax.ppermute(block, 'dom', route + [(j, i) for i, j in route])]
    unnamed x30 -> x24, local copies, waits for them, and re-layouts: 4.89 us -> 0.92 us
    ppermute x4, waiting for transfers between devices: 8.85 us -> 12.2 us  [paired(): return lax.ppermute(block, 'dom', route + [(j, i) for i, j in route])]
    pallas_call x3 -> x4, Pallas kernels: 7.82 us -> 8.82 us  [the longest x1 5.82 us: local(): call(element_kernel, 9, (shape(3, HALO, LANES), shape(3, HALO, LANES), sh...]
    all_to_all x2, starting transfers between devices: 21.9 us -> 21 us  [exchanged(): return lax.all_to_all(block, 'dom', split_axis=0, concat_axis=0, tiled=True)]
  transfers between devices with their start and end apart: 8 -> 8, of which waited for: 2 -> 3; matrix products, arithmetic and copies ran while one was open for 0% -> 0% of each run, Pallas kernels for 10% -> 12%
where the time goes in v3:
time: 56.7 us; the launch traced here: 55.7 us
  starting transfers between devices  29.5 us (52%)
  Pallas kernels  12.2 us (22%)
  waiting for transfers between devices  12.2 us (22%)
  local copies, waits for them, and re-layouts  0.93 us (2%)
  between operations  0.87 us (2%)
    all_to_all x2, starting transfers between devices, exchanged(): return lax.all_to_all(block, 'dom', split_axis=0, concat_axis=0, tiled=True)  21 us
    ppermute x4, waiting for transfers between devices, paired(): return lax.ppermute(block, 'dom', route + [(j, i) for i, j in route])  12.2 us
    ppermute x4, starting transfers between devices, paired(): return lax.ppermute(block, 'dom', route + [(j, i) for i, j in route])  8.36 us
    pallas_call x1, Pallas kernels, local(): call(element_kernel, 9, (shape(3, HALO, LANES), shape(3, HALO, LANES), sh...  5.82 us
    pallas_call x1, Pallas kernels, local(): call(pack_kernel, -4, (shape(PEERS * SLOTS, 4 * LANES, dtype=BF16), shape...  2.26 us
    pallas_call x1, Pallas kernels, local(): call(master_kernel, 4, (shape(PEERS * SLOTS, 3 * LANES, dtype=BF16), shap...  2.01 us
    pallas_call x1, Pallas kernels, local(): call(slave_kernel, 3, shape(3, SEG, LANES), 1 << 27)  1.33 us
  transfers between devices with their start and end apart: 8, of which 3 were waited for; matrix products, arithmetic and copies ran while one was open for 0% of the time, Pallas kernels for 12%

profile of v3, /device:TPU:30, one launch (start us, length us, event | category | flops | bytes accessed | tf_op | source)
XLA Modules:
  0.0 55.7 jit_solution(1031957691565072306)
XLA Ops:
  0.6 2.3 %shard_map.167 = (bf16[512,512]{1,0:T(8,128)(2,1)}, bf16[512,128]{1,0:T(8,128)(2,1)}) custom-call(s32[2,128]{1,0:T(2,128)} %bitcast.56, s32[2,128]{1,0:T(2,128)} %bitcast.57, s32[1,128]{1,0:T(1,128)} %active.1, bf16[3,128,128]{2,1,0:T(8,128)(2,1)} %bitcast.54), custom_call_target="tpu_custom_call" | custom-call | flops 134217728 | bytes 1048576 | tf_op jit(solution)/shard_map/pallas_call | solution.py:253
  2.9 0.0 copy-start.4
  2.9 0.0 copy-start
  2.9 0.0 copy-start.3
  2.9 11.3 %all-to-all-start = ((bf16[64,8,512]{2,1,0:T(8,128)(2,1)}), bf16[64,8,512]{2,1,0:T(8,128)(2,1)S(1)}, u32[]{:S(2)}, u32[]{:S(2)}) async-start(bf16[64,8,512]{2,1,0:T(8,128)(2,1)} %bitcast.51), calls=%async_computation | async-start | bytes 1048576 | tf_op jit(solution)/shard_map/all_to_all | solution.py:232
  14.2 0.0 copy-start.2
  14.2 0.0 copy-done.4
  14.2 0.9 %collective-permute-start.1 = (f32[3,16,128]{2,1,0:T(8,128)S(1)}, f32[3,16,128]{2,1,0:T(8,128)S(1)}, u32[]{:S(2)}, u32[]{:S(2)}) collective-permute-start(f32[3,16,128]{2,1,0:T(8,128)S(1)} %get-tuple-element.33), channel_id=1, source_target_pairs={{0,1},{2,3},{4,5},{6,7},{8,9},{10,11},{12,13},{14,15},{16,17},{18,... | collective-permute-start | bytes 73736 | tf_op jit(solution)/shard_map/ppermute | solution.py:224
  15.1 4.0 %collective-permute-start = (f32[3,16,128]{2,1,0:T(8,128)S(1)}, f32[3,16,128]{2,1,0:T(8,128)S(1)}, u32[]{:S(2)}, u32[]{:S(2)}) collective-permute-start(f32[3,16,128]{2,1,0:T(8,128)S(1)} %get-tuple-element.34), channel_id=1, source_target_pairs={{1,2},{3,4},{5,6},{7,8},{9,10},{11,12},{13,14},{15,16},{17,18},{19... | collective-permute-start | bytes 73736 | tf_op jit(solution)/shard_map/ppermute | solution.py:224
  19.1 0.0 copy-done
  19.1 0.0 copy-done.3
  19.1 0.0 copy-done.2
  19.1 0.0 copy-start.6
  19.2 0.0 copy-start.7
  19.2 0.0 copy-start.8
  19.2 0.0 copy-start.9
  19.2 0.0 copy-start.10
  19.2 0.1 collective-permute-start.4
  19.3 1.6 %collective-permute-done.1.near = f32[3,16,128]{2,1,0:T(8,128)S(1)} collective-permute-done((f32[3,16,128]{2,1,0:T(8,128)S(1)}, f32[3,16,128]{2,1,0:T(8,128)S(1)}, u32[]{:S(2)}, u32[]{:S(2)}) %collective-permute-start.1) | collective-permute-done | bytes 24608 | tf_op jit(solution)/shard_map/ppermute | solution.py:224
  21.0 4.1 %collective-permute-done.far = f32[3,16,128]{2,1,0:T(8,128)S(1)} collective-permute-done((f32[3,16,128]{2,1,0:T(8,128)S(1)}, f32[3,16,128]{2,1,0:T(8,128)S(1)}, u32[]{:S(2)}, u32[]{:S(2)}) %collective-permute-start) | collective-permute-done | bytes 24608 | tf_op jit(solution)/shard_map/ppermute | solution.py:224
  25.1 0.0 copy-done.6
  25.1 0.0 copy-done.7
  25.1 0.0 copy-done.8
  25.1 0.0 copy-done.9
  25.1 0.0 copy-done.10
  25.1 0.0 copy-start.5
  25.1 5.8 %shard_map.166 = (f32[3,16,128]{2,1,0:T(8,128)S(1)}, f32[3,16,128]{2,1,0:T(8,128)S(1)}, f32[3,32,128]{2,1,0:T(8,128)S(1)}) custom-call(s32[8,128]{1,0:T(8,128)S(1)} %broadcast_in_dim.9.parity, f32[3,16,128]{2,1,0:T(8,128)S(1)} %collective-permute-done.far, f32[3,16,128]{2,1,0:T(8,128)S(1)} %collective-permute-done.1.near, f32[3,32,128]{2,1,0:T(8,128)S(1)} %bitcast.44, ...), custom_call_target="tpu_custom_call" | custom-call | flops 4294967296 | bytes 1048576 | tf_op jit(solution)/shard_map/pallas_call | solution.py:273
  30.9 0.0 all-to-all-done
  31.0 0.0 copy-start.11
  31.0 0.0 collective-permute-done.4.rows
  31.0 0.0 copy-done.5
  31.0 0.6 %copy-done.11 = f32[128]{0:T(128)S(1)} copy-done((f32[128]{0:T(128)S(1)}, f32[128]{0:T(128)}, u32[]{:S(2)}) %copy-start.11) | copy-done | bytes 536
  31.6 2.0 %shard_map.169 = (bf16[512,384]{1,0:T(8,128)(2,1)}, f32[3,128,128]{2,1,0:T(8,128)S(1)}) custom-call(bf16[512,512]{1,0:T(8,128)(2,1)S(1)} %bitcast.39, f32[4,128,128]{2,1,0:T(8,128)S(1)} %collective-permute-done.4.rows, bf16[128,128]{1,0:T(8,128)(2,1)S(1)} %copy-done.5, f32[1,128]{1,0:T(1,128)S(1)} %bitcast.50), custom_call_target="tpu_custom_call" | custom-call | flops 268435456 | bytes 1048576 | tf_op jit(solution)/shard_map/pallas_call | solution.py:298
  33.6 9.8 %all-to-all-start.1 = ((bf16[64,8,384]{2,1,0:T(8,128)(2,1)}), bf16[64,8,384]{2,1,0:T(8,128)(2,1)S(1)}, u32[]{:S(2)}, u32[]{:S(2)}) async-start(bf16[64,8,384]{2,1,0:T(8,128)(2,1)} %bitcast.23), calls=%async_computation.1 | async-start | bytes 786432 | tf_op jit(solution)/shard_map/all_to_all | solution.py:232
  43.4 0.1 collective-permute-start.5
  43.5 3.4 %collective-permute-start.2 = (f32[3,16,128]{2,1,0:T(8,128)S(1)}, f32[3,16,128]{2,1,0:T(8,128)S(1)}, u32[]{:S(2)}, u32[]{:S(2)}) collective-permute-start(f32[3,16,128]{2,1,0:T(8,128)S(1)} %get-tuple-element.19), channel_id=1, source_target_pairs={{1,2},{3,4},{5,6},{7,8},{9,10},{11,12},{13,14},{15,16},{17,18},{19... | collective-permute-start | bytes 73736 | tf_op jit(solution)/shard_map/ppermute | solution.py:224
  46.9 0.1 collective-permute-start.3
  47.0 6.5 %collective-permute-done.2.far = f32[3,16,128]{2,1,0:T(8,128)S(1)} collective-permute-done((f32[3,16,128]{2,1,0:T(8,128)S(1)}, f32[3,16,128]{2,1,0:T(8,128)S(1)}, u32[]{:S(2)}, u32[]{:S(2)}) %collective-permute-start.2) | collective-permute-done | bytes 24608 | tf_op jit(solution)/shard_map/ppermute | solution.py:224
  53.4 0.0 collective-permute-done.3.near
  53.4 0.0 collective-permute-done.5.force
  53.4 0.0 copy-start.1
  53.4 0.7 %shard_map.170 = (f32[3,32,128]{2,1,0:T(8,128)}, f32[3,128,128]{2,1,0:T(8,128)}) custom-call(s32[8,128]{1,0:T(8,128)S(1)} %broadcast_in_dim.9.parity, f32[3,32,128]{2,1,0:T(8,128)S(1)} %get-tuple-element.15.own, f32[3,16,128]{2,1,0:T(8,128)S(1)} %collective-permute-done.2.far, f32[3,16,128]{2,1,0:T(8,128)S(1)} %collective-permute-done.3.near, ...), custom_call_target="tpu_custom_call" | custom-call | flops 1048576 | bytes 1048576 | tf_op jit(solution)/shard_map/pallas_call | solution.py:302
  54.1 0.0 all-to-all-done.1
  54.2 0.2 copy-done.1
  54.4 1.3 %shard_map.171 = f32[3,128,128]{2,1,0:T(8,128)} custom-call(bf16[512,384]{1,0:T(8,128)(2,1)S(1)} %bitcast.38, bf16[512,128]{1,0:T(8,128)(2,1)S(1)} %copy-done.1, bf16[128,128]{1,0:T(8,128)(2,1)S(1)} %copy-done.5), custom_call_target="tpu_custom_call" | custom-call | flops 134217728 | bytes 1048576 | tf_op jit(solution)/shard_map/pallas_call | solution.py:305
  (3 shorter events, 0.0 us)
Async XLA Ops:
  2.9 11.3 %copy-start.4 = (f32[1,3,4096]{2,0,1:T(1,128)S(1)}, f32[1,3,4096]{2,0,1:T(1,128)}, u32[]{:S(2)}) copy-start(f32[1,3,4096]{2,0,1:T(1,128)} %param.15) | copy-start | bytes 147460
  2.9 16.2 %copy-start = (f32[1,128,3,128]{3,1,2,0:T(8,128)S(1)}, f32[1,128,3,128]{3,1,2,0:T(8,128)}, u32[]{:S(2)}) copy-start(f32[1,128,3,128]{3,1,2,0:T(8,128)} %param.26) | copy-start | bytes 589828
  2.9 16.2 %copy-start.3 = (f32[1,128,128]{2,1,0:T(8,128)S(1)}, f32[1,128,128]{2,1,0:T(8,128)}, u32[]{:S(2)}) copy-start(f32[1,128,128]{2,1,0:T(8,128)} %param.25) | copy-start | bytes 196612
  2.9 28.0 %all-to-all-start = ((bf16[64,8,512]{2,1,0:T(8,128)(2,1)}), bf16[64,8,512]{2,1,0:T(8,128)(2,1)S(1)}, u32[]{:S(2)}, u32[]{:S(2)}) async-start(bf16[64,8,512]{2,1,0:T(8,128)(2,1)} %bitcast.51), calls=%async_computation | async-start | bytes 1048576 | tf_op jit(solution)/shard_map/all_to_all | solution.py:232
  14.2 5.0 %copy-start.2 = (bf16[1,128,3,128]{3,1,2,0:T(8,128)(2,1)S(1)}, bf16[1,128,3,128]{3,1,2,0:T(8,128)(2,1)}, u32[]{:S(2)}) copy-start(bf16[1,128,3,128]{3,1,2,0:T(8,128)(2,1)} %param.27) | copy-start | bytes 294916
  14.2 6.7 %collective-permute-start.1 = (f32[3,16,128]{2,1,0:T(8,128)S(1)}, f32[3,16,128]{2,1,0:T(8,128)S(1)}, u32[]{:S(2)}, u32[]{:S(2)}) collective-permute-start(f32[3,16,128]{2,1,0:T(8,128)S(1)} %get-tuple-element.33), channel_id=1, source_target_pairs={{0,1},{2,3},{4,5},{6,7},{8,9},{10,11},{12,13},{14,15},{16,17},{18,... | collective-permute-start | bytes 73736 | tf_op jit(solution)/shard_map/ppermute | solution.py:224
  15.1 9.9 %collective-permute-start = (f32[3,16,128]{2,1,0:T(8,128)S(1)}, f32[3,16,128]{2,1,0:T(8,128)S(1)}, u32[]{:S(2)}, u32[]{:S(2)}) collective-permute-start(f32[3,16,128]{2,1,0:T(8,128)S(1)} %get-tuple-element.34), channel_id=1, source_target_pairs={{1,2},{3,4},{5,6},{7,8},{9,10},{11,12},{13,14},{15,16},{17,18},{19... | collective-permute-start | bytes 73736 | tf_op jit(solution)/shard_map/ppermute | solution.py:224
  19.1 5.9 %copy-start.6 = (s32[1,8,4096]{2,1,0:T(8,128)S(1)}, s32[1,8,4096]{2,1,0:T(8,128)}, u32[]{:S(2)}) copy-start(s32[1,8,4096]{2,1,0:T(8,128)} %param.16) | copy-start | bytes 393220
  19.2 5.9 %copy-start.7 = (f32[1,6,4096]{2,0,1:T(1,128)S(1)}, f32[1,6,4096]{2,0,1:T(1,128)}, u32[]{:S(2)}) copy-start(f32[1,6,4096]{2,0,1:T(1,128)} %param.17) | copy-start | bytes 294916
  19.2 5.9 %copy-start.8 = (f32[1,3,4096]{2,0,1:T(1,128)S(1)}, f32[1,3,4096]{2,0,1:T(1,128)}, u32[]{:S(2)}) copy-start(f32[1,3,4096]{2,0,1:T(1,128)} %param.20) | copy-start | bytes 147460
  19.2 5.9 %copy-start.9 = (f32[1,4096]{1,0:T(1,128)S(1)}, f32[1,4096]{1,0:T(1,128)}, u32[]{:S(2)}) copy-start(f32[1,4096]{1,0:T(1,128)} %param.18) | copy-start | bytes 49156
  19.2 5.9 %copy-start.10 = (f32[1,4096]{1,0:T(1,128)S(1)}, f32[1,4096]{1,0:T(1,128)}, u32[]{:S(2)}) copy-start(f32[1,4096]{1,0:T(1,128)} %param.19) | copy-start | bytes 49156
  19.2 11.7 %collective-permute-start.4 = (f32[4,128,128]{2,1,0:T(8,128)S(1)}, f32[4,128,128]{2,1,0:T(8,128)S(1)}, u32[]{:S(2)}, u32[]{:S(2)}) collective-permute-start(f32[4,128,128]{2,1,0:T(8,128)S(1)} %shard_map.168), channel_id=1, source_target_pairs={{0,64},{64,0},{1,65},{65,1},{2,66},{66,2},{3,67},{67,3},{4,68},{68... | collective-permute-start | bytes 786440 | tf_op jit(solution)/shard_map/ppermute | solution.py:228
  25.1 5.9 %copy-start.5 = (bf16[128,128]{1,0:T(8,128)(2,1)S(1)}, bf16[128,128]{1,0:T(8,128)(2,1)}, u32[]{:S(2)}) copy-start(bf16[128,128]{1,0:T(8,128)(2,1)} %coupling.3) | copy-start | bytes 98308
  31.0 0.7 %copy-start.11 = (f32[128]{0:T(128)S(1)}, f32[128]{0:T(128)}, u32[]{:S(2)}) copy-start(f32[128]{0:T(128)} %param.29) | copy-start | bytes 1540
  33.6 20.5 %all-to-all-start.1 = ((bf16[64,8,384]{2,1,0:T(8,128)(2,1)}), bf16[64,8,384]{2,1,0:T(8,128)(2,1)S(1)}, u32[]{:S(2)}, u32[]{:S(2)}) async-start(bf16[64,8,384]{2,1,0:T(8,128)(2,1)} %bitcast.23), calls=%async_computation.1 | async-start | bytes 786432 | tf_op jit(solution)/shard_map/all_to_all | solution.py:232
  43.4 10.0 %collective-permute-start.5 = (f32[3,128,128]{2,1,0:T(8,128)S(1)}, f32[3,128,128]{2,1,0:T(8,128)S(1)}, u32[]{:S(2)}, u32[]{:S(2)}) collective-permute-start(f32[3,128,128]{2,1,0:T(8,128)S(1)} %get-tuple-element.22), channel_id=1, source_target_pairs={{0,64},{64,0},{1,65},{65,1},{2,66},{66,2},{3,67},{67,3},{4,68},{68... | collective-permute-start | bytes 589832 | tf_op jit(solution)/shard_map/ppermute | solution.py:228
  43.5 9.9 %collective-permute-start.2 = (f32[3,16,128]{2,1,0:T(8,128)S(1)}, f32[3,16,128]{2,1,0:T(8,128)S(1)}, u32[]{:S(2)}, u32[]{:S(2)}) collective-permute-start(f32[3,16,128]{2,1,0:T(8,128)S(1)} %get-tuple-element.19), channel_id=1, source_target_pairs={{1,2},{3,4},{5,6},{7,8},{9,10},{11,12},{13,14},{15,16},{17,18},{19... | collective-permute-start | bytes 73736 | tf_op jit(solution)/shard_map/ppermute | solution.py:224
  46.9 6.6 %collective-permute-start.3 = (f32[3,16,128]{2,1,0:T(8,128)S(1)}, f32[3,16,128]{2,1,0:T(8,128)S(1)}, u32[]{:S(2)}, u32[]{:S(2)}) collective-permute-start(f32[3,16,128]{2,1,0:T(8,128)S(1)} %get-tuple-element.20), channel_id=1, source_target_pairs={{0,1},{2,3},{4,5},{6,7},{8,9},{10,11},{12,13},{14,15},{16,17},{18,... | collective-permute-start | bytes 73736 | tf_op jit(solution)/shard_map/ppermute | solution.py:224
  53.4 1.0 %copy-start.1 = (bf16[512,128]{1,0:T(8,128)(2,1)S(1)}, bf16[512,128]{1,0:T(8,128)(2,1)}, u32[]{:S(2)}) copy-start(bf16[512,128]{1,0:T(8,128)(2,1)} %get-tuple-element.25.place) | copy-start | bytes 393220

commit v4 on v3

--- a/solution.py
+++ b/solution.py
@@ -153,7 +153,9 @@
     send[:, 3 * LANES :] = dot(meta.astype(BF16), ones).astype(BF16)
 
 
-def rows_kernel(gap, normal, mdisp, rows):
+def rows_kernel(gap, normal, mdisp, coupling, quad_weight, rows, mortar, weight):
+    mortar[...] = mortar_of(coupling)
+    weight[...] = jnp.broadcast_to(quad_weight[...], weight.shape)
     total = gap[...]
     for c in range(3):
         n = normal[c]
@@ -172,8 +174,8 @@
     return top, (x - top.astype(F32)).astype(BF16)
 
 
-def master_kernel(got, rows, coupling, weight, back, force):
-    mortar = mortar_of(coupling)
+def master_kernel(got, rows, mortar_ref, weight, back, force):
+    mortar = mortar_ref[...]
     table = [split(rows[c]) for c in range(4)]
     name = iota((SEG, LANES), 1, F32) + 1.0
     totals = [jnp.zeros((SEG, LANES), F32)] * 3
@@ -184,7 +186,7 @@
         normal = (n0, n1, n2)
         for c in range(3):
             gap = gap - normal[c] * dot(got[span, c * LANES : (c + 1) * LANES], mortar)
-        press = weight[...] * (2.0 * jnp.maximum(gap, 0.0))
+        press = weight[0:1, :] * (2.0 * jnp.maximum(gap, 0.0))
         for c in range(3):
             top, low = split(press * normal[c])
             back[span, c * LANES : (c + 1) * LANES] = top
@@ -193,8 +195,8 @@
         force[c] = -totals[c]
 
 
-def slave_kernel(got, place, coupling, out):
-    mortar = mortar_of(coupling)
+def slave_kernel(got, place, mortar_ref, out):
+    mortar = mortar_ref[...]
     for c in range(3):
         pair = dot(place[...], got[:, c * LANES : (c + 1) * LANES], TN).astype(BF16)
         out[c] = dot(pair, mortar, NT)
@@ -265,9 +267,9 @@
     first, last = own[:, :HALO], own[:, BLOCKS - HALO :]
     far = paired(jnp.where(odd == 1, last, first), 1)
     near = paired(jnp.where(odd == 1, first, last), 0)
-    rows = call(rows_kernel, 3, shape(4, SEG, LANES), 1 << 20)(
-        master_gap[0], seg_major(master_normal), seg_major(master_disp)
-    )
+    rows, mortar, weight = call(
+        rows_kernel, 5, (shape(4, SEG, LANES), shape(LANES, LANES, dtype=BF16), shape(8, LANES)), 1 << 20
+    )(master_gap[0], seg_major(master_normal), seg_major(master_disp), coupling, quad_weight.reshape(1, LANES))
     rows = swapped(rows)
     links = jnp.transpose(connectivity[0].reshape(8, BLOCKS, LANES), (1, 0, 2)).reshape(8 * BLOCKS, LANES)
     far_force, near_force, own_force = call(
@@ -297,12 +299,13 @@
     got, far_force, near_force = lax.optimization_barrier((got, far_force, near_force))
     back, force = call(
         master_kernel, 4, (shape(PEERS * SLOTS, 3 * LANES, dtype=BF16), shape(3, SEG, LANES)), 1 << 28
-    )(got, rows, coupling, quad_weight.reshape(1, LANES))
+    )(got, rows, mortar, weight)
     returned = exchanged(back)
+    slave_force = call(slave_kernel, 3, shape(3, SEG, LANES), 1 << 27)(returned, place, mortar)
+    parity_late, slave_force = lax.optimization_barrier((parity, slave_force))
     residual, master_force = call(finish_kernel, 5, (shape(3, BLOCKS, LANES), shape(3, SEG, LANES)), 1 << 20)(
-        parity, own_force, paired(far_force, 1), paired(near_force, 0), swapped(force)
-    )
-    slave_force = call(slave_kernel, 3, shape(3, SEG, LANES), 1 << 27)(returned, place, coupling)
+        parity_late, own_force, paired(far_force, 1), paired(near_force, 0), swapped(force)
+    )
     return (
         residual.reshape(1, 3, BLOCKS * LANES),
         jnp.transpose(slave_force, (1, 0, 2))[None],

time: 56.7 us -> 57 us (level)
  the two profiles are of different devices: /device:TPU:30 before, /device:TPU:0 now
where the time goes in v4:
time: 57 us; the launch traced here: 56.6 us
  starting transfers between devices  32.6 us (57%)
  Pallas kernels  12.2 us (21%)
  waiting for transfers between devices  10.4 us (18%)
  between operations  0.83 us (1%)
  local copies, waits for them, and re-layouts  0.66 us (1%)
    all_to_all x2, starting transfers between devices, exchanged(): return lax.all_to_all(block, 'dom', split_axis=0, concat_axis=0, tiled=True)  25.1 us
    all_to_all x2, waiting for transfers between devices, exchanged(): return lax.all_to_all(block, 'dom', split_axis=0, concat_axis=0, tiled=True)  8.35 us
    ppermute x4, starting transfers between devices, paired(): return lax.ppermute(block, 'dom', route + [(j, i) for i, j in route])  7.32 us
    pallas_call x1, Pallas kernels, local(): call(element_kernel, 9, (shape(3, HALO, LANES), shape(3, HALO, LANES), sh...  5.81 us
    pallas_call x1, Pallas kernels, local(): call(pack_kernel, -4, (shape(PEERS * SLOTS, 4 * LANES, dtype=BF16), shape...  2.27 us
    pallas_call x1, Pallas kernels, local(): call(master_kernel, 4, (shape(PEERS * SLOTS, 3 * LANES, dtype=BF16), shap...  2 us
    ppermute x4, waiting for transfers between devices, paired(): return lax.ppermute(block, 'dom', route + [(j, i) for i, j in route])  1.99 us
    pallas_call x1, Pallas kernels, local(): call(slave_kernel, 3, shape(3, SEG, LANES), 1 << 27)  1.34 us
  transfers between devices with their start and end apart: 8, of which 3 were waited for; matrix products, arithmetic and copies ran while one was open for 0% of the time, Pallas kernels for 13%

profile of v4, /device:TPU:0, one launch (start us, length us, event | category | flops | bytes accessed | tf_op | source)
XLA Modules:
  0.0 56.6 jit_solution(12006149113605181292)
XLA Ops:
  0.6 2.3 %shard_map.166 = (bf16[512,512]{1,0:T(8,128)(2,1)}, bf16[512,128]{1,0:T(8,128)(2,1)}) custom-call(s32[2,128]{1,0:T(2,128)} %bitcast.56, s32[2,128]{1,0:T(2,128)} %bitcast.57, s32[1,128]{1,0:T(1,128)} %active.1, bf16[3,128,128]{2,1,0:T(8,128)(2,1)} %bitcast.54), custom_call_target="tpu_custom_call" | custom-call | flops 134217728 | bytes 1048576 | tf_op jit(solution)/shard_map/pallas_call | solution.py:255
  2.9 0.0 copy-start.4
  2.9 0.0 copy-start
  2.9 0.0 copy-start.3
  2.9 0.0 copy-start.5
  2.9 11.7 %all-to-all-start = ((bf16[64,8,512]{2,1,0:T(8,128)(2,1)}), bf16[64,8,512]{2,1,0:T(8,128)(2,1)S(1)}, u32[]{:S(2)}, u32[]{:S(2)}) async-start(bf16[64,8,512]{2,1,0:T(8,128)(2,1)} %bitcast.51), calls=%async_computation | async-start | bytes 1048576 | tf_op jit(solution)/shard_map/all_to_all | solution.py:234
  14.6 0.0 copy-start.2
  14.6 0.0 copy-done.4
  14.7 1.6 %collective-permute-start.1 = (f32[3,16,128]{2,1,0:T(8,128)S(1)}, f32[3,16,128]{2,1,0:T(8,128)S(1)}, u32[]{:S(2)}, u32[]{:S(2)}) collective-permute-start(f32[3,16,128]{2,1,0:T(8,128)S(1)} %get-tuple-element.43), channel_id=1, source_target_pairs={{0,1},{2,3},{4,5},{6,7},{8,9},{10,11},{12,13},{14,15},{16,17},{18,... | collective-permute-start | bytes 73736 | tf_op jit(solution)/shard_map/ppermute | solution.py:226
  16.3 0.7 %collective-permute-start = (f32[3,16,128]{2,1,0:T(8,128)S(1)}, f32[3,16,128]{2,1,0:T(8,128)S(1)}, u32[]{:S(2)}, u32[]{:S(2)}) collective-permute-start(f32[3,16,128]{2,1,0:T(8,128)S(1)} %get-tuple-element.44), channel_id=1, source_target_pairs={{1,2},{3,4},{5,6},{7,8},{9,10},{11,12},{13,14},{15,16},{17,18},{19... | collective-permute-start | bytes 73736 | tf_op jit(solution)/shard_map/ppermute | solution.py:226
  17.0 0.0 copy-start.6
  17.0 0.0 copy-done
  17.0 0.0 copy-done.3
  17.0 0.0 copy-done.5
  17.0 0.0 copy-done.2
  17.0 0.6 %copy-done.6 = f32[128]{0:T(128)S(1)} copy-done((f32[128]{0:T(128)S(1)}, f32[128]{0:T(128)}, u32[]{:S(2)}) %copy-start.6) | copy-done | bytes 536
  17.6 0.0 copy-start.7
  17.6 0.0 copy-start.8
  17.6 0.0 copy-start.9
  17.6 0.0 copy-start.10
  17.6 0.0 copy-start.11
  17.7 0.1 collective-permute-start.2
  17.8 2.0 %collective-permute-done.1.near = f32[3,16,128]{2,1,0:T(8,128)S(1)} collective-permute-done((f32[3,16,128]{2,1,0:T(8,128)S(1)}, f32[3,16,128]{2,1,0:T(8,128)S(1)}, u32[]{:S(2)}, u32[]{:S(2)}) %collective-permute-start.1) | collective-permute-done | bytes 24608 | tf_op jit(solution)/shard_map/ppermute | solution.py:226
  19.8 0.0 collective-permute-done.far
  19.8 0.0 copy-done.7
  19.8 0.0 copy-done.8
  19.8 0.0 copy-done.9
  19.8 0.0 copy-done.10
  19.8 0.0 copy-done.11
  19.8 5.8 %shard_map.167 = (f32[3,16,128]{2,1,0:T(8,128)S(1)}, f32[3,16,128]{2,1,0:T(8,128)S(1)}, f32[3,32,128]{2,1,0:T(8,128)S(1)}) custom-call(s32[8,128]{1,0:T(8,128)S(1)} %broadcast_in_dim.9.parity, f32[3,16,128]{2,1,0:T(8,128)S(1)} %collective-permute-done.far, f32[3,16,128]{2,1,0:T(8,128)S(1)} %collective-permute-done.1.near, f32[3,32,128]{2,1,0:T(8,128)S(1)} %bitcast.44, ...), custom_call_target="tpu_custom_call" | custom-call | flops 4294967296 | bytes 1048576 | tf_op jit(solution)/shard_map/pallas_call | solution.py:275
  25.6 2.2 %all-to-all-done = bf16[64,8,512]{2,1,0:T(8,128)(2,1)S(1)} async-done(((bf16[64,8,512]{2,1,0:T(8,128)(2,1)}), bf16[64,8,512]{2,1,0:T(8,128)(2,1)S(1)}, u32[]{:S(2)}, u32[]{:S(2)}) %all-to-all-start) | async-done | bytes 524320 | tf_op jit(solution)/shard_map/all_to_all | solution.py:234
  27.9 0.0 collective-permute-done.2.rows
  27.9 2.0 %shard_map.169 = (bf16[512,384]{1,0:T(8,128)(2,1)}, f32[3,128,128]{2,1,0:T(8,128)S(1)}) custom-call(bf16[512,512]{1,0:T(8,128)(2,1)S(1)} %bitcast.39, f32[4,128,128]{2,1,0:T(8,128)S(1)} %collective-permute-done.2.rows, bf16[128,128]{1,0:T(8,128)(2,1)S(1)} %get-tuple-element.25.mortar_ref, f32[8,128]{1,0:T(8,128)S(1)} %get-tuple-element.26.weight), custom_call_target="tpu_custom_call" | custom-call | flops 268435456 | bytes 1048576 | tf_op jit(solution)/shard_map/pallas_call | solution.py:300
  29.9 0.0 copy-start.1
  29.9 13.4 %all-to-all-start.1 = ((bf16[64,8,384]{2,1,0:T(8,128)(2,1)}), bf16[64,8,384]{2,1,0:T(8,128)(2,1)S(1)}, u32[]{:S(2)}, u32[]{:S(2)}) async-start(bf16[64,8,384]{2,1,0:T(8,128)(2,1)} %bitcast.22), calls=%async_computation.1 | async-start | bytes 786432 | tf_op jit(solution)/shard_map/all_to_all | solution.py:234
  43.3 0.1 collective-permute-start.5
  43.4 0.7 %collective-permute-start.3 = (f32[3,16,128]{2,1,0:T(8,128)S(1)}, f32[3,16,128]{2,1,0:T(8,128)S(1)}, u32[]{:S(2)}, u32[]{:S(2)}) collective-permute-start(f32[3,16,128]{2,1,0:T(8,128)S(1)} %get-tuple-element.31), channel_id=1, source_target_pairs={{1,2},{3,4},{5,6},{7,8},{9,10},{11,12},{13,14},{15,16},{17,18},{19... | collective-permute-start | bytes 73736 | tf_op jit(solution)/shard_map/ppermute | solution.py:226
  44.1 4.4 %collective-permute-start.4 = (f32[3,16,128]{2,1,0:T(8,128)S(1)}, f32[3,16,128]{2,1,0:T(8,128)S(1)}, u32[]{:S(2)}, u32[]{:S(2)}) collective-permute-start(f32[3,16,128]{2,1,0:T(8,128)S(1)} %get-tuple-element.32), channel_id=1, source_target_pairs={{0,1},{2,3},{4,5},{6,7},{8,9},{10,11},{12,13},{14,15},{16,17},{18,... | collective-permute-start | bytes 73736 | tf_op jit(solution)/shard_map/ppermute | solution.py:226
  48.4 6.1 %all-to-all-done.1 = bf16[64,8,384]{2,1,0:T(8,128)(2,1)S(1)} async-done(((bf16[64,8,384]{2,1,0:T(8,128)(2,1)}), bf16[64,8,384]{2,1,0:T(8,128)(2,1)S(1)}, u32[]{:S(2)}, u32[]{:S(2)}) %all-to-all-start.1) | async-done | bytes 393248 | tf_op jit(solution)/shard_map/all_to_all | solution.py:234
  54.5 0.0 copy-done.1
  54.6 1.3 %shard_map.170 = f32[3,128,128]{2,1,0:T(8,128)} custom-call(bf16[512,384]{1,0:T(8,128)(2,1)S(1)} %bitcast.38, bf16[512,128]{1,0:T(8,128)(2,1)S(1)} %copy-done.1, bf16[128,128]{1,0:T(8,128)(2,1)S(1)} %get-tuple-element.25.mortar_ref), custom_call_target="tpu_custom_call" | custom-call | flops 134217728 | bytes 1048576 | tf_op jit(solution)/shard_map/pallas_call | solution.py:304
  55.9 0.0 collective-permute-done.3.far
  55.9 0.0 collective-permute-done.4.near
  55.9 0.0 collective-permute-done.5.force
  55.9 0.7 %shard_map.171 = (f32[3,32,128]{2,1,0:T(8,128)}, f32[3,128,128]{2,1,0:T(8,128)}) custom-call(s32[8,128]{1,0:T(8,128)S(1)} %broadcast_in_dim.9.parity, f32[3,32,128]{2,1,0:T(8,128)S(1)} %get-tuple-element.30.own, f32[3,16,128]{2,1,0:T(8,128)S(1)} %collective-permute-done.3.far, f32[3,16,128]{2,1,0:T(8,128)S(1)} %collective-permute-done.4.near, ...), custom_call_target="tpu_custom_call" | custom-call | flops 1048576 | bytes 1048576 | tf_op jit(solution)/shard_map/pallas_call | solution.py:306
  (3 shorter events, 0.1 us)
Async XLA Ops:
  2.9 11.7 %copy-start.4 = (f32[1,3,4096]{2,0,1:T(1,128)S(1)}, f32[1,3,4096]{2,0,1:T(1,128)}, u32[]{:S(2)}) copy-start(f32[1,3,4096]{2,0,1:T(1,128)} %param.15) | copy-start | bytes 147460
  2.9 14.1 %copy-start = (f32[1,128,3,128]{3,1,2,0:T(8,128)S(1)}, f32[1,128,3,128]{3,1,2,0:T(8,128)}, u32[]{:S(2)}) copy-start(f32[1,128,3,128]{3,1,2,0:T(8,128)} %param.26) | copy-start | bytes 589828
  2.9 14.1 %copy-start.3 = (f32[1,128,128]{2,1,0:T(8,128)S(1)}, f32[1,128,128]{2,1,0:T(8,128)}, u32[]{:S(2)}) copy-start(f32[1,128,128]{2,1,0:T(8,128)} %param.25) | copy-start | bytes 196612
  2.9 14.1 %copy-start.5 = (bf16[128,128]{1,0:T(8,128)(2,1)S(1)}, bf16[128,128]{1,0:T(8,128)(2,1)}, u32[]{:S(2)}) copy-start(bf16[128,128]{1,0:T(8,128)(2,1)} %coupling.1) | copy-start | bytes 98308
  2.9 25.0 %all-to-all-start = ((bf16[64,8,512]{2,1,0:T(8,128)(2,1)}), bf16[64,8,512]{2,1,0:T(8,128)(2,1)S(1)}, u32[]{:S(2)}, u32[]{:S(2)}) async-start(bf16[64,8,512]{2,1,0:T(8,128)(2,1)} %bitcast.51), calls=%async_computation | async-start | bytes 1048576 | tf_op jit(solution)/shard_map/all_to_all | solution.py:234
  14.6 2.4 %copy-start.2 = (bf16[1,128,3,128]{3,1,2,0:T(8,128)(2,1)S(1)}, bf16[1,128,3,128]{3,1,2,0:T(8,128)(2,1)}, u32[]{:S(2)}) copy-start(bf16[1,128,3,128]{3,1,2,0:T(8,128)(2,1)} %param.27) | copy-start | bytes 294916
  14.7 5.1 %collective-permute-start.1 = (f32[3,16,128]{2,1,0:T(8,128)S(1)}, f32[3,16,128]{2,1,0:T(8,128)S(1)}, u32[]{:S(2)}, u32[]{:S(2)}) collective-permute-start(f32[3,16,128]{2,1,0:T(8,128)S(1)} %get-tuple-element.43), channel_id=1, source_target_pairs={{0,1},{2,3},{4,5},{6,7},{8,9},{10,11},{12,13},{14,15},{16,17},{18,... | collective-permute-start | bytes 73736 | tf_op jit(solution)/shard_map/ppermute | solution.py:226
  16.3 3.5 %collective-permute-start = (f32[3,16,128]{2,1,0:T(8,128)S(1)}, f32[3,16,128]{2,1,0:T(8,128)S(1)}, u32[]{:S(2)}, u32[]{:S(2)}) collective-permute-start(f32[3,16,128]{2,1,0:T(8,128)S(1)} %get-tuple-element.44), channel_id=1, source_target_pairs={{1,2},{3,4},{5,6},{7,8},{9,10},{11,12},{13,14},{15,16},{17,18},{19... | collective-permute-start | bytes 73736 | tf_op jit(solution)/shard_map/ppermute | solution.py:226
  17.0 0.7 %copy-start.6 = (f32[128]{0:T(128)S(1)}, f32[128]{0:T(128)}, u32[]{:S(2)}) copy-start(f32[128]{0:T(128)} %param.29) | copy-start | bytes 1540
  17.6 2.2 %copy-start.7 = (s32[1,8,4096]{2,1,0:T(8,128)S(1)}, s32[1,8,4096]{2,1,0:T(8,128)}, u32[]{:S(2)}) copy-start(s32[1,8,4096]{2,1,0:T(8,128)} %param.16) | copy-start | bytes 393220
  17.6 2.2 %copy-start.8 = (f32[1,6,4096]{2,0,1:T(1,128)S(1)}, f32[1,6,4096]{2,0,1:T(1,128)}, u32[]{:S(2)}) copy-start(f32[1,6,4096]{2,0,1:T(1,128)} %param.17) | copy-start | bytes 294916
  17.6 2.2 %copy-start.9 = (f32[1,3,4096]{2,0,1:T(1,128)S(1)}, f32[1,3,4096]{2,0,1:T(1,128)}, u32[]{:S(2)}) copy-start(f32[1,3,4096]{2,0,1:T(1,128)} %param.20) | copy-start | bytes 147460
  17.6 2.2 %copy-start.10 = (f32[1,4096]{1,0:T(1,128)S(1)}, f32[1,4096]{1,0:T(1,128)}, u32[]{:S(2)}) copy-start(f32[1,4096]{1,0:T(1,128)} %param.18) | copy-start | bytes 49156
  17.6 2.2 %copy-start.11 = (f32[1,4096]{1,0:T(1,128)S(1)}, f32[1,4096]{1,0:T(1,128)}, u32[]{:S(2)}) copy-start(f32[1,4096]{1,0:T(1,128)} %param.19) | copy-start | bytes 49156
  17.7 10.2 %collective-permute-start.2 = (f32[4,128,128]{2,1,0:T(8,128)S(1)}, f32[4,128,128]{2,1,0:T(8,128)S(1)}, u32[]{:S(2)}, u32[]{:S(2)}) collective-permute-start(f32[4,128,128]{2,1,0:T(8,128)S(1)} %get-tuple-element.24), channel_id=1, source_target_pairs={{0,64},{64,0},{1,65},{65,1},{2,66},{66,2},{3,67},{67,3},{4,68},{68... | collective-permute-start | bytes 786440 | tf_op jit(solution)/shard_map/ppermute | solution.py:230
  29.9 24.7 %copy-start.1 = (bf16[512,128]{1,0:T(8,128)(2,1)S(1)}, bf16[512,128]{1,0:T(8,128)(2,1)}, u32[]{:S(2)}) copy-start(bf16[512,128]{1,0:T(8,128)(2,1)} %get-tuple-element.28.place) | copy-start | bytes 393220
  29.9 24.6 %all-to-all-start.1 = ((bf16[64,8,384]{2,1,0:T(8,128)(2,1)}), bf16[64,8,384]{2,1,0:T(8,128)(2,1)S(1)}, u32[]{:S(2)}, u32[]{:S(2)}) async-start(bf16[64,8,384]{2,1,0:T(8,128)(2,1)} %bitcast.22), calls=%async_computation.1 | async-start | bytes 786432 | tf_op jit(solution)/shard_map/all_to_all | solution.py:234
  43.3 12.6 %collective-permute-start.5 = (f32[3,128,128]{2,1,0:T(8,128)S(1)}, f32[3,128,128]{2,1,0:T(8,128)S(1)}, u32[]{:S(2)}, u32[]{:S(2)}) collective-permute-start(f32[3,128,128]{2,1,0:T(8,128)S(1)} %get-tuple-element.33), channel_id=1, source_target_pairs={{0,64},{64,0},{1,65},{65,1},{2,66},{66,2},{3,67},{67,3},{4,68},{68... | collective-permute-start | bytes 589832 | tf_op jit(solution)/shard_map/ppermute | solution.py:230
  43.4 12.5 %collective-permute-start.3 = (f32[3,16,128]{2,1,0:T(8,128)S(1)}, f32[3,16,128]{2,1,0:T(8,128)S(1)}, u32[]{:S(2)}, u32[]{:S(2)}) collective-permute-start(f32[3,16,128]{2,1,0:T(8,128)S(1)} %get-tuple-element.31), channel_id=1, source_target_pairs={{1,2},{3,4},{5,6},{7,8},{9,10},{11,12},{13,14},{15,16},{17,18},{19... | collective-permute-start | bytes 73736 | tf_op jit(solution)/shard_map/ppermute | solution.py:226
  44.1 11.8 %collective-permute-start.4 = (f32[3,16,128]{2,1,0:T(8,128)S(1)}, f32[3,16,128]{2,1,0:T(8,128)S(1)}, u32[]{:S(2)}, u32[]{:S(2)}) collective-permute-start(f32[3,16,128]{2,1,0:T(8,128)S(1)} %get-tuple-element.32), channel_id=1, source_target_pairs={{0,1},{2,3},{4,5},{6,7},{8,9},{10,11},{12,13},{14,15},{16,17},{18,... | collective-permute-start | bytes 73736 | tf_op jit(solution)/shard_map/ppermute | solution.py:226

commit v5 on v4

--- a/solution.py
+++ b/solution.py
@@ -8,7 +8,6 @@
 
 
 LANES = 128
-WINDOW = 48
 HALO = 16
 BLOCKS = 32
 SLOTS = 8
@@ -29,41 +28,80 @@
     return lax.broadcasted_iota(jnp.int32, shape, dim).astype(dtype)
 
 
-def element_kernel(parity, far, near, own, links, strain, edge_ref, yield_ref, ext, far_out, near_out, own_out,
-                   disp, lo_s, hi_s, force_s, acc):
+def own_rows(m):
+    return range(max(0, HALO - 8 * m), min(33, HALO + BLOCKS - 7 - 8 * m))
+
+
+def reach_of(links, m, a):
+    return links[pl.ds(64 * m + a, 8, stride=8), :] + iota((8, LANES), 1)
+
+
+def gather_rows(disp, links, m, a, hs, base, got):
+    reach = reach_of(links, m, a)
+    hi, lo = reach >> 7, reach & 127
+    chains = [list(got), [jnp.zeros((8, LANES), F32)] * 3]
+    for n, h in enumerate(hs):
+        here = hi == h
+        chain = chains[n & 1]
+        for i in range(3):
+            rows = disp[i, 8 * m + h - base : 8 * m + h - base + 8, :]
+            chain[i] = jnp.where(here, jnp.take_along_axis(rows, lo, axis=1), chain[i])
+    return [x + y for x, y in zip(*chains)]
+
+
+GROUP = 4
+
+
+def gather_kernel(own, links, nodal):
+    for m in range(BLOCKS // 8):
+
+        @pl.loop(0, 8 // GROUP)
+        def _(step):
+            for c in range(GROUP):
+                a = step * GROUP + c
+                got = gather_rows(own, links, m, a, own_rows(m), HALO, [jnp.zeros((8, LANES), F32)] * 3)
+                at = pl.multiple_of(a * BLOCKS + 8 * m, 8)
+                for i in range(3):
+                    nodal[i, pl.ds(at, 8), :] = got[i]
+
+
+def element_kernel(parity, far, near, own, links, part, strain, edge_ref, yield_ref, ext, far_out, near_out, own_out,
+                   disp, lo_s, hi_s, nodal_s, acc):
     odd = parity[0:1, :] == 1
     disp[:, 0:HALO, :] = jnp.where(odd, near[...], far[...])
     disp[:, HALO : HALO + BLOCKS, :] = own[...]
     disp[:, HALO + BLOCKS : 2 * HALO + BLOCKS, :] = jnp.where(odd, far[...], near[...])
     acc[...] = jnp.zeros_like(acc)
-    lane = iota((8, LANES), 1)
-    block = iota((8, LANES), 0)
+    block = iota((8, LANES), 0) * LANES
     for m in range(BLOCKS // 8):
-        nodal = []
-        for a in range(8):
-            reach = links[pl.ds(64 * m + a, 8, stride=8), :] + lane
-            hi = reach >> 7
-            lo = reach & 127
-            lo_s[a * BLOCKS + 8 * m : a * BLOCKS + 8 * m + 8, :] = lo.astype(F32)
-            hi_s[a * BLOCKS + 8 * m : a * BLOCKS + 8 * m + 8, :] = (hi + block).astype(F32)
-            got = [jnp.zeros((8, LANES), F32)] * 3
-            for h in range(33):
-                here = hi == h
+
+        @pl.loop(0, 8 // GROUP)
+        def _(step):
+            for c in range(GROUP):
+                a = step * GROUP + c
+                at = pl.ds(pl.multiple_of(a * BLOCKS + 8 * m, 8), 8)
+                rest = [h for h in range(33) if h not in own_rows(m)]
+                got = gather_rows(disp, links, m, a, rest, 0, [part[i, at, :] for i in range(3)])
                 for i in range(3):
-                    rows = disp[i, 8 * m + h : 8 * m + h + 8, :]
-                    got[i] = jnp.where(here, jnp.take_along_axis(rows, lo, axis=1), got[i])
-            nodal.append(got)
-        edge = edge_ref[8 * m : 8 * m + 8, :]
+                    nodal_s[i, at, :] = got[i]
+                reach = reach_of(links, m, a) + block
+                hi_s[at, :] = (reach >> 6).astype(F32)
+                lo_s[at, :] = (reach & 63).astype(F32)
+
+    @pl.loop(0, BLOCKS // 8)
+    def _(m):
+        at = lambda a: pl.ds(pl.multiple_of(a * BLOCKS + 8 * m, 8), 8)
+        rows = at(0)
+        edge = edge_ref[rows, :]
         scale = 0.25 / edge
         grad = [[None] * 3 for _ in range(3)]
         for i in range(3):
-            u = [nodal[a][i] for a in range(8)]
+            u = [nodal_s[i, at(a), :] for a in range(8)]
             for j in range(3):
                 plus = [u[a] for a in range(8) if a >> j & 1]
                 minus = [u[a] for a in range(8) if not a >> j & 1]
-                total = sum(p - q for p, q in zip(plus, minus))
-                grad[i][j] = total * scale
-        old = [strain[c, 8 * m : 8 * m + 8, :] for c in range(6)]
+                grad[i][j] = sum(p - q for p, q in zip(plus, minus)) * scale
+        old = [strain[c, rows, :] for c in range(6)]
         exx = grad[0][0] - old[0]
         eyy = grad[1][1] - old[1]
         ezz = grad[2][2] - old[2]
@@ -77,7 +115,7 @@
         mean = (sxx + syy + szz) / 3.0
         dxx, dyy, dzz = sxx - mean, syy - mean, szz - mean
         size = jnp.sqrt(dxx * dxx + dyy * dyy + dzz * dzz + 2.0 * (exy * exy + eyz * eyz + ezx * ezx))
-        radius = np.float32(np.sqrt(2.0 / 3.0)) * yield_ref[8 * m : 8 * m + 8, :]
+        radius = np.float32(np.sqrt(2.0 / 3.0)) * yield_ref[rows, :]
         factor = radius / jnp.maximum(size, radius)
         area = 0.25 * edge * edge
         xy, yz, zx = area * factor * exy, area * factor * eyz, area * factor * ezx
@@ -88,10 +126,10 @@
             four = [tx + ty, ty - tx, tx - ty, -tx - ty]
             for a in range(8):
                 pick = four[(0 if a & 1 else 1) if a & 2 else (2 if a & 1 else 3)]
-                f = pick + tz if a & 4 else pick - tz
-                force_s[i, a * BLOCKS + 8 * m : a * BLOCKS + 8 * m + 8, :] = f
+                nodal_s[i, at(a), :] = pick + tz if a & 4 else pick - tz
+
     row = iota((16, LANES), 0, F32)
-    rows = [(row + 16.0 * t).astype(BF16) for t in range(8)]
+    tiles = [(row + 16.0 * t).astype(BF16) for t in range(5)]
     zero = jnp.zeros((16, LANES), BF16)
     one = jnp.ones((16, LANES), BF16)
 
@@ -99,27 +137,27 @@
         return jnp.broadcast_to(ref[at], (16, LANES)).astype(BF16)
 
     for m in range(BLOCKS // 8):
-        sums = jnp.zeros((3 * WINDOW, LANES), F32)
+        sums = jnp.zeros((80, 3 * 64), F32)
         for s in range(8):
             left, right = [], []
             for a in range(8):
                 at = slice(a * BLOCKS + 8 * m + s, a * BLOCKS + 8 * m + s + 1)
                 hi = wide(hi_s, at, slice(None))
                 lo = wide(lo_s, at, slice(None))
-                here = [hi == rows[t] for t in range(WINDOW // 16)]
-                parts = []
-                for i in range(3):
-                    f = wide(force_s, i, at, slice(None))
-                    parts += [jnp.where(h, f, zero) for h in here]
-                left.append(jnp.concatenate(parts, axis=0))
-                right.append(jnp.concatenate([jnp.where(lo == r, one, zero) for r in rows], axis=0))
+                left.append(jnp.concatenate([jnp.where(hi == t, one, zero) for t in tiles], axis=0))
+                here = [lo == t for t in tiles[:4]]
+                force = [wide(nodal_s, i, at, slice(None)) for i in range(3)]
+                right.append(jnp.concatenate([jnp.where(h, f, zero) for f in force for h in here], axis=0))
             sums = sums + dot(jnp.concatenate(left, axis=1), jnp.concatenate(right, axis=1), NT)
-        for i in range(3):
-            acc[i, 8 * m : 8 * m + WINDOW, :] += sums[i * WINDOW : (i + 1) * WINDOW]
-    low, high = acc[:, 0:HALO, :], acc[:, HALO + BLOCKS : 2 * HALO + BLOCKS, :]
-    far_out[...] = jnp.where(odd, high, low)
-    near_out[...] = jnp.where(odd, low, high)
-    own_out[...] = acc[:, HALO : HALO + BLOCKS, :] - ext[...]
+        acc[0, 16 * m : 16 * m + 80, :] += sums[:, :LANES]
+        acc[1, 16 * m : 16 * m + 80, :64] += sums[:, LANES:]
+    for i in range(3):
+        pair = [acc[i // 2, pl.ds(p, 2 * HALO + BLOCKS, stride=2), :] for p in range(2)]
+        nodes = jnp.concatenate([x[:, 64 * (i % 2) : 64 * (i % 2) + 64] for x in pair], axis=1)
+        low, high = nodes[0:HALO], nodes[HALO + BLOCKS :]
+        far_out[i] = jnp.where(odd, high, low)
+        near_out[i] = jnp.where(odd, low, high)
+        own_out[i] = nodes[HALO : HALO + BLOCKS] - ext[i]
 
 
 def finish_kernel(parity, own, far, near, force, out, force_out):
@@ -272,17 +310,18 @@
     )(master_gap[0], seg_major(master_normal), seg_major(master_disp), coupling, quad_weight.reshape(1, LANES))
     rows = swapped(rows)
     links = jnp.transpose(connectivity[0].reshape(8, BLOCKS, LANES), (1, 0, 2)).reshape(8 * BLOCKS, LANES)
+    part = call(gather_kernel, 2, shape(3, 8 * BLOCKS, LANES), 1 << 30)(own, links)
     far_force, near_force, own_force = call(
         element_kernel,
-        9,
+        10,
         (shape(3, HALO, LANES), shape(3, HALO, LANES), shape(3, BLOCKS, LANES)),
         1 << 32,
         (
-            pltpu.VMEM((3, 2 * HALO + BLOCKS + 16, LANES), F32),
+            pltpu.VMEM((3, 2 * HALO + BLOCKS + 8, LANES), F32),
             pltpu.VMEM((8 * BLOCKS, LANES), F32),
             pltpu.VMEM((8 * BLOCKS, LANES), F32),
             pltpu.VMEM((3, 8 * BLOCKS, LANES), F32),
-            pltpu.VMEM((3, 2 * HALO + BLOCKS + 16, LANES), F32),
+            pltpu.VMEM((2, 4 * HALO + 2 * BLOCKS + 16, LANES), F32),
         ),
     )(
         parity,
@@ -290,6 +329,7 @@
         near,
         own,
         links,
+        part,
         plastic_strain[0].reshape(6, BLOCKS, LANES),
         element_size.reshape(BLOCKS, LANES),
         yield_stress.reshape(BLOCKS, LANES),

time: 57 us -> 57.5 us (level)
  waiting for transfers between devices: 10.4 us -> 6.18 us
  Pallas kernels: 12.2 us -> 15.6 us
  local copies, waits for them, and re-layouts: 0.66 us -> 1.42 us
    pallas_call x1 -> x2, Pallas kernels: 5.81 us -> 9.2 us  [the longest x1 6.37 us: local(): call(element_kernel, 10, (shape(3, HALO, LANES), shape(3, HALO, LANES), s...]
    all_to_all x2, waiting for transfers between devices: 8.35 us -> 6.17 us  [exchanged(): return lax.all_to_all(block, 'dom', split_axis=0, concat_axis=0, tiled=True)]
    ppermute x4, waiting for transfers between devices: 1.99 us -> 0.01 us  [paired(): return lax.ppermute(block, 'dom', route + [(j, i) for i, j in route])]
    unnamed x24, local copies, waits for them, and re-layouts: 0.66 us -> 1.42 us
  transfers between devices with their start and end apart: 8 -> 8, of which waited for: 3 -> 2; matrix products, arithmetic and copies ran while one was open for 0% -> 0% of each run, Pallas kernels for 13% -> 18%
where the time goes in v5:
time: 57.5 us; the launch traced here: 57.2 us
  starting transfers between devices  33.1 us (58%)
  Pallas kernels  15.6 us (27%)
  waiting for transfers between devices  6.18 us (11%)
  local copies, waits for them, and re-layouts  1.42 us (2%)
  between operations  0.85 us (1%)
    all_to_all x2, starting transfers between devices, exchanged(): return lax.all_to_all(block, 'dom', split_axis=0, concat_axis=0, tiled=True)  25.6 us
    ppermute x4, starting transfers between devices, paired(): return lax.ppermute(block, 'dom', route + [(j, i) for i, j in route])  7.32 us
    pallas_call x1, Pallas kernels, local(): call(element_kernel, 10, (shape(3, HALO, LANES), shape(3, HALO, LANES), s...  6.37 us
    all_to_all x2, waiting for transfers between devices, exchanged(): return lax.all_to_all(block, 'dom', split_axis=0, concat_axis=0, tiled=True)  6.17 us
    pallas_call x1, Pallas kernels, local(): call(gather_kernel, 2, shape(3, 8 * BLOCKS, LANES), 1 << 30)(own, links)  2.82 us
    pallas_call x1, Pallas kernels, local(): call(pack_kernel, -4, (shape(PEERS * SLOTS, 4 * LANES, dtype=BF16), shape...  2.27 us
    pallas_call x1, Pallas kernels, local(): call(master_kernel, 4, (shape(PEERS * SLOTS, 3 * LANES, dtype=BF16), shap...  2 us
    unnamed x24, local copies, waits for them, and re-layouts  1.42 us
  transfers between devices with their start and end apart: 8, of which 2 were waited for; matrix products, arithmetic and copies ran while one was open for 0% of the time, Pallas kernels for 18%

profile of v5, /device:TPU:0, one launch (start us, length us, event | category | flops | bytes accessed | tf_op | source)
XLA Modules:
  0.0 57.2 jit_solution(12970604731514226745)
XLA Ops:
  0.6 2.3 %shard_map.166 = (bf16[512,512]{1,0:T(8,128)(2,1)}, bf16[512,128]{1,0:T(8,128)(2,1)}) custom-call(s32[2,128]{1,0:T(2,128)} %bitcast.58, s32[2,128]{1,0:T(2,128)} %bitcast.59, s32[1,128]{1,0:T(1,128)} %active.1, bf16[3,128,128]{2,1,0:T(8,128)(2,1)} %bitcast.56), custom_call_target="tpu_custom_call" | custom-call | flops 134217728 | bytes 1048576 | tf_op jit(solution)/shard_map/pallas_call | solution.py:293
  2.9 0.0 copy-start.4
  2.9 0.0 copy-start
  2.9 0.0 copy-start.3
  2.9 0.0 copy-start.5
  2.9 11.7 %all-to-all-start = ((bf16[64,8,512]{2,1,0:T(8,128)(2,1)}), bf16[64,8,512]{2,1,0:T(8,128)(2,1)S(1)}, u32[]{:S(2)}, u32[]{:S(2)}) async-start(bf16[64,8,512]{2,1,0:T(8,128)(2,1)} %bitcast.53), calls=%async_computation | async-start | bytes 1048576 | tf_op jit(solution)/shard_map/all_to_all | solution.py:272
  14.6 0.0 copy-start.2
  14.6 0.0 copy-done.4
  14.7 1.6 %collective-permute-start.1 = (f32[3,16,128]{2,1,0:T(8,128)S(1)}, f32[3,16,128]{2,1,0:T(8,128)S(1)}, u32[]{:S(2)}, u32[]{:S(2)}) collective-permute-start(f32[3,16,128]{2,1,0:T(8,128)S(1)} %get-tuple-element.43), channel_id=1, source_target_pairs={{0,1},{2,3},{4,5},{6,7},{8,9},{10,11},{12,13},{14,15},{16,17},{18,... | collective-permute-start | bytes 73736 | tf_op jit(solution)/shard_map/ppermute | solution.py:264
  16.3 0.7 %collective-permute-start = (f32[3,16,128]{2,1,0:T(8,128)S(1)}, f32[3,16,128]{2,1,0:T(8,128)S(1)}, u32[]{:S(2)}, u32[]{:S(2)}) collective-permute-start(f32[3,16,128]{2,1,0:T(8,128)S(1)} %get-tuple-element.44), channel_id=1, source_target_pairs={{1,2},{3,4},{5,6},{7,8},{9,10},{11,12},{13,14},{15,16},{17,18},{19... | collective-permute-start | bytes 73736 | tf_op jit(solution)/shard_map/ppermute | solution.py:264
  17.0 0.0 copy-start.6
  17.0 0.0 copy-done
  17.0 0.0 copy-done.3
  17.0 0.0 copy-done.5
  17.0 0.0 copy-done.2
  17.0 0.6 %copy-done.6 = f32[128]{0:T(128)S(1)} copy-done((f32[128]{0:T(128)S(1)}, f32[128]{0:T(128)}, u32[]{:S(2)}) %copy-start.6) | copy-done | bytes 536
  17.6 0.0 copy-start.7
  17.7 0.1 collective-permute-start.2
  17.8 0.8 %copy-done.7 = s32[1,8,4096]{2,1,0:T(8,128)S(1)} copy-done((s32[1,8,4096]{2,1,0:T(8,128)S(1)}, s32[1,8,4096]{2,1,0:T(8,128)}, u32[]{:S(2)}) %copy-start.7) | copy-done | bytes 131096
  18.5 0.0 copy-start.8
  18.5 0.0 copy-start.9
  18.5 0.0 copy-start.10
  18.5 0.0 copy-start.11
  18.5 2.8 %shard_map.167.part = f32[3,256,128]{2,1,0:T(8,128)S(1)} custom-call(f32[3,32,128]{2,1,0:T(8,128)S(1)} %bitcast.44, s32[256,128]{1,0:T(8,128)S(1)} %bitcast.47), custom_call_target="tpu_custom_call" | custom-call | flops 1073741824 | bytes 1048576 | tf_op jit(solution)/shard_map/pallas_call | solution.py:313
  21.4 0.0 collective-permute-done.1.near
  21.4 0.0 collective-permute-done.far
  21.4 0.0 copy-done.8
  21.4 0.0 copy-done.9
  21.4 0.0 copy-done.10
  21.4 0.0 copy-done.11
  21.4 6.4 %shard_map.168 = (f32[3,16,128]{2,1,0:T(8,128)S(1)}, f32[3,16,128]{2,1,0:T(8,128)S(1)}, f32[3,32,128]{2,1,0:T(8,128)S(1)}) custom-call(s32[8,128]{1,0:T(8,128)S(1)} %broadcast_in_dim.9.parity, f32[3,16,128]{2,1,0:T(8,128)S(1)} %collective-permute-done.far, f32[3,16,128]{2,1,0:T(8,128)S(1)} %collective-permute-done.1.near, f32[3,32,128]{2,1,0:T(8,128)S(1)} %bitcast.45, ...), custom_call_target="tpu_custom_call" | custom-call | flops 4294967296 | bytes 1048576 | tf_op jit(solution)/shard_map/pallas_call | solution.py:314
  27.8 0.1 all-to-all-done
  27.9 0.0 collective-permute-done.2.rows
  27.9 2.0 %shard_map.170 = (bf16[512,384]{1,0:T(8,128)(2,1)}, f32[3,128,128]{2,1,0:T(8,128)S(1)}) custom-call(bf16[512,512]{1,0:T(8,128)(2,1)S(1)} %bitcast.39, f32[4,128,128]{2,1,0:T(8,128)S(1)} %collective-permute-done.2.rows, bf16[128,128]{1,0:T(8,128)(2,1)S(1)} %get-tuple-element.25.mortar_ref, f32[8,128]{1,0:T(8,128)S(1)} %get-tuple-element.26.weight), custom_call_target="tpu_custom_call" | custom-call | flops 268435456 | bytes 1048576 | tf_op jit(solution)/shard_map/pallas_call | solution.py:340
  29.9 0.0 copy-start.1
  29.9 14.0 %all-to-all-start.1 = ((bf16[64,8,384]{2,1,0:T(8,128)(2,1)}), bf16[64,8,384]{2,1,0:T(8,128)(2,1)S(1)}, u32[]{:S(2)}, u32[]{:S(2)}) async-start(bf16[64,8,384]{2,1,0:T(8,128)(2,1)} %bitcast.24), calls=%async_computation.1 | async-start | bytes 786432 | tf_op jit(solution)/shard_map/all_to_all | solution.py:272
  43.9 0.1 collective-permute-start.5
  44.0 0.7 %collective-permute-start.3 = (f32[3,16,128]{2,1,0:T(8,128)S(1)}, f32[3,16,128]{2,1,0:T(8,128)S(1)}, u32[]{:S(2)}, u32[]{:S(2)}) collective-permute-start(f32[3,16,128]{2,1,0:T(8,128)S(1)} %get-tuple-element.31), channel_id=1, source_target_pairs={{1,2},{3,4},{5,6},{7,8},{9,10},{11,12},{13,14},{15,16},{17,18},{19... | collective-permute-start | bytes 73736 | tf_op jit(solution)/shard_map/ppermute | solution.py:264
  44.6 4.4 %collective-permute-start.4 = (f32[3,16,128]{2,1,0:T(8,128)S(1)}, f32[3,16,128]{2,1,0:T(8,128)S(1)}, u32[]{:S(2)}, u32[]{:S(2)}) collective-permute-start(f32[3,16,128]{2,1,0:T(8,128)S(1)} %get-tuple-element.32), channel_id=1, source_target_pairs={{0,1},{2,3},{4,5},{6,7},{8,9},{10,11},{12,13},{14,15},{16,17},{18,... | collective-permute-start | bytes 73736 | tf_op jit(solution)/shard_map/ppermute | solution.py:264
  49.0 6.1 %all-to-all-done.1 = bf16[64,8,384]{2,1,0:T(8,128)(2,1)S(1)} async-done(((bf16[64,8,384]{2,1,0:T(8,128)(2,1)}), bf16[64,8,384]{2,1,0:T(8,128)(2,1)S(1)}, u32[]{:S(2)}, u32[]{:S(2)}) %all-to-all-start.1) | async-done | bytes 393248 | tf_op jit(solution)/shard_map/all_to_all | solution.py:272
  55.1 0.0 copy-done.1
  55.1 1.3 %shard_map.171 = f32[3,128,128]{2,1,0:T(8,128)} custom-call(bf16[512,384]{1,0:T(8,128)(2,1)S(1)} %bitcast.38, bf16[512,128]{1,0:T(8,128)(2,1)S(1)} %copy-done.1, bf16[128,128]{1,0:T(8,128)(2,1)S(1)} %get-tuple-element.25.mortar_ref), custom_call_target="tpu_custom_call" | custom-call | flops 134217728 | bytes 1048576 | tf_op jit(solution)/shard_map/pallas_call | solution.py:344
  56.4 0.0 collective-permute-done.3.far
  56.4 0.0 collective-permute-done.4.near
  56.4 0.0 collective-permute-done.5.force
  56.5 0.7 %shard_map.172 = (f32[3,32,128]{2,1,0:T(8,128)}, f32[3,128,128]{2,1,0:T(8,128)}) custom-call(s32[8,128]{1,0:T(8,128)S(1)} %broadcast_in_dim.9.parity, f32[3,32,128]{2,1,0:T(8,128)S(1)} %get-tuple-element.30.own, f32[3,16,128]{2,1,0:T(8,128)S(1)} %collective-permute-done.3.far, f32[3,16,128]{2,1,0:T(8,128)S(1)} %collective-permute-done.4.near, ...), custom_call_target="tpu_custom_call" | custom-call | flops 1048576 | bytes 1048576 | tf_op jit(solution)/shard_map/pallas_call | solution.py:346
  (3 shorter events, 0.1 us)
Async XLA Ops:
  2.9 11.7 %copy-start.4 = (f32[1,3,4096]{2,0,1:T(1,128)S(1)}, f32[1,3,4096]{2,0,1:T(1,128)}, u32[]{:S(2)}) copy-start(f32[1,3,4096]{2,0,1:T(1,128)} %param.15) | copy-start | bytes 147460
  2.9 14.1 %copy-start = (f32[1,128,3,128]{3,1,2,0:T(8,128)S(1)}, f32[1,128,3,128]{3,1,2,0:T(8,128)}, u32[]{:S(2)}) copy-start(f32[1,128,3,128]{3,1,2,0:T(8,128)} %param.26) | copy-start | bytes 589828
  2.9 14.1 %copy-start.3 = (f32[1,128,128]{2,1,0:T(8,128)S(1)}, f32[1,128,128]{2,1,0:T(8,128)}, u32[]{:S(2)}) copy-start(f32[1,128,128]{2,1,0:T(8,128)} %param.25) | copy-start | bytes 196612
  2.9 14.1 %copy-start.5 = (bf16[128,128]{1,0:T(8,128)(2,1)S(1)}, bf16[128,128]{1,0:T(8,128)(2,1)}, u32[]{:S(2)}) copy-start(bf16[128,128]{1,0:T(8,128)(2,1)} %coupling.1) | copy-start | bytes 98308
  2.9 25.0 %all-to-all-start = ((bf16[64,8,512]{2,1,0:T(8,128)(2,1)}), bf16[64,8,512]{2,1,0:T(8,128)(2,1)S(1)}, u32[]{:S(2)}, u32[]{:S(2)}) async-start(bf16[64,8,512]{2,1,0:T(8,128)(2,1)} %bitcast.53), calls=%async_computation | async-start | bytes 1048576 | tf_op jit(solution)/shard_map/all_to_all | solution.py:272
  14.6 2.4 %copy-start.2 = (bf16[1,128,3,128]{3,1,2,0:T(8,128)(2,1)S(1)}, bf16[1,128,3,128]{3,1,2,0:T(8,128)(2,1)}, u32[]{:S(2)}) copy-start(bf16[1,128,3,128]{3,1,2,0:T(8,128)(2,1)} %param.27) | copy-start | bytes 294916
  14.7 6.7 %collective-permute-start.1 = (f32[3,16,128]{2,1,0:T(8,128)S(1)}, f32[3,16,128]{2,1,0:T(8,128)S(1)}, u32[]{:S(2)}, u32[]{:S(2)}) collective-permute-start(f32[3,16,128]{2,1,0:T(8,128)S(1)} %get-tuple-element.43), channel_id=1, source_target_pairs={{0,1},{2,3},{4,5},{6,7},{8,9},{10,11},{12,13},{14,15},{16,17},{18,... | collective-permute-start | bytes 73736 | tf_op jit(solution)/shard_map/ppermute | solution.py:264
  16.3 5.1 %collective-permute-start = (f32[3,16,128]{2,1,0:T(8,128)S(1)}, f32[3,16,128]{2,1,0:T(8,128)S(1)}, u32[]{:S(2)}, u32[]{:S(2)}) collective-permute-start(f32[3,16,128]{2,1,0:T(8,128)S(1)} %get-tuple-element.44), channel_id=1, source_target_pairs={{1,2},{3,4},{5,6},{7,8},{9,10},{11,12},{13,14},{15,16},{17,18},{19... | collective-permute-start | bytes 73736 | tf_op jit(solution)/shard_map/ppermute | solution.py:264
  17.0 0.7 %copy-start.6 = (f32[128]{0:T(128)S(1)}, f32[128]{0:T(128)}, u32[]{:S(2)}) copy-start(f32[128]{0:T(128)} %param.29) | copy-start | bytes 1540
  17.6 0.9 %copy-start.7 = (s32[1,8,4096]{2,1,0:T(8,128)S(1)}, s32[1,8,4096]{2,1,0:T(8,128)}, u32[]{:S(2)}) copy-start(s32[1,8,4096]{2,1,0:T(8,128)} %param.16) | copy-start | bytes 393220
  17.7 10.2 %collective-permute-start.2 = (f32[4,128,128]{2,1,0:T(8,128)S(1)}, f32[4,128,128]{2,1,0:T(8,128)S(1)}, u32[]{:S(2)}, u32[]{:S(2)}) collective-permute-start(f32[4,128,128]{2,1,0:T(8,128)S(1)} %get-tuple-element.24), channel_id=1, source_target_pairs={{0,64},{64,0},{1,65},{65,1},{2,66},{66,2},{3,67},{67,3},{4,68},{68... | collective-permute-start | bytes 786440 | tf_op jit(solution)/shard_map/ppermute | solution.py:268
  18.5 2.9 %copy-start.8 = (f32[1,6,4096]{2,0,1:T(1,128)S(1)}, f32[1,6,4096]{2,0,1:T(1,128)}, u32[]{:S(2)}) copy-start(f32[1,6,4096]{2,0,1:T(1,128)} %param.17) | copy-start | bytes 294916
  18.5 2.9 %copy-start.9 = (f32[1,3,4096]{2,0,1:T(1,128)S(1)}, f32[1,3,4096]{2,0,1:T(1,128)}, u32[]{:S(2)}) copy-start(f32[1,3,4096]{2,0,1:T(1,128)} %param.20) | copy-start | bytes 147460
  18.5 2.9 %copy-start.10 = (f32[1,4096]{1,0:T(1,128)S(1)}, f32[1,4096]{1,0:T(1,128)}, u32[]{:S(2)}) copy-start(f32[1,4096]{1,0:T(1,128)} %param.18) | copy-start | bytes 49156
  18.5 2.9 %copy-start.11 = (f32[1,4096]{1,0:T(1,128)S(1)}, f32[1,4096]{1,0:T(1,128)}, u32[]{:S(2)}) copy-start(f32[1,4096]{1,0:T(1,128)} %param.19) | copy-start | bytes 49156
  29.9 25.2 %copy-start.1 = (bf16[512,128]{1,0:T(8,128)(2,1)S(1)}, bf16[512,128]{1,0:T(8,128)(2,1)}, u32[]{:S(2)}) copy-start(bf16[512,128]{1,0:T(8,128)(2,1)} %get-tuple-element.28.place) | copy-start | bytes 393220
  29.9 25.2 %all-to-all-start.1 = ((bf16[64,8,384]{2,1,0:T(8,128)(2,1)}), bf16[64,8,384]{2,1,0:T(8,128)(2,1)S(1)}, u32[]{:S(2)}, u32[]{:S(2)}) async-start(bf16[64,8,384]{2,1,0:T(8,128)(2,1)} %bitcast.24), calls=%async_computation.1 | async-start | bytes 786432 | tf_op jit(solution)/shard_map/all_to_all | solution.py:272
  43.9 12.6 %collective-permute-start.5 = (f32[3,128,128]{2,1,0:T(8,128)S(1)}, f32[3,128,128]{2,1,0:T(8,128)S(1)}, u32[]{:S(2)}, u32[]{:S(2)}) collective-permute-start(f32[3,128,128]{2,1,0:T(8,128)S(1)} %get-tuple-element.33), channel_id=1, source_target_pairs={{0,64},{64,0},{1,65},{65,1},{2,66},{66,2},{3,67},{67,3},{4,68},{68... | collective-permute-start | bytes 589832 | tf_op jit(solution)/shard_map/ppermute | solution.py:268
  44.0 12.5 %collective-permute-start.3 = (f32[3,16,128]{2,1,0:T(8,128)S(1)}, f32[3,16,128]{2,1,0:T(8,128)S(1)}, u32[]{:S(2)}, u32[]{:S(2)}) collective-permute-start(f32[3,16,128]{2,1,0:T(8,128)S(1)} %get-tuple-element.31), channel_id=1, source_target_pairs={{1,2},{3,4},{5,6},{7,8},{9,10},{11,12},{13,14},{15,16},{17,18},{19... | collective-permute-start | bytes 73736 | tf_op jit(solution)/shard_map/ppermute | solution.py:264
  44.6 11.8 %collective-permute-start.4 = (f32[3,16,128]{2,1,0:T(8,128)S(1)}, f32[3,16,128]{2,1,0:T(8,128)S(1)}, u32[]{:S(2)}, u32[]{:S(2)}) collective-permute-start(f32[3,16,128]{2,1,0:T(8,128)S(1)} %get-tuple-element.32), channel_id=1, source_target_pairs={{0,1},{2,3},{4,5},{6,7},{8,9},{10,11},{12,13},{14,15},{16,17},{18,... | collective-permute-start | bytes 73736 | tf_op jit(solution)/shard_map/ppermute | solution.py:264

commit v6 on v4

--- a/solution.py
+++ b/solution.py
@@ -8,9 +8,9 @@
 
 
 LANES = 128
-WINDOW = 48
 HALO = 16
 BLOCKS = 32
+WINDOW = 48
 SLOTS = 8
 PEERS = 64
 SEG = 128
@@ -29,30 +29,68 @@
     return lax.broadcasted_iota(jnp.int32, shape, dim).astype(dtype)
 
 
-def element_kernel(parity, far, near, own, links, strain, edge_ref, yield_ref, ext, far_out, near_out, own_out,
-                   disp, lo_s, hi_s, force_s, acc):
+def own_rows(m):
+    return range(max(0, HALO - 8 * m), min(33, HALO + BLOCKS - 7 - 8 * m))
+
+
+def reach_of(links, m, a):
+    return links[pl.ds(64 * m + a, 8, stride=8), :] + iota((8, LANES), 1)
+
+
+def pack_pair(x, y, table):
+    most = jnp.max(jnp.maximum(jnp.abs(x), jnp.abs(y)), axis=0, keepdims=True)
+    most = jnp.maximum(jnp.max(most, axis=1, keepdims=True), 1e-30)
+    scale = 32767.0 / most
+
+    def whole(v):
+        v = v * scale
+        return (v + jnp.where(v < 0.0, -0.5, 0.5)).astype(jnp.int32)
+
+    table[0 : x.shape[0], :] = (whole(x) << 16) | (whole(y) & 65535)
+    return most / 32767.0
+
+
+def gather_rows(table, third, unit, links, m, a, hs, base):
+    reach = reach_of(links, m, a)
+    hi, lo = reach >> 7, reach & 127
+    pair, single = jnp.zeros((8, LANES), jnp.int32), jnp.zeros((8, LANES), F32)
+    for h in hs:
+        here = hi == h
+        rows = slice(8 * m + h - base, 8 * m + h - base + 8)
+        pair = jnp.where(here, jnp.take_along_axis(table[rows, :], lo, axis=1), pair)
+        single = jnp.where(here, jnp.take_along_axis(third[2, rows, :], lo, axis=1), single)
+    return [(pair >> 16).astype(F32) * unit, ((pair << 16) >> 16).astype(F32) * unit, single]
+
+
+def gather_kernel(own, links, nodal, table):
+    unit = pack_pair(own[0], own[1], table)
+    for m in range(BLOCKS // 8):
+        for a in range(8):
+            got = gather_rows(table, own, unit, links, m, a, own_rows(m), HALO)
+            at = a * BLOCKS + 8 * m
+            for i in range(3):
+                nodal[i, at : at + 8, :] = got[i]
+
+
+def element_kernel(parity, far, near, own, links, part, strain, edge_ref, yield_ref, ext, far_out, near_out, own_out,
+                   disp, table, lo_s, hi_s, force_s, acc):
     odd = parity[0:1, :] == 1
     disp[:, 0:HALO, :] = jnp.where(odd, near[...], far[...])
     disp[:, HALO : HALO + BLOCKS, :] = own[...]
     disp[:, HALO + BLOCKS : 2 * HALO + BLOCKS, :] = jnp.where(odd, far[...], near[...])
     acc[...] = jnp.zeros_like(acc)
-    lane = iota((8, LANES), 1)
-    block = iota((8, LANES), 0)
+    unit = pack_pair(disp[0, : 2 * HALO + BLOCKS], disp[1, : 2 * HALO + BLOCKS], table)
+    block = iota((8, LANES), 0) * LANES
     for m in range(BLOCKS // 8):
+        rest = [h for h in range(33) if h not in own_rows(m)]
         nodal = []
         for a in range(8):
-            reach = links[pl.ds(64 * m + a, 8, stride=8), :] + lane
-            hi = reach >> 7
-            lo = reach & 127
-            lo_s[a * BLOCKS + 8 * m : a * BLOCKS + 8 * m + 8, :] = lo.astype(F32)
-            hi_s[a * BLOCKS + 8 * m : a * BLOCKS + 8 * m + 8, :] = (hi + block).astype(F32)
-            got = [jnp.zeros((8, LANES), F32)] * 3
-            for h in range(33):
-                here = hi == h
-                for i in range(3):
-                    rows = disp[i, 8 * m + h : 8 * m + h + 8, :]
-                    got[i] = jnp.where(here, jnp.take_along_axis(rows, lo, axis=1), got[i])
-            nodal.append(got)
+            at = slice(a * BLOCKS + 8 * m, a * BLOCKS + 8 * m + 8)
+            got = gather_rows(table, disp, unit, links, m, a, rest, 0)
+            nodal.append([got[i] + part[i, at, :] for i in range(3)])
+            reach = reach_of(links, m, a) + block
+            hi_s[at, :] = (reach >> 7).astype(F32)
+            lo_s[at, :] = (reach & 127).astype(F32)
         edge = edge_ref[8 * m : 8 * m + 8, :]
         scale = 0.25 / edge
         grad = [[None] * 3 for _ in range(3)]
@@ -272,13 +310,17 @@
     )(master_gap[0], seg_major(master_normal), seg_major(master_disp), coupling, quad_weight.reshape(1, LANES))
     rows = swapped(rows)
     links = jnp.transpose(connectivity[0].reshape(8, BLOCKS, LANES), (1, 0, 2)).reshape(8 * BLOCKS, LANES)
+    part = call(
+        gather_kernel, 2, shape(3, 8 * BLOCKS, LANES), 1 << 30, (pltpu.VMEM((BLOCKS, LANES), jnp.int32),)
+    )(own, links)
     far_force, near_force, own_force = call(
         element_kernel,
-        9,
+        10,
         (shape(3, HALO, LANES), shape(3, HALO, LANES), shape(3, BLOCKS, LANES)),
         1 << 32,
         (
-            pltpu.VMEM((3, 2 * HALO + BLOCKS + 16, LANES), F32),
+            pltpu.VMEM((3, 2 * HALO + BLOCKS + 8, LANES), F32),
+            pltpu.VMEM((2 * HALO + BLOCKS + 8, LANES), jnp.int32),
             pltpu.VMEM((8 * BLOCKS, LANES), F32),
             pltpu.VMEM((8 * BLOCKS, LANES), F32),
             pltpu.VMEM((3, 8 * BLOCKS, LANES), F32),
@@ -290,6 +332,7 @@
         near,
         own,
         links,
+        part,
         plastic_strain[0].reshape(6, BLOCKS, LANES),
         element_size.reshape(BLOCKS, LANES),
         yield_stress.reshape(BLOCKS, LANES),

time: 57 us -> 55.1 us (0.967)
  starting transfers between devices: 32.6 us -> 30.7 us
  local copies, waits for them, and re-layouts: 0.66 us -> 1.42 us
  waiting for transfers between devices: 10.4 us -> 9.75 us
    ppermute x4, waiting for transfers between devices: 1.99 us -> 0.01 us  [paired(): return lax.ppermute(block, 'dom', route + [(j, i) for i, j in route])]
    all_to_all x2, starting transfers between devices: 25.1 us -> 23.2 us  [exchanged(): return lax.all_to_all(block, 'dom', split_axis=0, concat_axis=0, tiled=True)]
    all_to_all x2, waiting for transfers between devices: 8.35 us -> 9.73 us  [exchanged(): return lax.all_to_all(block, 'dom', split_axis=0, concat_axis=0, tiled=True)]
    unnamed x24, local copies, waits for them, and re-layouts: 0.66 us -> 1.42 us
    pallas_call x1 -> x2, Pallas kernels: 5.81 us -> 5.64 us  [the longest x1 3.97 us: local(): call(element_kernel, 10, (shape(3, HALO, LANES), shape(3, HALO, LANES), s...]
  transfers between devices with their start and end apart: 8 -> 8, of which waited for: 3 -> 2; matrix products, arithmetic and copies ran while one was open for 0% -> 0% of each run, Pallas kernels for 13% -> 13%
where the time goes in v6:
time: 55.1 us; the launch traced here: 54.7 us
  starting transfers between devices  30.7 us (56%)
  Pallas kernels  12 us (22%)
  waiting for transfers between devices  9.75 us (18%)
  local copies, waits for them, and re-layouts  1.42 us (3%)
  between operations  0.84 us (2%)
    all_to_all x2, starting transfers between devices, exchanged(): return lax.all_to_all(block, 'dom', split_axis=0, concat_axis=0, tiled=True)  23.2 us
    all_to_all x2, waiting for transfers between devices, exchanged(): return lax.all_to_all(block, 'dom', split_axis=0, concat_axis=0, tiled=True)  9.73 us
    ppermute x4, starting transfers between devices, paired(): return lax.ppermute(block, 'dom', route + [(j, i) for i, j in route])  7.32 us
    pallas_call x1, Pallas kernels, local(): call(element_kernel, 10, (shape(3, HALO, LANES), shape(3, HALO, LANES), s...  3.97 us
    pallas_call x1, Pallas kernels, local(): call(pack_kernel, -4, (shape(PEERS * SLOTS, 4 * LANES, dtype=BF16), shape...  2.27 us
    pallas_call x1, Pallas kernels, local(): call(master_kernel, 4, (shape(PEERS * SLOTS, 3 * LANES, dtype=BF16), shap...  2 us
    pallas_call x1, Pallas kernels, local(): call(gather_kernel, 2, shape(3, 8 * BLOCKS, LANES), 1 << 30, (pltpu.VMEM(...  1.67 us
    unnamed x24, local copies, waits for them, and re-layouts  1.42 us
  transfers between devices with their start and end apart: 8, of which 2 were waited for; matrix products, arithmetic and copies ran while one was open for 0% of the time, Pallas kernels for 13%

profile of v6, /device:TPU:0, one launch (start us, length us, event | category | flops | bytes accessed | tf_op | source)
XLA Modules:
  0.0 54.7 jit_solution(14844590391205835467)
XLA Ops:
  0.6 2.3 %shard_map.166 = (bf16[512,512]{1,0:T(8,128)(2,1)}, bf16[512,128]{1,0:T(8,128)(2,1)}) custom-call(s32[2,128]{1,0:T(2,128)} %bitcast.58, s32[2,128]{1,0:T(2,128)} %bitcast.59, s32[1,128]{1,0:T(1,128)} %active.1, bf16[3,128,128]{2,1,0:T(8,128)(2,1)} %bitcast.56), custom_call_target="tpu_custom_call" | custom-call | flops 134217728 | bytes 1048576 | tf_op jit(solution)/shard_map/pallas_call | solution.py:293
  2.9 0.0 copy-start.4
  2.9 0.0 copy-start
  2.9 0.0 copy-start.3
  2.9 0.0 copy-start.5
  2.9 11.7 %all-to-all-start = ((bf16[64,8,512]{2,1,0:T(8,128)(2,1)}), bf16[64,8,512]{2,1,0:T(8,128)(2,1)S(1)}, u32[]{:S(2)}, u32[]{:S(2)}) async-start(bf16[64,8,512]{2,1,0:T(8,128)(2,1)} %bitcast.53), calls=%async_computation | async-start | bytes 1048576 | tf_op jit(solution)/shard_map/all_to_all | solution.py:272
  14.6 0.0 copy-start.2
  14.6 0.0 copy-done.4
  14.7 1.6 %collective-permute-start.1 = (f32[3,16,128]{2,1,0:T(8,128)S(1)}, f32[3,16,128]{2,1,0:T(8,128)S(1)}, u32[]{:S(2)}, u32[]{:S(2)}) collective-permute-start(f32[3,16,128]{2,1,0:T(8,128)S(1)} %get-tuple-element.43), channel_id=1, source_target_pairs={{0,1},{2,3},{4,5},{6,7},{8,9},{10,11},{12,13},{14,15},{16,17},{18,... | collective-permute-start | bytes 73736 | tf_op jit(solution)/shard_map/ppermute | solution.py:264
  16.3 0.7 %collective-permute-start = (f32[3,16,128]{2,1,0:T(8,128)S(1)}, f32[3,16,128]{2,1,0:T(8,128)S(1)}, u32[]{:S(2)}, u32[]{:S(2)}) collective-permute-start(f32[3,16,128]{2,1,0:T(8,128)S(1)} %get-tuple-element.44), channel_id=1, source_target_pairs={{1,2},{3,4},{5,6},{7,8},{9,10},{11,12},{13,14},{15,16},{17,18},{19... | collective-permute-start | bytes 73736 | tf_op jit(solution)/shard_map/ppermute | solution.py:264
  17.0 0.0 copy-start.6
  17.0 0.0 copy-done
  17.0 0.0 copy-done.3
  17.0 0.0 copy-done.5
  17.0 0.0 copy-done.2
  17.0 0.6 %copy-done.6 = f32[128]{0:T(128)S(1)} copy-done((f32[128]{0:T(128)S(1)}, f32[128]{0:T(128)}, u32[]{:S(2)}) %copy-start.6) | copy-done | bytes 536
  17.6 0.0 copy-start.7
  17.7 0.1 collective-permute-start.2
  17.8 0.8 %copy-done.7 = s32[1,8,4096]{2,1,0:T(8,128)S(1)} copy-done((s32[1,8,4096]{2,1,0:T(8,128)S(1)}, s32[1,8,4096]{2,1,0:T(8,128)}, u32[]{:S(2)}) %copy-start.7) | copy-done | bytes 131096
  18.5 0.0 copy-start.8
  18.5 0.0 copy-start.9
  18.5 0.0 copy-start.10
  18.5 0.0 copy-start.11
  18.5 1.7 %shard_map.167.part = f32[3,256,128]{2,1,0:T(8,128)S(1)} custom-call(f32[3,32,128]{2,1,0:T(8,128)S(1)} %bitcast.44, s32[256,128]{1,0:T(8,128)S(1)} %bitcast.47), custom_call_target="tpu_custom_call" | custom-call | flops 1073741824 | bytes 1048576 | tf_op jit(solution)/shard_map/pallas_call | solution.py:313
  20.2 0.0 collective-permute-done.1.near
  20.2 0.0 collective-permute-done.far
  20.2 0.0 copy-done.8
  20.3 0.0 copy-done.9
  20.3 0.0 copy-done.10
  20.3 0.0 copy-done.11
  20.3 4.0 %shard_map.168 = (f32[3,16,128]{2,1,0:T(8,128)S(1)}, f32[3,16,128]{2,1,0:T(8,128)S(1)}, f32[3,32,128]{2,1,0:T(8,128)S(1)}) custom-call(s32[8,128]{1,0:T(8,128)S(1)} %broadcast_in_dim.9.parity, f32[3,16,128]{2,1,0:T(8,128)S(1)} %collective-permute-done.far, f32[3,16,128]{2,1,0:T(8,128)S(1)} %collective-permute-done.1.near, f32[3,32,128]{2,1,0:T(8,128)S(1)} %bitcast.45, ...), custom_call_target="tpu_custom_call" | custom-call | flops 4294967296 | bytes 1048576 | tf_op jit(solution)/shard_map/pallas_call | solution.py:316
  24.3 3.6 %all-to-all-done = bf16[64,8,512]{2,1,0:T(8,128)(2,1)S(1)} async-done(((bf16[64,8,512]{2,1,0:T(8,128)(2,1)}), bf16[64,8,512]{2,1,0:T(8,128)(2,1)S(1)}, u32[]{:S(2)}, u32[]{:S(2)}) %all-to-all-start) | async-done | bytes 524320 | tf_op jit(solution)/shard_map/all_to_all | solution.py:272
  27.9 0.0 collective-permute-done.2.rows
  27.9 2.0 %shard_map.170 = (bf16[512,384]{1,0:T(8,128)(2,1)}, f32[3,128,128]{2,1,0:T(8,128)S(1)}) custom-call(bf16[512,512]{1,0:T(8,128)(2,1)S(1)} %bitcast.39, f32[4,128,128]{2,1,0:T(8,128)S(1)} %collective-permute-done.2.rows, bf16[128,128]{1,0:T(8,128)(2,1)S(1)} %get-tuple-element.25.mortar_ref, f32[8,128]{1,0:T(8,128)S(1)} %get-tuple-element.26.weight), custom_call_target="tpu_custom_call" | custom-call | flops 268435456 | bytes 1048576 | tf_op jit(solution)/shard_map/pallas_call | solution.py:343
  29.9 0.0 copy-start.1
  29.9 11.6 %all-to-all-start.1 = ((bf16[64,8,384]{2,1,0:T(8,128)(2,1)}), bf16[64,8,384]{2,1,0:T(8,128)(2,1)S(1)}, u32[]{:S(2)}, u32[]{:S(2)}) async-start(bf16[64,8,384]{2,1,0:T(8,128)(2,1)} %bitcast.24), calls=%async_computation.1 | async-start | bytes 786432 | tf_op jit(solution)/shard_map/all_to_all | solution.py:272
  41.5 0.1 collective-permute-start.5
  41.6 0.7 %collective-permute-start.3 = (f32[3,16,128]{2,1,0:T(8,128)S(1)}, f32[3,16,128]{2,1,0:T(8,128)S(1)}, u32[]{:S(2)}, u32[]{:S(2)}) collective-permute-start(f32[3,16,128]{2,1,0:T(8,128)S(1)} %get-tuple-element.31), channel_id=1, source_target_pairs={{1,2},{3,4},{5,6},{7,8},{9,10},{11,12},{13,14},{15,16},{17,18},{19... | collective-permute-start | bytes 73736 | tf_op jit(solution)/shard_map/ppermute | solution.py:264
  42.2 4.4 %collective-permute-start.4 = (f32[3,16,128]{2,1,0:T(8,128)S(1)}, f32[3,16,128]{2,1,0:T(8,128)S(1)}, u32[]{:S(2)}, u32[]{:S(2)}) collective-permute-start(f32[3,16,128]{2,1,0:T(8,128)S(1)} %get-tuple-element.32), channel_id=1, source_target_pairs={{0,1},{2,3},{4,5},{6,7},{8,9},{10,11},{12,13},{14,15},{16,17},{18,... | collective-permute-start | bytes 73736 | tf_op jit(solution)/shard_map/ppermute | solution.py:264
  46.6 6.1 %all-to-all-done.1 = bf16[64,8,384]{2,1,0:T(8,128)(2,1)S(1)} async-done(((bf16[64,8,384]{2,1,0:T(8,128)(2,1)}), bf16[64,8,384]{2,1,0:T(8,128)(2,1)S(1)}, u32[]{:S(2)}, u32[]{:S(2)}) %all-to-all-start.1) | async-done | bytes 393248 | tf_op jit(solution)/shard_map/all_to_all | solution.py:272
  52.7 0.0 copy-done.1
  52.7 1.3 %shard_map.171 = f32[3,128,128]{2,1,0:T(8,128)} custom-call(bf16[512,384]{1,0:T(8,128)(2,1)S(1)} %bitcast.38, bf16[512,128]{1,0:T(8,128)(2,1)S(1)} %copy-done.1, bf16[128,128]{1,0:T(8,128)(2,1)S(1)} %get-tuple-element.25.mortar_ref), custom_call_target="tpu_custom_call" | custom-call | flops 134217728 | bytes 1048576 | tf_op jit(solution)/shard_map/pallas_call | solution.py:347
  54.0 0.0 collective-permute-done.3.far
  54.0 0.0 collective-permute-done.4.near
  54.0 0.0 collective-permute-done.5.force
  54.0 0.7 %shard_map.172 = (f32[3,32,128]{2,1,0:T(8,128)}, f32[3,128,128]{2,1,0:T(8,128)}) custom-call(s32[8,128]{1,0:T(8,128)S(1)} %broadcast_in_dim.9.parity, f32[3,32,128]{2,1,0:T(8,128)S(1)} %get-tuple-element.30.own, f32[3,16,128]{2,1,0:T(8,128)S(1)} %collective-permute-done.3.far, f32[3,16,128]{2,1,0:T(8,128)S(1)} %collective-permute-done.4.near, ...), custom_call_target="tpu_custom_call" | custom-call | flops 1048576 | bytes 1048576 | tf_op jit(solution)/shard_map/pallas_call | solution.py:349
  (3 shorter events, 0.1 us)
Async XLA Ops:
  2.9 11.7 %copy-start.4 = (f32[1,3,4096]{2,0,1:T(1,128)S(1)}, f32[1,3,4096]{2,0,1:T(1,128)}, u32[]{:S(2)}) copy-start(f32[1,3,4096]{2,0,1:T(1,128)} %param.15) | copy-start | bytes 147460
  2.9 14.1 %copy-start = (f32[1,128,3,128]{3,1,2,0:T(8,128)S(1)}, f32[1,128,3,128]{3,1,2,0:T(8,128)}, u32[]{:S(2)}) copy-start(f32[1,128,3,128]{3,1,2,0:T(8,128)} %param.26) | copy-start | bytes 589828
  2.9 14.1 %copy-start.3 = (f32[1,128,128]{2,1,0:T(8,128)S(1)}, f32[1,128,128]{2,1,0:T(8,128)}, u32[]{:S(2)}) copy-start(f32[1,128,128]{2,1,0:T(8,128)} %param.25) | copy-start | bytes 196612
  2.9 14.1 %copy-start.5 = (bf16[128,128]{1,0:T(8,128)(2,1)S(1)}, bf16[128,128]{1,0:T(8,128)(2,1)}, u32[]{:S(2)}) copy-start(bf16[128,128]{1,0:T(8,128)(2,1)} %coupling.1) | copy-start | bytes 98308
  2.9 25.0 %all-to-all-start = ((bf16[64,8,512]{2,1,0:T(8,128)(2,1)}), bf16[64,8,512]{2,1,0:T(8,128)(2,1)S(1)}, u32[]{:S(2)}, u32[]{:S(2)}) async-start(bf16[64,8,512]{2,1,0:T(8,128)(2,1)} %bitcast.53), calls=%async_computation | async-start | bytes 1048576 | tf_op jit(solution)/shard_map/all_to_all | solution.py:272
  14.6 2.4 %copy-start.2 = (bf16[1,128,3,128]{3,1,2,0:T(8,128)(2,1)S(1)}, bf16[1,128,3,128]{3,1,2,0:T(8,128)(2,1)}, u32[]{:S(2)}) copy-start(bf16[1,128,3,128]{3,1,2,0:T(8,128)(2,1)} %param.27) | copy-start | bytes 294916
  14.7 5.6 %collective-permute-start.1 = (f32[3,16,128]{2,1,0:T(8,128)S(1)}, f32[3,16,128]{2,1,0:T(8,128)S(1)}, u32[]{:S(2)}, u32[]{:S(2)}) collective-permute-start(f32[3,16,128]{2,1,0:T(8,128)S(1)} %get-tuple-element.43), channel_id=1, source_target_pairs={{0,1},{2,3},{4,5},{6,7},{8,9},{10,11},{12,13},{14,15},{16,17},{18,... | collective-permute-start | bytes 73736 | tf_op jit(solution)/shard_map/ppermute | solution.py:264
  16.3 3.9 %collective-permute-start = (f32[3,16,128]{2,1,0:T(8,128)S(1)}, f32[3,16,128]{2,1,0:T(8,128)S(1)}, u32[]{:S(2)}, u32[]{:S(2)}) collective-permute-start(f32[3,16,128]{2,1,0:T(8,128)S(1)} %get-tuple-element.44), channel_id=1, source_target_pairs={{1,2},{3,4},{5,6},{7,8},{9,10},{11,12},{13,14},{15,16},{17,18},{19... | collective-permute-start | bytes 73736 | tf_op jit(solution)/shard_map/ppermute | solution.py:264
  17.0 0.7 %copy-start.6 = (f32[128]{0:T(128)S(1)}, f32[128]{0:T(128)}, u32[]{:S(2)}) copy-start(f32[128]{0:T(128)} %param.29) | copy-start | bytes 1540
  17.6 0.9 %copy-start.7 = (s32[1,8,4096]{2,1,0:T(8,128)S(1)}, s32[1,8,4096]{2,1,0:T(8,128)}, u32[]{:S(2)}) copy-start(s32[1,8,4096]{2,1,0:T(8,128)} %param.16) | copy-start | bytes 393220
  17.7 10.2 %collective-permute-start.2 = (f32[4,128,128]{2,1,0:T(8,128)S(1)}, f32[4,128,128]{2,1,0:T(8,128)S(1)}, u32[]{:S(2)}, u32[]{:S(2)}) collective-permute-start(f32[4,128,128]{2,1,0:T(8,128)S(1)} %get-tuple-element.24), channel_id=1, source_target_pairs={{0,64},{64,0},{1,65},{65,1},{2,66},{66,2},{3,67},{67,3},{4,68},{68... | collective-permute-start | bytes 786440 | tf_op jit(solution)/shard_map/ppermute | solution.py:268
  18.5 1.7 %copy-start.8 = (f32[1,6,4096]{2,0,1:T(1,128)S(1)}, f32[1,6,4096]{2,0,1:T(1,128)}, u32[]{:S(2)}) copy-start(f32[1,6,4096]{2,0,1:T(1,128)} %param.17) | copy-start | bytes 294916
  18.5 1.7 %copy-start.9 = (f32[1,3,4096]{2,0,1:T(1,128)S(1)}, f32[1,3,4096]{2,0,1:T(1,128)}, u32[]{:S(2)}) copy-start(f32[1,3,4096]{2,0,1:T(1,128)} %param.20) | copy-start | bytes 147460
  18.5 1.7 %copy-start.10 = (f32[1,4096]{1,0:T(1,128)S(1)}, f32[1,4096]{1,0:T(1,128)}, u32[]{:S(2)}) copy-start(f32[1,4096]{1,0:T(1,128)} %param.18) | copy-start | bytes 49156
  18.5 1.7 %copy-start.11 = (f32[1,4096]{1,0:T(1,128)S(1)}, f32[1,4096]{1,0:T(1,128)}, u32[]{:S(2)}) copy-start(f32[1,4096]{1,0:T(1,128)} %param.19) | copy-start | bytes 49156
  29.9 22.8 %copy-start.1 = (bf16[512,128]{1,0:T(8,128)(2,1)S(1)}, bf16[512,128]{1,0:T(8,128)(2,1)}, u32[]{:S(2)}) copy-start(bf16[512,128]{1,0:T(8,128)(2,1)} %get-tuple-element.28.place) | copy-start | bytes 393220
  29.9 22.8 %all-to-all-start.1 = ((bf16[64,8,384]{2,1,0:T(8,128)(2,1)}), bf16[64,8,384]{2,1,0:T(8,128)(2,1)S(1)}, u32[]{:S(2)}, u32[]{:S(2)}) async-start(bf16[64,8,384]{2,1,0:T(8,128)(2,1)} %bitcast.24), calls=%async_computation.1 | async-start | bytes 786432 | tf_op jit(solution)/shard_map/all_to_all | solution.py:272
  41.5 12.6 %collective-permute-start.5 = (f32[3,128,128]{2,1,0:T(8,128)S(1)}, f32[3,128,128]{2,1,0:T(8,128)S(1)}, u32[]{:S(2)}, u32[]{:S(2)}) collective-permute-start(f32[3,128,128]{2,1,0:T(8,128)S(1)} %get-tuple-element.33), channel_id=1, source_target_pairs={{0,64},{64,0},{1,65},{65,1},{2,66},{66,2},{3,67},{67,3},{4,68},{68... | collective-permute-start | bytes 589832 | tf_op jit(solution)/shard_map/ppermute | solution.py:268
  41.6 12.5 %collective-permute-start.3 = (f32[3,16,128]{2,1,0:T(8,128)S(1)}, f32[3,16,128]{2,1,0:T(8,128)S(1)}, u32[]{:S(2)}, u32[]{:S(2)}) collective-permute-start(f32[3,16,128]{2,1,0:T(8,128)S(1)} %get-tuple-element.31), channel_id=1, source_target_pairs={{1,2},{3,4},{5,6},{7,8},{9,10},{11,12},{13,14},{15,16},{17,18},{19... | collective-permute-start | bytes 73736 | tf_op jit(solution)/shard_map/ppermute | solution.py:264
  42.2 11.8 %collective-permute-start.4 = (f32[3,16,128]{2,1,0:T(8,128)S(1)}, f32[3,16,128]{2,1,0:T(8,128)S(1)}, u32[]{:S(2)}, u32[]{:S(2)}) collective-permute-start(f32[3,16,128]{2,1,0:T(8,128)S(1)} %get-tuple-element.32), channel_id=1, source_target_pairs={{0,1},{2,3},{4,5},{6,7},{8,9},{10,11},{12,13},{14,15},{16,17},{18,... | collective-permute-start | bytes 73736 | tf_op jit(solution)/shard_map/ppermute | solution.py:264

commit v7 on v6

--- a/solution.py
+++ b/solution.py
@@ -167,31 +167,37 @@
     out[:, HALO:BLOCKS, :] = own[:, HALO:BLOCKS, :] + jnp.where(odd, far[...], near[...])
 
 
-def pack_kernel(owner, where, active, disp, send, place):
+def pack_kernel(owner, where, active, disp, send, slots, held, sem):
     names = iota((PEERS, SEG), 0)
     earlier = jnp.where(iota((SEG, SEG), 0) < iota((SEG, SEG), 1), 1.0, 0.0).astype(BF16)
     ones = jnp.ones((SEG, SEG), BF16)
     hot = [owner[k : k + 1, :] == names for k in range(2)]
     hot16 = [jnp.where(h, 1.0, 0.0).astype(BF16) for h in hot]
     before = [dot(hot16[0], earlier), dot(hot16[1], earlier) + dot(hot16[0], ones)]
-    slots = iota((PEERS * SLOTS, SEG), 0)
-    sent = jnp.zeros((PEERS * SLOTS, SEG), F32)
-    meta = jnp.zeros((PEERS * SLOTS, SEG), F32)
+    slot, mark = [], []
     for k in range(2):
         rank = jnp.sum(jnp.where(hot[k], before[k], 0.0), axis=0, keepdims=True)
-        slot = owner[k : k + 1, :] * SLOTS + rank.astype(jnp.int32)
-        mark = ((where[k : k + 1, :] + 1) * active[...]).astype(F32)
-        here = slot == slots
-        sent = jnp.where(here, 1.0, sent)
-        meta = jnp.where(here, mark, meta)
-    sent = sent.astype(BF16)
-    place[...] = sent
-    for c in range(3):
-        send[:, c * LANES : (c + 1) * LANES] = dot(sent, disp[c]).astype(BF16)
-    send[:, 3 * LANES :] = dot(meta.astype(BF16), ones).astype(BF16)
-
-
-def rows_kernel(gap, normal, mdisp, coupling, quad_weight, rows, mortar, weight):
+        slot.append(owner[k : k + 1, :] * SLOTS + rank.astype(jnp.int32))
+        mark.append(((where[k : k + 1, :] + 1) * active[...]).astype(F32))
+        slots[k : k + 1, :] = slot[k]
+    copies = []
+    for part in range(PEERS * SLOTS // SEG):
+        span = slice(part * SEG, (part + 1) * SEG)
+        rows = iota((SEG, SEG), 0) + part * SEG
+        here = [slot[k] == rows for k in range(2)]
+        sent = jnp.where(here[0] | here[1], 1.0, 0.0).astype(BF16)
+        meta = jnp.where(here[0], mark[0], jnp.where(here[1], mark[1], 0.0)).astype(BF16)
+        for c in range(3):
+            held[span, c * LANES : (c + 1) * LANES] = dot(sent, disp[c]).astype(BF16)
+        held[span, 3 * LANES :] = dot(meta, ones).astype(BF16)
+        copies.append(pltpu.make_async_copy(held.at[span], send.at[span], sem.at[part]))
+        copies[-1].start()
+    for copy in copies:
+        copy.wait()
+
+
+def rows_kernel(gap, normal, mdisp, coupling, quad_weight, slots, rows, mortar, weight, slots_out):
+    slots_out[...] = slots[...]
     mortar[...] = mortar_of(coupling)
     weight[...] = jnp.broadcast_to(quad_weight[...], weight.shape)
     total = gap[...]
@@ -212,32 +218,49 @@
     return top, (x - top.astype(F32)).astype(BF16)
 
 
-def master_kernel(got, rows, mortar_ref, weight, back, force):
+def master_kernel(got, rows, mortar_ref, weight, back, force, held, table, sem):
     mortar = mortar_ref[...]
-    table = [split(rows[c]) for c in range(4)]
+    for c in range(4):
+        table[0:SEG, c * LANES : (c + 1) * LANES], table[SEG:, c * LANES : (c + 1) * LANES] = split(rows[c])
     name = iota((SEG, LANES), 1, F32) + 1.0
-    totals = [jnp.zeros((SEG, LANES), F32)] * 3
-    for part in range(PEERS * SLOTS // SEG):
+    parts = range(PEERS * SLOTS // SEG)
+    hots, copies = [], []
+    for part in parts:
         span = slice(part * SEG, (part + 1) * SEG)
         hot = jnp.where(got[span, 3 * LANES :].astype(F32) == name, 1.0, 0.0).astype(BF16)
-        gap, n0, n1, n2 = (dot(hot, t) + dot(hot, b) for t, b in table)
-        normal = (n0, n1, n2)
+        hots.append(hot)
+        found = dot(jnp.concatenate([hot, hot], axis=1), table[...])
+        gap = found[:, :LANES]
+        normal = [found[:, (1 + c) * LANES : (2 + c) * LANES] for c in range(3)]
         for c in range(3):
             gap = gap - normal[c] * dot(got[span, c * LANES : (c + 1) * LANES], mortar)
         press = weight[0:1, :] * (2.0 * jnp.maximum(gap, 0.0))
         for c in range(3):
-            top, low = split(press * normal[c])
-            back[span, c * LANES : (c + 1) * LANES] = top
-            totals[c] = totals[c] + dot(hot, top, TN) + dot(hot, low, TN)
+            held[span, c * LANES : (c + 1) * LANES] = (press * normal[c]).astype(BF16)
+        copies.append(pltpu.make_async_copy(held.at[span], back.at[span], sem.at[part]))
+        copies[-1].start()
+    total = dot(jnp.concatenate(hots, axis=0), held[...], TN)
     for c in range(3):
-        force[c] = -totals[c]
-
-
-def slave_kernel(got, place, mortar_ref, out):
+        force[c] = -total[:, c * LANES : (c + 1) * LANES]
+    for copy in copies:
+        copy.wait()
+
+
+def slave_kernel(got, slots, mortar_ref, out, held, sem):
     mortar = mortar_ref[...]
+    place = []
+    for part in range(PEERS * SLOTS // SEG):
+        rows = iota((SEG, SEG), 0) + part * SEG
+        here = (slots[0:1, :] == rows) | (slots[1:2, :] == rows)
+        place.append(jnp.where(here, 1.0, 0.0).astype(BF16))
+    pair = dot(jnp.concatenate(place, axis=0), got[...], TN).astype(BF16)
+    copies = []
     for c in range(3):
-        pair = dot(place[...], got[:, c * LANES : (c + 1) * LANES], TN).astype(BF16)
-        out[c] = dot(pair, mortar, NT)
+        held[c] = dot(pair[:, c * LANES : (c + 1) * LANES], mortar, NT)
+        copies.append(pltpu.make_async_copy(held.at[c], out.at[c], sem.at[c]))
+        copies[-1].start()
+    for copy in copies:
+        copy.wait()
 
 
 def shape(*dims, dtype=F32):
@@ -247,12 +270,15 @@
 VMEM = pl.BlockSpec(memory_space=pltpu.VMEM)
 
 
-def call(kernel, ins, outs, cost, scratch=(), grant=8 << 20):
+HBM = pl.BlockSpec(memory_space=pl.ANY)
+
+
+def call(kernel, ins, outs, cost, scratch=(), grant=8 << 20, places=None):
     return pl.pallas_call(
         kernel,
         out_shape=outs,
         in_specs=[VMEM] * ins if ins > 0 else [pl.BlockSpec()] * -ins,
-        out_specs=jax.tree.map(lambda _: VMEM if ins > 0 else pl.BlockSpec(), outs),
+        out_specs=jax.tree.map(lambda _: VMEM, outs) if places is None else places,
         scratch_shapes=scratch,
         compiler_params=pltpu.CompilerParams(vmem_limit_bytes=grant),
         cost_estimate=pl.CostEstimate(flops=cost, bytes_accessed=1 << 20, transcendentals=0),
@@ -290,12 +316,14 @@
     quad_weight,
 ):
     seg_major = lambda x: jnp.transpose(x[0], (1, 0, 2))
-    send, place = call(
+    send, slots = call(
         pack_kernel,
         -4,
-        (shape(PEERS * SLOTS, 4 * LANES, dtype=BF16), shape(PEERS * SLOTS, SEG, dtype=BF16)),
+        (shape(PEERS * SLOTS, 4 * LANES, dtype=BF16), shape(2, SEG, dtype=jnp.int32)),
         1 << 27,
+        (pltpu.VMEM((PEERS * SLOTS, 4 * LANES), BF16), pltpu.SemaphoreType.DMA((4,))),
         grant=60 << 20,
+        places=(HBM, pl.BlockSpec()),
     )(pair_owner[0].T, pair_local[0].T, active, seg_major(slave_disp))
     got = exchanged(send)
 
@@ -305,9 +333,17 @@
     first, last = own[:, :HALO], own[:, BLOCKS - HALO :]
     far = paired(jnp.where(odd == 1, last, first), 1)
     near = paired(jnp.where(odd == 1, first, last), 0)
-    rows, mortar, weight = call(
-        rows_kernel, 5, (shape(4, SEG, LANES), shape(LANES, LANES, dtype=BF16), shape(8, LANES)), 1 << 20
-    )(master_gap[0], seg_major(master_normal), seg_major(master_disp), coupling, quad_weight.reshape(1, LANES))
+    rows, mortar, weight, slots = call(
+        rows_kernel,
+        6,
+        (
+            shape(4, SEG, LANES),
+            shape(LANES, LANES, dtype=BF16),
+            shape(8, LANES),
+            shape(2, SEG, dtype=jnp.int32),
+        ),
+        1 << 20,
+    )(master_gap[0], seg_major(master_normal), seg_major(master_disp), coupling, quad_weight.reshape(1, LANES), slots)
     rows = swapped(rows)
     links = jnp.transpose(connectivity[0].reshape(8, BLOCKS, LANES), (1, 0, 2)).reshape(8 * BLOCKS, LANES)
     part = call(
@@ -341,13 +377,28 @@
 
     got, far_force, near_force = lax.optimization_barrier((got, far_force, near_force))
     back, force = call(
-        master_kernel, 4, (shape(PEERS * SLOTS, 3 * LANES, dtype=BF16), shape(3, SEG, LANES)), 1 << 28
+        master_kernel,
+        4,
+        (shape(PEERS * SLOTS, 3 * LANES, dtype=BF16), shape(3, SEG, LANES)),
+        1 << 28,
+        (
+            pltpu.VMEM((PEERS * SLOTS, 3 * LANES), BF16),
+            pltpu.VMEM((2 * SEG, 4 * LANES), BF16),
+            pltpu.SemaphoreType.DMA((4,)),
+        ),
+        places=(HBM, VMEM),
     )(got, rows, mortar, weight)
     returned = exchanged(back)
-    slave_force = call(slave_kernel, 3, shape(3, SEG, LANES), 1 << 27)(returned, place, mortar)
-    parity_late, slave_force = lax.optimization_barrier((parity, slave_force))
+    slave_force = call(
+        slave_kernel,
+        3,
+        shape(3, SEG, LANES),
+        1 << 27,
+        (pltpu.VMEM((3, SEG, LANES), F32), pltpu.SemaphoreType.DMA((3,))),
+        places=HBM,
+    )(returned, slots, mortar)
     residual, master_force = call(finish_kernel, 5, (shape(3, BLOCKS, LANES), shape(3, SEG, LANES)), 1 << 20)(
-        parity_late, own_force, paired(far_force, 1), paired(near_force, 0), swapped(force)
+        parity, own_force, paired(far_force, 1), paired(near_force, 0), swapped(force)
     )
     return (
         residual.reshape(1, 3, BLOCKS * LANES),

time: 55.1 us -> 53.7 us (0.975)
  waiting for transfers between devices: 9.75 us -> 9.02 us
  Pallas kernels: 12 us -> 11.4 us
    all_to_all x2, waiting for transfers between devices: 9.73 us -> 6.9 us  [exchanged(): return lax.all_to_all(block, 'dom', split_axis=0, concat_axis=0, tiled=True)]
    ppermute x4, waiting for transfers between devices: 0.01 us -> 2.12 us  [paired(): return lax.ppermute(block, 'dom', route + [(j, i) for i, j in route])]
    pallas_call x1, Pallas kernels: 2 us -> 1.24 us  [local(): call(master_kernel, 4, (shape(PEERS * SLOTS, 3 * LANES, dtype=BF16), shap...]
  transfers between devices with their start and end apart: 8 -> 8, of which waited for: 2 -> 3; matrix products, arithmetic and copies ran while one was open for 0% -> 0% of each run, Pallas kernels for 13% -> 12%
where the time goes in v7:
time: 53.7 us; the launch traced here: 53.4 us
  starting transfers between devices  30.6 us (57%)
  Pallas kernels  11.4 us (21%)
  waiting for transfers between devices  9.02 us (17%)
  local copies, waits for them, and re-layouts  1.45 us (3%)
  between operations  0.88 us (2%)
    all_to_all x2, starting transfers between devices, exchanged(): return lax.all_to_all(block, 'dom', split_axis=0, concat_axis=0, tiled=True)  23.1 us
    ppermute x4, starting transfers between devices, paired(): return lax.ppermute(block, 'dom', route + [(j, i) for i, j in route])  7.32 us
    all_to_all x2, waiting for transfers between devices, exchanged(): return lax.all_to_all(block, 'dom', split_axis=0, concat_axis=0, tiled=True)  6.9 us
    pallas_call x1, Pallas kernels, local(): call(element_kernel, 10, (shape(3, HALO, LANES), shape(3, HALO, LANES), s...  3.95 us
    pallas_call x1, Pallas kernels, local(): call(pack_kernel, -4, (shape(PEERS * SLOTS, 4 * LANES, dtype=BF16), shape...  2.73 us
    ppermute x4, waiting for transfers between devices, paired(): return lax.ppermute(block, 'dom', route + [(j, i) for i, j in route])  2.12 us
    pallas_call x1, Pallas kernels, local(): call(gather_kernel, 2, shape(3, 8 * BLOCKS, LANES), 1 << 30, (pltpu.VMEM(...  1.67 us
    unnamed x24, local copies, waits for them, and re-layouts  1.44 us
  transfers between devices with their start and end apart: 8, of which 3 were waited for; matrix products, arithmetic and copies ran while one was open for 0% of the time, Pallas kernels for 12%

profile of v7, /device:TPU:0, one launch (start us, length us, event | category | flops | bytes accessed | tf_op | source)
XLA Modules:
  0.0 53.4 jit_solution(93207801077794684)
XLA Ops:
  0.6 2.7 %shard_map.168 = (bf16[512,512]{1,0:T(8,128)(2,1)}, s32[2,128]{1,0:T(2,128)}) custom-call(s32[2,128]{1,0:T(2,128)} %bitcast.58, s32[2,128]{1,0:T(2,128)} %bitcast.59, s32[1,128]{1,0:T(1,128)} %active.1, bf16[3,128,128]{2,1,0:T(8,128)(2,1)} %bitcast.56), custom_call_target="tpu_custom_call" | custom-call | flops 134217728 | bytes 1048576 | tf_op jit(solution)/shard_map/pallas_call | solution.py:319
  3.4 0.0 copy-start.3
  3.4 0.0 copy-start
  3.4 0.0 copy-start.2
  3.4 0.0 copy-start.4
  3.4 11.7 %all-to-all-start = ((bf16[64,8,512]{2,1,0:T(8,128)(2,1)}), bf16[64,8,512]{2,1,0:T(8,128)(2,1)S(1)}, u32[]{:S(2)}, u32[]{:S(2)}) async-start(bf16[64,8,512]{2,1,0:T(8,128)(2,1)} %bitcast.53), calls=%async_computation | async-start | bytes 1048576 | tf_op jit(solution)/shard_map/all_to_all | solution.py:298
  15.1 0.0 copy-start.1
  15.1 0.0 copy-done.3
  15.1 1.6 %collective-permute-start.1 = (f32[3,16,128]{2,1,0:T(8,128)S(1)}, f32[3,16,128]{2,1,0:T(8,128)S(1)}, u32[]{:S(2)}, u32[]{:S(2)}) collective-permute-start(f32[3,16,128]{2,1,0:T(8,128)S(1)} %get-tuple-element.41), channel_id=1, source_target_pairs={{0,1},{2,3},{4,5},{6,7},{8,9},{10,11},{12,13},{14,15},{16,17},{18,... | collective-permute-start | bytes 73736 | tf_op jit(solution)/shard_map/ppermute | solution.py:290
  16.8 0.7 %collective-permute-start = (f32[3,16,128]{2,1,0:T(8,128)S(1)}, f32[3,16,128]{2,1,0:T(8,128)S(1)}, u32[]{:S(2)}, u32[]{:S(2)}) collective-permute-start(f32[3,16,128]{2,1,0:T(8,128)S(1)} %get-tuple-element.42), channel_id=1, source_target_pairs={{1,2},{3,4},{5,6},{7,8},{9,10},{11,12},{13,14},{15,16},{17,18},{19... | collective-permute-start | bytes 73736 | tf_op jit(solution)/shard_map/ppermute | solution.py:290
  17.4 0.0 copy-start.5
  17.5 0.0 copy-start.6
  17.5 0.0 copy-done
  17.5 0.0 copy-done.2
  17.5 0.0 copy-done.4
  17.5 0.0 copy-done.1
  17.5 0.6 %copy-done.5 = s32[2,128]{1,0:T(2,128)S(1)} copy-done((s32[2,128]{1,0:T(2,128)S(1)}, s32[2,128]{1,0:T(2,128)}, u32[]{:S(2)}) %copy-start.5) | copy-done | bytes 1048
  18.1 0.0 copy-done.6
  18.1 0.0 copy-start.7
  18.2 0.1 collective-permute-start.4
  18.3 0.8 %copy-done.7 = s32[1,8,4096]{2,1,0:T(8,128)S(1)} copy-done((s32[1,8,4096]{2,1,0:T(8,128)S(1)}, s32[1,8,4096]{2,1,0:T(8,128)}, u32[]{:S(2)}) %copy-start.7) | copy-done | bytes 131096
  19.0 0.0 copy-start.8
  19.0 0.0 copy-start.9
  19.0 0.0 copy-start.10
  19.0 0.0 copy-start.11
  19.0 1.7 %shard_map.166.part = f32[3,256,128]{2,1,0:T(8,128)S(1)} custom-call(f32[3,32,128]{2,1,0:T(8,128)S(1)} %bitcast.44, s32[256,128]{1,0:T(8,128)S(1)} %bitcast.47), custom_call_target="tpu_custom_call" | custom-call | flops 1073741824 | bytes 1048576 | tf_op jit(solution)/shard_map/pallas_call | solution.py:349
  20.7 0.0 collective-permute-done.1.near
  20.7 0.0 collective-permute-done.far
  20.8 0.0 copy-done.8
  20.8 0.0 copy-done.9
  20.8 0.0 copy-done.10
  20.8 0.0 copy-done.11
  20.8 3.9 %shard_map.167 = (f32[3,16,128]{2,1,0:T(8,128)S(1)}, f32[3,16,128]{2,1,0:T(8,128)S(1)}, f32[3,32,128]{2,1,0:T(8,128)S(1)}) custom-call(s32[8,128]{1,0:T(8,128)S(1)} %broadcast_in_dim.9.parity, f32[3,16,128]{2,1,0:T(8,128)S(1)} %collective-permute-done.far, f32[3,16,128]{2,1,0:T(8,128)S(1)} %collective-permute-done.1.near, f32[3,32,128]{2,1,0:T(8,128)S(1)} %bitcast.45, ...), custom_call_target="tpu_custom_call" | custom-call | flops 4294967296 | bytes 1048576 | tf_op jit(solution)/shard_map/pallas_call | solution.py:352
  24.7 3.6 %all-to-all-done = bf16[64,8,512]{2,1,0:T(8,128)(2,1)S(1)} async-done(((bf16[64,8,512]{2,1,0:T(8,128)(2,1)}), bf16[64,8,512]{2,1,0:T(8,128)(2,1)S(1)}, u32[]{:S(2)}, u32[]{:S(2)}) %all-to-all-start) | async-done | bytes 524320 | tf_op jit(solution)/shard_map/all_to_all | solution.py:298
  28.4 0.0 collective-permute-done.4.rows
  28.4 1.2 %shard_map.170 = (bf16[512,384]{1,0:T(8,128)(2,1)}, f32[3,128,128]{2,1,0:T(8,128)S(1)}) custom-call(bf16[512,512]{1,0:T(8,128)(2,1)S(1)} %bitcast.39, f32[4,128,128]{2,1,0:T(8,128)S(1)} %collective-permute-done.4.rows, bf16[128,128]{1,0:T(8,128)(2,1)S(1)} %get-tuple-element.28.mortar_ref, f32[8,128]{1,0:T(8,128)S(1)} %get-tuple-element.29.weight), custom_call_target="tpu_custom_call" | custom-call | flops 268435456 | bytes 1048576 | tf_op jit(solution)/shard_map/pallas_call | solution.py:379
  29.6 11.4 %all-to-all-start.1 = ((bf16[64,8,384]{2,1,0:T(8,128)(2,1)}), bf16[64,8,384]{2,1,0:T(8,128)(2,1)S(1)}, u32[]{:S(2)}, u32[]{:S(2)}) async-start(bf16[64,8,384]{2,1,0:T(8,128)(2,1)} %bitcast.25), calls=%async_computation.1 | async-start | bytes 786432 | tf_op jit(solution)/shard_map/all_to_all | solution.py:298
  41.0 0.1 collective-permute-start.5
  41.1 0.7 %collective-permute-start.2 = (f32[3,16,128]{2,1,0:T(8,128)S(1)}, f32[3,16,128]{2,1,0:T(8,128)S(1)}, u32[]{:S(2)}, u32[]{:S(2)}) collective-permute-start(f32[3,16,128]{2,1,0:T(8,128)S(1)} %get-tuple-element.23), channel_id=1, source_target_pairs={{1,2},{3,4},{5,6},{7,8},{9,10},{11,12},{13,14},{15,16},{17,18},{19... | collective-permute-start | bytes 73736 | tf_op jit(solution)/shard_map/ppermute | solution.py:290
  41.8 4.4 %collective-permute-start.3 = (f32[3,16,128]{2,1,0:T(8,128)S(1)}, f32[3,16,128]{2,1,0:T(8,128)S(1)}, u32[]{:S(2)}, u32[]{:S(2)}) collective-permute-start(f32[3,16,128]{2,1,0:T(8,128)S(1)} %get-tuple-element.24), channel_id=1, source_target_pairs={{0,1},{2,3},{4,5},{6,7},{8,9},{10,11},{12,13},{14,15},{16,17},{18,... | collective-permute-start | bytes 73736 | tf_op jit(solution)/shard_map/ppermute | solution.py:290
  46.2 0.0 collective-permute-done.2.far
  46.2 2.1 %collective-permute-done.3.near = f32[3,16,128]{2,1,0:T(8,128)S(1)} collective-permute-done((f32[3,16,128]{2,1,0:T(8,128)S(1)}, f32[3,16,128]{2,1,0:T(8,128)S(1)}, u32[]{:S(2)}, u32[]{:S(2)}) %collective-permute-start.3) | collective-permute-done | bytes 24608 | tf_op jit(solution)/shard_map/ppermute | solution.py:290
  48.3 0.0 collective-permute-done.5.force
  48.3 0.7 %shard_map.171 = (f32[3,32,128]{2,1,0:T(8,128)}, f32[3,128,128]{2,1,0:T(8,128)}) custom-call(s32[8,128]{1,0:T(8,128)S(1)} %broadcast_in_dim.9.parity, f32[3,32,128]{2,1,0:T(8,128)S(1)} %get-tuple-element.19.own, f32[3,16,128]{2,1,0:T(8,128)S(1)} %collective-permute-done.2.far, f32[3,16,128]{2,1,0:T(8,128)S(1)} %collective-permute-done.3.near, ...), custom_call_target="tpu_custom_call" | custom-call | flops 1048576 | bytes 1048576 | tf_op jit(solution)/shard_map/pallas_call | solution.py:400
  49.0 3.3 %all-to-all-done.1 = bf16[64,8,384]{2,1,0:T(8,128)(2,1)S(1)} async-done(((bf16[64,8,384]{2,1,0:T(8,128)(2,1)}), bf16[64,8,384]{2,1,0:T(8,128)(2,1)S(1)}, u32[]{:S(2)}, u32[]{:S(2)}) %all-to-all-start.1) | async-done | bytes 393248 | tf_op jit(solution)/shard_map/all_to_all | solution.py:298
  52.3 1.1 %shard_map.172 = f32[3,128,128]{2,1,0:T(8,128)} custom-call(bf16[512,384]{1,0:T(8,128)(2,1)S(1)} %bitcast.38, s32[2,128]{1,0:T(2,128)S(1)} %get-tuple-element.33.slots, bf16[128,128]{1,0:T(8,128)(2,1)S(1)} %get-tuple-element.28.mortar_ref), custom_call_target="tpu_custom_call" | custom-call | flops 134217728 | bytes 1048576 | tf_op jit(solution)/shard_map/pallas_call | solution.py:392
  (3 shorter events, 0.1 us)
Async XLA Ops:
  3.4 11.7 %copy-start.3 = (f32[1,3,4096]{2,0,1:T(1,128)S(1)}, f32[1,3,4096]{2,0,1:T(1,128)}, u32[]{:S(2)}) copy-start(f32[1,3,4096]{2,0,1:T(1,128)} %param.15) | copy-start | bytes 147460
  3.4 14.1 %copy-start = (f32[1,128,3,128]{3,1,2,0:T(8,128)S(1)}, f32[1,128,3,128]{3,1,2,0:T(8,128)}, u32[]{:S(2)}) copy-start(f32[1,128,3,128]{3,1,2,0:T(8,128)} %param.26) | copy-start | bytes 589828
  3.4 14.1 %copy-start.2 = (f32[1,128,128]{2,1,0:T(8,128)S(1)}, f32[1,128,128]{2,1,0:T(8,128)}, u32[]{:S(2)}) copy-start(f32[1,128,128]{2,1,0:T(8,128)} %param.25) | copy-start | bytes 196612
  3.4 14.1 %copy-start.4 = (bf16[128,128]{1,0:T(8,128)(2,1)S(1)}, bf16[128,128]{1,0:T(8,128)(2,1)}, u32[]{:S(2)}) copy-start(bf16[128,128]{1,0:T(8,128)(2,1)} %coupling.1) | copy-start | bytes 98308
  3.4 24.9 %all-to-all-start = ((bf16[64,8,512]{2,1,0:T(8,128)(2,1)}), bf16[64,8,512]{2,1,0:T(8,128)(2,1)S(1)}, u32[]{:S(2)}, u32[]{:S(2)}) async-start(bf16[64,8,512]{2,1,0:T(8,128)(2,1)} %bitcast.53), calls=%async_computation | async-start | bytes 1048576 | tf_op jit(solution)/shard_map/all_to_all | solution.py:298
  15.1 2.4 %copy-start.1 = (bf16[1,128,3,128]{3,1,2,0:T(8,128)(2,1)S(1)}, bf16[1,128,3,128]{3,1,2,0:T(8,128)(2,1)}, u32[]{:S(2)}) copy-start(bf16[1,128,3,128]{3,1,2,0:T(8,128)(2,1)} %param.27) | copy-start | bytes 294916
  15.1 5.6 %collective-permute-start.1 = (f32[3,16,128]{2,1,0:T(8,128)S(1)}, f32[3,16,128]{2,1,0:T(8,128)S(1)}, u32[]{:S(2)}, u32[]{:S(2)}) collective-permute-start(f32[3,16,128]{2,1,0:T(8,128)S(1)} %get-tuple-element.41), channel_id=1, source_target_pairs={{0,1},{2,3},{4,5},{6,7},{8,9},{10,11},{12,13},{14,15},{16,17},{18,... | collective-permute-start | bytes 73736 | tf_op jit(solution)/shard_map/ppermute | solution.py:290
  16.8 3.9 %collective-permute-start = (f32[3,16,128]{2,1,0:T(8,128)S(1)}, f32[3,16,128]{2,1,0:T(8,128)S(1)}, u32[]{:S(2)}, u32[]{:S(2)}) collective-permute-start(f32[3,16,128]{2,1,0:T(8,128)S(1)} %get-tuple-element.42), channel_id=1, source_target_pairs={{1,2},{3,4},{5,6},{7,8},{9,10},{11,12},{13,14},{15,16},{17,18},{19... | collective-permute-start | bytes 73736 | tf_op jit(solution)/shard_map/ppermute | solution.py:290
  17.4 0.7 %copy-start.5 = (s32[2,128]{1,0:T(2,128)S(1)}, s32[2,128]{1,0:T(2,128)}, u32[]{:S(2)}) copy-start(s32[2,128]{1,0:T(2,128)} %get-tuple-element.26.slots) | copy-start | bytes 3076
  17.5 0.7 %copy-start.6 = (f32[128]{0:T(128)S(1)}, f32[128]{0:T(128)}, u32[]{:S(2)}) copy-start(f32[128]{0:T(128)} %param.29) | copy-start | bytes 1540
  18.1 0.9 %copy-start.7 = (s32[1,8,4096]{2,1,0:T(8,128)S(1)}, s32[1,8,4096]{2,1,0:T(8,128)}, u32[]{:S(2)}) copy-start(s32[1,8,4096]{2,1,0:T(8,128)} %param.16) | copy-start | bytes 393220
  18.2 10.2 %collective-permute-start.4 = (f32[4,128,128]{2,1,0:T(8,128)S(1)}, f32[4,128,128]{2,1,0:T(8,128)S(1)}, u32[]{:S(2)}, u32[]{:S(2)}) collective-permute-start(f32[4,128,128]{2,1,0:T(8,128)S(1)} %get-tuple-element.27), channel_id=1, source_target_pairs={{0,64},{64,0},{1,65},{65,1},{2,66},{66,2},{3,67},{67,3},{4,68},{68... | collective-permute-start | bytes 786440 | tf_op jit(solution)/shard_map/ppermute | solution.py:294
  19.0 1.7 %copy-start.8 = (f32[1,6,4096]{2,0,1:T(1,128)S(1)}, f32[1,6,4096]{2,0,1:T(1,128)}, u32[]{:S(2)}) copy-start(f32[1,6,4096]{2,0,1:T(1,128)} %param.17) | copy-start | bytes 294916
  19.0 1.7 %copy-start.9 = (f32[1,3,4096]{2,0,1:T(1,128)S(1)}, f32[1,3,4096]{2,0,1:T(1,128)}, u32[]{:S(2)}) copy-start(f32[1,3,4096]{2,0,1:T(1,128)} %param.20) | copy-start | bytes 147460
  19.0 1.7 %copy-start.10 = (f32[1,4096]{1,0:T(1,128)S(1)}, f32[1,4096]{1,0:T(1,128)}, u32[]{:S(2)}) copy-start(f32[1,4096]{1,0:T(1,128)} %param.18) | copy-start | bytes 49156
  19.0 1.7 %copy-start.11 = (f32[1,4096]{1,0:T(1,128)S(1)}, f32[1,4096]{1,0:T(1,128)}, u32[]{:S(2)}) copy-start(f32[1,4096]{1,0:T(1,128)} %param.19) | copy-start | bytes 49156
  29.6 22.7 %all-to-all-start.1 = ((bf16[64,8,384]{2,1,0:T(8,128)(2,1)}), bf16[64,8,384]{2,1,0:T(8,128)(2,1)S(1)}, u32[]{:S(2)}, u32[]{:S(2)}) async-start(bf16[64,8,384]{2,1,0:T(8,128)(2,1)} %bitcast.25), calls=%async_computation.1 | async-start | bytes 786432 | tf_op jit(solution)/shard_map/all_to_all | solution.py:298
  41.0 7.2 %collective-permute-start.5 = (f32[3,128,128]{2,1,0:T(8,128)S(1)}, f32[3,128,128]{2,1,0:T(8,128)S(1)}, u32[]{:S(2)}, u32[]{:S(2)}) collective-permute-start(f32[3,128,128]{2,1,0:T(8,128)S(1)} %get-tuple-element.30), channel_id=1, source_target_pairs={{0,64},{64,0},{1,65},{65,1},{2,66},{66,2},{3,67},{67,3},{4,68},{68... | collective-permute-start | bytes 589832 | tf_op jit(solution)/shard_map/ppermute | solution.py:294
  41.1 5.0 %collective-permute-start.2 = (f32[3,16,128]{2,1,0:T(8,128)S(1)}, f32[3,16,128]{2,1,0:T(8,128)S(1)}, u32[]{:S(2)}, u32[]{:S(2)}) collective-permute-start(f32[3,16,128]{2,1,0:T(8,128)S(1)} %get-tuple-element.23), channel_id=1, source_target_pairs={{1,2},{3,4},{5,6},{7,8},{9,10},{11,12},{13,14},{15,16},{17,18},{19... | collective-permute-start | bytes 73736 | tf_op jit(solution)/shard_map/ppermute | solution.py:290
  41.8 6.5 %collective-permute-start.3 = (f32[3,16,128]{2,1,0:T(8,128)S(1)}, f32[3,16,128]{2,1,0:T(8,128)S(1)}, u32[]{:S(2)}, u32[]{:S(2)}) collective-permute-start(f32[3,16,128]{2,1,0:T(8,128)S(1)} %get-tuple-element.24), channel_id=1, source_target_pairs={{0,1},{2,3},{4,5},{6,7},{8,9},{10,11},{12,13},{14,15},{16,17},{18,... | collective-permute-start | bytes 73736 | tf_op jit(solution)/shard_map/ppermute | solution.py:290

commit v8 on v7

--- a/solution.py
+++ b/solution.py
@@ -167,33 +167,28 @@
     out[:, HALO:BLOCKS, :] = own[:, HALO:BLOCKS, :] + jnp.where(odd, far[...], near[...])
 
 
-def pack_kernel(owner, where, active, disp, send, slots, held, sem):
+def pack_kernel(owner, where, active, disp, send, slots):
     names = iota((PEERS, SEG), 0)
     earlier = jnp.where(iota((SEG, SEG), 0) < iota((SEG, SEG), 1), 1.0, 0.0).astype(BF16)
     ones = jnp.ones((SEG, SEG), BF16)
     hot = [owner[k : k + 1, :] == names for k in range(2)]
     hot16 = [jnp.where(h, 1.0, 0.0).astype(BF16) for h in hot]
     before = [dot(hot16[0], earlier), dot(hot16[1], earlier) + dot(hot16[0], ones)]
-    slot, mark = [], []
+    rows = iota((PEERS * SLOTS, SEG), 0)
+    sent = jnp.zeros((PEERS * SLOTS, SEG), F32)
+    meta = jnp.zeros((PEERS * SLOTS, SEG), F32)
     for k in range(2):
         rank = jnp.sum(jnp.where(hot[k], before[k], 0.0), axis=0, keepdims=True)
-        slot.append(owner[k : k + 1, :] * SLOTS + rank.astype(jnp.int32))
-        mark.append(((where[k : k + 1, :] + 1) * active[...]).astype(F32))
-        slots[k : k + 1, :] = slot[k]
-    copies = []
-    for part in range(PEERS * SLOTS // SEG):
-        span = slice(part * SEG, (part + 1) * SEG)
-        rows = iota((SEG, SEG), 0) + part * SEG
-        here = [slot[k] == rows for k in range(2)]
-        sent = jnp.where(here[0] | here[1], 1.0, 0.0).astype(BF16)
-        meta = jnp.where(here[0], mark[0], jnp.where(here[1], mark[1], 0.0)).astype(BF16)
-        for c in range(3):
-            held[span, c * LANES : (c + 1) * LANES] = dot(sent, disp[c]).astype(BF16)
-        held[span, 3 * LANES :] = dot(meta, ones).astype(BF16)
-        copies.append(pltpu.make_async_copy(held.at[span], send.at[span], sem.at[part]))
-        copies[-1].start()
-    for copy in copies:
-        copy.wait()
+        slot = owner[k : k + 1, :] * SLOTS + rank.astype(jnp.int32)
+        slots[k : k + 1, :] = slot
+        mark = ((where[k : k + 1, :] + 1) * active[...]).astype(F32)
+        here = slot == rows
+        sent = jnp.where(here, 1.0, sent)
+        meta = jnp.where(here, mark, meta)
+    sent = sent.astype(BF16)
+    for c in range(3):
+        send[:, c * LANES : (c + 1) * LANES] = dot(sent, disp[c]).astype(BF16)
+    send[:, 3 * LANES :] = dot(meta.astype(BF16), ones).astype(BF16)
 
 
 def rows_kernel(gap, normal, mdisp, coupling, quad_weight, slots, rows, mortar, weight, slots_out):
@@ -321,9 +316,8 @@
         -4,
         (shape(PEERS * SLOTS, 4 * LANES, dtype=BF16), shape(2, SEG, dtype=jnp.int32)),
         1 << 27,
-        (pltpu.VMEM((PEERS * SLOTS, 4 * LANES), BF16), pltpu.SemaphoreType.DMA((4,))),
         grant=60 << 20,
-        places=(HBM, pl.BlockSpec()),
+        places=(pl.BlockSpec(), pl.BlockSpec()),
     )(pair_owner[0].T, pair_local[0].T, active, seg_major(slave_disp))
     got = exchanged(send)
 

time: 53.7 us -> 53.2 us (level)
  no operation moved by 1% of the time
where the time goes in v8:
time: 53.2 us; the launch traced here: 52.9 us
  starting transfers between devices  30.6 us (58%)
  Pallas kernels  11 us (21%)
  waiting for transfers between devices  9.01 us (17%)
  local copies, waits for them, and re-layouts  1.44 us (3%)
  between operations  0.85 us (2%)
    all_to_all x2, starting transfers between devices, exchanged(): return lax.all_to_all(block, 'dom', split_axis=0, concat_axis=0, tiled=True)  23.1 us
    ppermute x4, starting transfers between devices, paired(): return lax.ppermute(block, 'dom', route + [(j, i) for i, j in route])  7.32 us
    all_to_all x2, waiting for transfers between devices, exchanged(): return lax.all_to_all(block, 'dom', split_axis=0, concat_axis=0, tiled=True)  6.89 us
    pallas_call x1, Pallas kernels, local(): call(element_kernel, 10, (shape(3, HALO, LANES), shape(3, HALO, LANES), s...  3.95 us
    pallas_call x1, Pallas kernels, local(): call(pack_kernel, -4, (shape(PEERS * SLOTS, 4 * LANES, dtype=BF16), shape...  2.28 us
    ppermute x4, waiting for transfers between devices, paired(): return lax.ppermute(block, 'dom', route + [(j, i) for i, j in route])  2.12 us
    pallas_call x1, Pallas kernels, local(): call(gather_kernel, 2, shape(3, 8 * BLOCKS, LANES), 1 << 30, (pltpu.VMEM(...  1.67 us
    unnamed x24, local copies, waits for them, and re-layouts  1.44 us
  transfers between devices with their start and end apart: 8, of which 3 were waited for; matrix products, arithmetic and copies ran while one was open for 0% of the time, Pallas kernels for 12%

profile of v8, /device:TPU:0, one launch (start us, length us, event | category | flops | bytes accessed | tf_op | source)
XLA Modules:
  0.0 52.9 jit_solution(8433290062371104668)
XLA Ops:
  0.6 2.3 %shard_map.168 = (bf16[512,512]{1,0:T(8,128)(2,1)}, s32[2,128]{1,0:T(2,128)}) custom-call(s32[2,128]{1,0:T(2,128)} %bitcast.58, s32[2,128]{1,0:T(2,128)} %bitcast.59, s32[1,128]{1,0:T(1,128)} %active.1, bf16[3,128,128]{2,1,0:T(8,128)(2,1)} %bitcast.56), custom_call_target="tpu_custom_call" | custom-call | flops 134217728 | bytes 1048576 | tf_op jit(solution)/shard_map/pallas_call | solution.py:314
  2.9 0.0 copy-start.3
  2.9 0.0 copy-start
  2.9 0.0 copy-start.2
  2.9 0.0 copy-start.4
  2.9 11.7 %all-to-all-start = ((bf16[64,8,512]{2,1,0:T(8,128)(2,1)}), bf16[64,8,512]{2,1,0:T(8,128)(2,1)S(1)}, u32[]{:S(2)}, u32[]{:S(2)}) async-start(bf16[64,8,512]{2,1,0:T(8,128)(2,1)} %bitcast.53), calls=%async_computation | async-start | bytes 1048576 | tf_op jit(solution)/shard_map/all_to_all | solution.py:293
  14.6 0.0 copy-start.1
  14.6 0.0 copy-done.3
  14.7 1.6 %collective-permute-start.1 = (f32[3,16,128]{2,1,0:T(8,128)S(1)}, f32[3,16,128]{2,1,0:T(8,128)S(1)}, u32[]{:S(2)}, u32[]{:S(2)}) collective-permute-start(f32[3,16,128]{2,1,0:T(8,128)S(1)} %get-tuple-element.41), channel_id=1, source_target_pairs={{0,1},{2,3},{4,5},{6,7},{8,9},{10,11},{12,13},{14,15},{16,17},{18,... | collective-permute-start | bytes 73736 | tf_op jit(solution)/shard_map/ppermute | solution.py:285
  16.3 0.7 %collective-permute-start = (f32[3,16,128]{2,1,0:T(8,128)S(1)}, f32[3,16,128]{2,1,0:T(8,128)S(1)}, u32[]{:S(2)}, u32[]{:S(2)}) collective-permute-start(f32[3,16,128]{2,1,0:T(8,128)S(1)} %get-tuple-element.42), channel_id=1, source_target_pairs={{1,2},{3,4},{5,6},{7,8},{9,10},{11,12},{13,14},{15,16},{17,18},{19... | collective-permute-start | bytes 73736 | tf_op jit(solution)/shard_map/ppermute | solution.py:285
  17.0 0.0 copy-start.5
  17.0 0.0 copy-start.6
  17.0 0.0 copy-done
  17.0 0.0 copy-done.2
  17.0 0.0 copy-done.4
  17.0 0.0 copy-done.1
  17.0 0.6 %copy-done.5 = s32[2,128]{1,0:T(2,128)S(1)} copy-done((s32[2,128]{1,0:T(2,128)S(1)}, s32[2,128]{1,0:T(2,128)}, u32[]{:S(2)}) %copy-start.5) | copy-done | bytes 1048
  17.7 0.0 copy-done.6
  17.7 0.0 copy-start.7
  17.7 0.1 collective-permute-start.4
  17.8 0.8 %copy-done.7 = s32[1,8,4096]{2,1,0:T(8,128)S(1)} copy-done((s32[1,8,4096]{2,1,0:T(8,128)S(1)}, s32[1,8,4096]{2,1,0:T(8,128)}, u32[]{:S(2)}) %copy-start.7) | copy-done | bytes 131096
  18.6 0.0 copy-start.8
  18.6 0.0 copy-start.9
  18.6 0.0 copy-start.10
  18.6 0.0 copy-start.11
  18.6 1.7 %shard_map.166.part = f32[3,256,128]{2,1,0:T(8,128)S(1)} custom-call(f32[3,32,128]{2,1,0:T(8,128)S(1)} %bitcast.44, s32[256,128]{1,0:T(8,128)S(1)} %bitcast.47), custom_call_target="tpu_custom_call" | custom-call | flops 1073741824 | bytes 1048576 | tf_op jit(solution)/shard_map/pallas_call | solution.py:343
  20.2 0.0 collective-permute-done.1.near
  20.3 0.0 collective-permute-done.far
  20.3 0.0 copy-done.8
  20.3 0.0 copy-done.9
  20.3 0.0 copy-done.10
  20.3 0.0 copy-done.11
  20.3 3.9 %shard_map.167 = (f32[3,16,128]{2,1,0:T(8,128)S(1)}, f32[3,16,128]{2,1,0:T(8,128)S(1)}, f32[3,32,128]{2,1,0:T(8,128)S(1)}) custom-call(s32[8,128]{1,0:T(8,128)S(1)} %broadcast_in_dim.9.parity, f32[3,16,128]{2,1,0:T(8,128)S(1)} %collective-permute-done.far, f32[3,16,128]{2,1,0:T(8,128)S(1)} %collective-permute-done.1.near, f32[3,32,128]{2,1,0:T(8,128)S(1)} %bitcast.45, ...), custom_call_target="tpu_custom_call" | custom-call | flops 4294967296 | bytes 1048576 | tf_op jit(solution)/shard_map/pallas_call | solution.py:346
  24.3 3.6 %all-to-all-done = bf16[64,8,512]{2,1,0:T(8,128)(2,1)S(1)} async-done(((bf16[64,8,512]{2,1,0:T(8,128)(2,1)}), bf16[64,8,512]{2,1,0:T(8,128)(2,1)S(1)}, u32[]{:S(2)}, u32[]{:S(2)}) %all-to-all-start) | async-done | bytes 524320 | tf_op jit(solution)/shard_map/all_to_all | solution.py:293
  27.9 0.0 collective-permute-done.4.rows
  27.9 1.2 %shard_map.170 = (bf16[512,384]{1,0:T(8,128)(2,1)}, f32[3,128,128]{2,1,0:T(8,128)S(1)}) custom-call(bf16[512,512]{1,0:T(8,128)(2,1)S(1)} %bitcast.39, f32[4,128,128]{2,1,0:T(8,128)S(1)} %collective-permute-done.4.rows, bf16[128,128]{1,0:T(8,128)(2,1)S(1)} %get-tuple-element.28.mortar_ref, f32[8,128]{1,0:T(8,128)S(1)} %get-tuple-element.29.weight), custom_call_target="tpu_custom_call" | custom-call | flops 268435456 | bytes 1048576 | tf_op jit(solution)/shard_map/pallas_call | solution.py:373
  29.1 11.4 %all-to-all-start.1 = ((bf16[64,8,384]{2,1,0:T(8,128)(2,1)}), bf16[64,8,384]{2,1,0:T(8,128)(2,1)S(1)}, u32[]{:S(2)}, u32[]{:S(2)}) async-start(bf16[64,8,384]{2,1,0:T(8,128)(2,1)} %bitcast.25), calls=%async_computation.1 | async-start | bytes 786432 | tf_op jit(solution)/shard_map/all_to_all | solution.py:293
  40.6 0.1 collective-permute-start.5
  40.7 0.7 %collective-permute-start.2 = (f32[3,16,128]{2,1,0:T(8,128)S(1)}, f32[3,16,128]{2,1,0:T(8,128)S(1)}, u32[]{:S(2)}, u32[]{:S(2)}) collective-permute-start(f32[3,16,128]{2,1,0:T(8,128)S(1)} %get-tuple-element.23), channel_id=1, source_target_pairs={{1,2},{3,4},{5,6},{7,8},{9,10},{11,12},{13,14},{15,16},{17,18},{19... | collective-permute-start | bytes 73736 | tf_op jit(solution)/shard_map/ppermute | solution.py:285
  41.3 4.4 %collective-permute-start.3 = (f32[3,16,128]{2,1,0:T(8,128)S(1)}, f32[3,16,128]{2,1,0:T(8,128)S(1)}, u32[]{:S(2)}, u32[]{:S(2)}) collective-permute-start(f32[3,16,128]{2,1,0:T(8,128)S(1)} %get-tuple-element.24), channel_id=1, source_target_pairs={{0,1},{2,3},{4,5},{6,7},{8,9},{10,11},{12,13},{14,15},{16,17},{18,... | collective-permute-start | bytes 73736 | tf_op jit(solution)/shard_map/ppermute | solution.py:285
  45.7 0.0 collective-permute-done.2.far
  45.7 2.1 %collective-permute-done.3.near = f32[3,16,128]{2,1,0:T(8,128)S(1)} collective-permute-done((f32[3,16,128]{2,1,0:T(8,128)S(1)}, f32[3,16,128]{2,1,0:T(8,128)S(1)}, u32[]{:S(2)}, u32[]{:S(2)}) %collective-permute-start.3) | collective-permute-done | bytes 24608 | tf_op jit(solution)/shard_map/ppermute | solution.py:285
  47.8 0.0 collective-permute-done.5.force
  47.8 0.7 %shard_map.171 = (f32[3,32,128]{2,1,0:T(8,128)}, f32[3,128,128]{2,1,0:T(8,128)}) custom-call(s32[8,128]{1,0:T(8,128)S(1)} %broadcast_in_dim.9.parity, f32[3,32,128]{2,1,0:T(8,128)S(1)} %get-tuple-element.19.own, f32[3,16,128]{2,1,0:T(8,128)S(1)} %collective-permute-done.2.far, f32[3,16,128]{2,1,0:T(8,128)S(1)} %collective-permute-done.3.near, ...), custom_call_target="tpu_custom_call" | custom-call | flops 1048576 | bytes 1048576 | tf_op jit(solution)/shard_map/pallas_call | solution.py:394
  48.5 3.3 %all-to-all-done.1 = bf16[64,8,384]{2,1,0:T(8,128)(2,1)S(1)} async-done(((bf16[64,8,384]{2,1,0:T(8,128)(2,1)}), bf16[64,8,384]{2,1,0:T(8,128)(2,1)S(1)}, u32[]{:S(2)}, u32[]{:S(2)}) %all-to-all-start.1) | async-done | bytes 393248 | tf_op jit(solution)/shard_map/all_to_all | solution.py:293
  51.8 1.1 %shard_map.172 = f32[3,128,128]{2,1,0:T(8,128)} custom-call(bf16[512,384]{1,0:T(8,128)(2,1)S(1)} %bitcast.38, s32[2,128]{1,0:T(2,128)S(1)} %get-tuple-element.33.slots, bf16[128,128]{1,0:T(8,128)(2,1)S(1)} %get-tuple-element.28.mortar_ref), custom_call_target="tpu_custom_call" | custom-call | flops 134217728 | bytes 1048576 | tf_op jit(solution)/shard_map/pallas_call | solution.py:386
  (3 shorter events, 0.1 us)
Async XLA Ops:
  2.9 11.7 %copy-start.3 = (f32[1,3,4096]{2,0,1:T(1,128)S(1)}, f32[1,3,4096]{2,0,1:T(1,128)}, u32[]{:S(2)}) copy-start(f32[1,3,4096]{2,0,1:T(1,128)} %param.15) | copy-start | bytes 147460
  2.9 14.1 %copy-start = (f32[1,128,3,128]{3,1,2,0:T(8,128)S(1)}, f32[1,128,3,128]{3,1,2,0:T(8,128)}, u32[]{:S(2)}) copy-start(f32[1,128,3,128]{3,1,2,0:T(8,128)} %param.26) | copy-start | bytes 589828
  2.9 14.1 %copy-start.2 = (f32[1,128,128]{2,1,0:T(8,128)S(1)}, f32[1,128,128]{2,1,0:T(8,128)}, u32[]{:S(2)}) copy-start(f32[1,128,128]{2,1,0:T(8,128)} %param.25) | copy-start | bytes 196612
  2.9 14.1 %copy-start.4 = (bf16[128,128]{1,0:T(8,128)(2,1)S(1)}, bf16[128,128]{1,0:T(8,128)(2,1)}, u32[]{:S(2)}) copy-start(bf16[128,128]{1,0:T(8,128)(2,1)} %coupling.1) | copy-start | bytes 98308
  2.9 24.9 %all-to-all-start = ((bf16[64,8,512]{2,1,0:T(8,128)(2,1)}), bf16[64,8,512]{2,1,0:T(8,128)(2,1)S(1)}, u32[]{:S(2)}, u32[]{:S(2)}) async-start(bf16[64,8,512]{2,1,0:T(8,128)(2,1)} %bitcast.53), calls=%async_computation | async-start | bytes 1048576 | tf_op jit(solution)/shard_map/all_to_all | solution.py:293
  14.6 2.4 %copy-start.1 = (bf16[1,128,3,128]{3,1,2,0:T(8,128)(2,1)S(1)}, bf16[1,128,3,128]{3,1,2,0:T(8,128)(2,1)}, u32[]{:S(2)}) copy-start(bf16[1,128,3,128]{3,1,2,0:T(8,128)(2,1)} %param.27) | copy-start | bytes 294916
  14.7 5.6 %collective-permute-start.1 = (f32[3,16,128]{2,1,0:T(8,128)S(1)}, f32[3,16,128]{2,1,0:T(8,128)S(1)}, u32[]{:S(2)}, u32[]{:S(2)}) collective-permute-start(f32[3,16,128]{2,1,0:T(8,128)S(1)} %get-tuple-element.41), channel_id=1, source_target_pairs={{0,1},{2,3},{4,5},{6,7},{8,9},{10,11},{12,13},{14,15},{16,17},{18,... | collective-permute-start | bytes 73736 | tf_op jit(solution)/shard_map/ppermute | solution.py:285
  16.3 3.9 %collective-permute-start = (f32[3,16,128]{2,1,0:T(8,128)S(1)}, f32[3,16,128]{2,1,0:T(8,128)S(1)}, u32[]{:S(2)}, u32[]{:S(2)}) collective-permute-start(f32[3,16,128]{2,1,0:T(8,128)S(1)} %get-tuple-element.42), channel_id=1, source_target_pairs={{1,2},{3,4},{5,6},{7,8},{9,10},{11,12},{13,14},{15,16},{17,18},{19... | collective-permute-start | bytes 73736 | tf_op jit(solution)/shard_map/ppermute | solution.py:285
  17.0 0.7 %copy-start.5 = (s32[2,128]{1,0:T(2,128)S(1)}, s32[2,128]{1,0:T(2,128)}, u32[]{:S(2)}) copy-start(s32[2,128]{1,0:T(2,128)} %get-tuple-element.26.slots) | copy-start | bytes 3076
  17.0 0.7 %copy-start.6 = (f32[128]{0:T(128)S(1)}, f32[128]{0:T(128)}, u32[]{:S(2)}) copy-start(f32[128]{0:T(128)} %param.29) | copy-start | bytes 1540
  17.7 0.9 %copy-start.7 = (s32[1,8,4096]{2,1,0:T(8,128)S(1)}, s32[1,8,4096]{2,1,0:T(8,128)}, u32[]{:S(2)}) copy-start(s32[1,8,4096]{2,1,0:T(8,128)} %param.16) | copy-start | bytes 393220
  17.7 10.2 %collective-permute-start.4 = (f32[4,128,128]{2,1,0:T(8,128)S(1)}, f32[4,128,128]{2,1,0:T(8,128)S(1)}, u32[]{:S(2)}, u32[]{:S(2)}) collective-permute-start(f32[4,128,128]{2,1,0:T(8,128)S(1)} %get-tuple-element.27), channel_id=1, source_target_pairs={{0,64},{64,0},{1,65},{65,1},{2,66},{66,2},{3,67},{67,3},{4,68},{68... | collective-permute-start | bytes 786440 | tf_op jit(solution)/shard_map/ppermute | solution.py:289
  18.6 1.7 %copy-start.8 = (f32[1,6,4096]{2,0,1:T(1,128)S(1)}, f32[1,6,4096]{2,0,1:T(1,128)}, u32[]{:S(2)}) copy-start(f32[1,6,4096]{2,0,1:T(1,128)} %param.17) | copy-start | bytes 294916
  18.6 1.7 %copy-start.9 = (f32[1,3,4096]{2,0,1:T(1,128)S(1)}, f32[1,3,4096]{2,0,1:T(1,128)}, u32[]{:S(2)}) copy-start(f32[1,3,4096]{2,0,1:T(1,128)} %param.20) | copy-start | bytes 147460
  18.6 1.7 %copy-start.10 = (f32[1,4096]{1,0:T(1,128)S(1)}, f32[1,4096]{1,0:T(1,128)}, u32[]{:S(2)}) copy-start(f32[1,4096]{1,0:T(1,128)} %param.18) | copy-start | bytes 49156
  18.6 1.7 %copy-start.11 = (f32[1,4096]{1,0:T(1,128)S(1)}, f32[1,4096]{1,0:T(1,128)}, u32[]{:S(2)}) copy-start(f32[1,4096]{1,0:T(1,128)} %param.19) | copy-start | bytes 49156
  29.1 22.7 %all-to-all-start.1 = ((bf16[64,8,384]{2,1,0:T(8,128)(2,1)}), bf16[64,8,384]{2,1,0:T(8,128)(2,1)S(1)}, u32[]{:S(2)}, u32[]{:S(2)}) async-start(bf16[64,8,384]{2,1,0:T(8,128)(2,1)} %bitcast.25), calls=%async_computation.1 | async-start | bytes 786432 | tf_op jit(solution)/shard_map/all_to_all | solution.py:293
  40.6 7.2 %collective-permute-start.5 = (f32[3,128,128]{2,1,0:T(8,128)S(1)}, f32[3,128,128]{2,1,0:T(8,128)S(1)}, u32[]{:S(2)}, u32[]{:S(2)}) collective-permute-start(f32[3,128,128]{2,1,0:T(8,128)S(1)} %get-tuple-element.30), channel_id=1, source_target_pairs={{0,64},{64,0},{1,65},{65,1},{2,66},{66,2},{3,67},{67,3},{4,68},{68... | collective-permute-start | bytes 589832 | tf_op jit(solution)/shard_map/ppermute | solution.py:289
  40.7 5.0 %collective-permute-start.2 = (f32[3,16,128]{2,1,0:T(8,128)S(1)}, f32[3,16,128]{2,1,0:T(8,128)S(1)}, u32[]{:S(2)}, u32[]{:S(2)}) collective-permute-start(f32[3,16,128]{2,1,0:T(8,128)S(1)} %get-tuple-element.23), channel_id=1, source_target_pairs={{1,2},{3,4},{5,6},{7,8},{9,10},{11,12},{13,14},{15,16},{17,18},{19... | collective-permute-start | bytes 73736 | tf_op jit(solution)/shard_map/ppermute | solution.py:285
  41.3 6.5 %collective-permute-start.3 = (f32[3,16,128]{2,1,0:T(8,128)S(1)}, f32[3,16,128]{2,1,0:T(8,128)S(1)}, u32[]{:S(2)}, u32[]{:S(2)}) collective-permute-start(f32[3,16,128]{2,1,0:T(8,128)S(1)} %get-tuple-element.24), channel_id=1, source_target_pairs={{0,1},{2,3},{4,5},{6,7},{8,9},{10,11},{12,13},{14,15},{16,17},{18,... | collective-permute-start | bytes 73736 | tf_op jit(solution)/shard_map/ppermute | solution.py:285

commit v9 on v8

--- a/solution.py
+++ b/solution.py
@@ -75,9 +75,10 @@
 def element_kernel(parity, far, near, own, links, part, strain, edge_ref, yield_ref, ext, far_out, near_out, own_out,
                    disp, table, lo_s, hi_s, force_s, acc):
     odd = parity[0:1, :] == 1
-    disp[:, 0:HALO, :] = jnp.where(odd, near[...], far[...])
+    near_halo, far_halo = near[...].astype(F32), far[...].astype(F32)
+    disp[:, 0:HALO, :] = jnp.where(odd, near_halo, far_halo)
     disp[:, HALO : HALO + BLOCKS, :] = own[...]
-    disp[:, HALO + BLOCKS : 2 * HALO + BLOCKS, :] = jnp.where(odd, far[...], near[...])
+    disp[:, HALO + BLOCKS : 2 * HALO + BLOCKS, :] = jnp.where(odd, far_halo, near_halo)
     acc[...] = jnp.zeros_like(acc)
     unit = pack_pair(disp[0, : 2 * HALO + BLOCKS], disp[1, : 2 * HALO + BLOCKS], table)
     block = iota((8, LANES), 0) * LANES
@@ -155,16 +156,17 @@
         for i in range(3):
             acc[i, 8 * m : 8 * m + WINDOW, :] += sums[i * WINDOW : (i + 1) * WINDOW]
     low, high = acc[:, 0:HALO, :], acc[:, HALO + BLOCKS : 2 * HALO + BLOCKS, :]
-    far_out[...] = jnp.where(odd, high, low)
-    near_out[...] = jnp.where(odd, low, high)
+    far_out[...] = jnp.where(odd, high, low).astype(BF16)
+    near_out[...] = jnp.where(odd, low, high).astype(BF16)
     own_out[...] = acc[:, HALO : HALO + BLOCKS, :] - ext[...]
 
 
 def finish_kernel(parity, own, far, near, force, out, force_out):
     odd = parity[0:1, :] == 1
     force_out[...] = force[...]
-    out[:, 0:HALO, :] = own[:, 0:HALO, :] + jnp.where(odd, near[...], far[...])
-    out[:, HALO:BLOCKS, :] = own[:, HALO:BLOCKS, :] + jnp.where(odd, far[...], near[...])
+    near_sum, far_sum = near[...].astype(F32), far[...].astype(F32)
+    out[:, 0:HALO, :] = own[:, 0:HALO, :] + jnp.where(odd, near_sum, far_sum)
+    out[:, HALO:BLOCKS, :] = own[:, HALO:BLOCKS, :] + jnp.where(odd, far_sum, near_sum)
 
 
 def pack_kernel(owner, where, active, disp, send, slots):
@@ -191,10 +193,10 @@
     send[:, 3 * LANES :] = dot(meta.astype(BF16), ones).astype(BF16)
 
 
-def rows_kernel(gap, normal, mdisp, coupling, quad_weight, slots, rows, mortar, weight, slots_out):
+def rows_kernel(gap, normal, mdisp, coupling, links, slots, quad_weight, rows, mortar, slots_out, weight):
+    weight[...] = jnp.broadcast_to(quad_weight[...], weight.shape)
     slots_out[...] = slots[...]
     mortar[...] = mortar_of(coupling)
-    weight[...] = jnp.broadcast_to(quad_weight[...], weight.shape)
     total = gap[...]
     for c in range(3):
         n = normal[c]
@@ -325,28 +327,40 @@
     odd = lax.axis_index("dom") & 1
     parity = jnp.full((8, LANES), odd, jnp.int32)
     first, last = own[:, :HALO], own[:, BLOCKS - HALO :]
-    far = paired(jnp.where(odd == 1, last, first), 1)
-    near = paired(jnp.where(odd == 1, first, last), 0)
-    rows, mortar, weight, slots = call(
+    far = paired(jnp.where(odd == 1, last, first).astype(BF16), 1)
+    near = paired(jnp.where(odd == 1, first, last).astype(BF16), 0)
+    links = jnp.transpose(connectivity[0].reshape(8, BLOCKS, LANES), (1, 0, 2)).reshape(8 * BLOCKS, LANES)
+    rows, mortar, slots, weight = call(
         rows_kernel,
-        6,
+        7,
         (
             shape(4, SEG, LANES),
             shape(LANES, LANES, dtype=BF16),
+            shape(2, SEG, dtype=jnp.int32),
             shape(8, LANES),
-            shape(2, SEG, dtype=jnp.int32),
         ),
         1 << 20,
-    )(master_gap[0], seg_major(master_normal), seg_major(master_disp), coupling, quad_weight.reshape(1, LANES), slots)
+    )(
+        master_gap[0],
+        seg_major(master_normal),
+        seg_major(master_disp),
+        coupling,
+        links,
+        slots,
+        quad_weight.reshape(1, LANES),
+    )
     rows = swapped(rows)
-    links = jnp.transpose(connectivity[0].reshape(8, BLOCKS, LANES), (1, 0, 2)).reshape(8 * BLOCKS, LANES)
     part = call(
         gather_kernel, 2, shape(3, 8 * BLOCKS, LANES), 1 << 30, (pltpu.VMEM((BLOCKS, LANES), jnp.int32),)
     )(own, links)
     far_force, near_force, own_force = call(
         element_kernel,
         10,
-        (shape(3, HALO, LANES), shape(3, HALO, LANES), shape(3, BLOCKS, LANES)),
+        (
+            shape(3, HALO, LANES, dtype=BF16),
+            shape(3, HALO, LANES, dtype=BF16),
+            shape(3, BLOCKS, LANES),
+        ),
         1 << 32,
         (
             pltpu.VMEM((3, 2 * HALO + BLOCKS + 8, LANES), F32),

time: 53.2 us -> 53 us (level)
  waiting for transfers between devices: 9.01 us -> 9.79 us
  local copies, waits for them, and re-layouts: 1.44 us -> 0.68 us
    all_to_all x2, waiting for transfers between devices: 6.89 us -> 7.97 us  [exchanged(): return lax.all_to_all(block, 'dom', split_axis=0, concat_axis=0, tiled=True)]
    unnamed x24, local copies, waits for them, and re-layouts: 1.44 us -> 0.67 us
where the time goes in v9:
time: 53 us; the launch traced here: 52.7 us
  starting transfers between devices  30.4 us (57%)
  Pallas kernels  10.9 us (21%)
  waiting for transfers between devices  9.79 us (18%)
  between operations  0.9 us (2%)
  local copies, waits for them, and re-layouts  0.68 us (1%)
    all_to_all x2, starting transfers between devices, exchanged(): return lax.all_to_all(block, 'dom', split_axis=0, concat_axis=0, tiled=True)  22.9 us
    all_to_all x2, waiting for transfers between devices, exchanged(): return lax.all_to_all(block, 'dom', split_axis=0, concat_axis=0, tiled=True)  7.97 us
    ppermute x4, starting transfers between devices, paired(): return lax.ppermute(block, 'dom', route + [(j, i) for i, j in route])  7.32 us
    pallas_call x1, Pallas kernels, local(): call(element_kernel, 10, (shape(3, HALO, LANES, dtype=BF16), shape(3, HAL...  3.9 us
    pallas_call x1, Pallas kernels, local(): call(pack_kernel, -4, (shape(PEERS * SLOTS, 4 * LANES, dtype=BF16), shape...  2.28 us
    ppermute x4, waiting for transfers between devices, paired(): return lax.ppermute(block, 'dom', route + [(j, i) for i, j in route])  1.81 us
    pallas_call x1, Pallas kernels, local(): call(gather_kernel, 2, shape(3, 8 * BLOCKS, LANES), 1 << 30, (pltpu.VMEM(...  1.67 us
    pallas_call x1, Pallas kernels, local(): call(master_kernel, 4, (shape(PEERS * SLOTS, 3 * LANES, dtype=BF16), shap...  1.22 us
  transfers between devices with their start and end apart: 8, of which 3 were waited for; matrix products, arithmetic and copies ran while one was open for 0% of the time, Pallas kernels for 12%

profile of v9, /device:TPU:0, one launch (start us, length us, event | category | flops | bytes accessed | tf_op | source)
XLA Modules:
  0.0 52.7 jit_solution(990904599983580230)
XLA Ops:
  0.6 2.3 %shard_map.168 = (bf16[512,512]{1,0:T(8,128)(2,1)}, s32[2,128]{1,0:T(2,128)}) custom-call(s32[2,128]{1,0:T(2,128)} %bitcast.59, s32[2,128]{1,0:T(2,128)} %bitcast.60, s32[1,128]{1,0:T(1,128)} %active.1, bf16[3,128,128]{2,1,0:T(8,128)(2,1)} %bitcast.57), custom_call_target="tpu_custom_call" | custom-call | flops 134217728 | bytes 1048576 | tf_op jit(solution)/shard_map/pallas_call | solution.py:316
  2.9 0.0 copy-start.5
  2.9 0.0 copy-start
  2.9 0.0 copy-start.1
  2.9 0.0 copy-start.2
  2.9 0.0 copy-start.4
  3.0 11.7 %all-to-all-start = ((bf16[64,8,512]{2,1,0:T(8,128)(2,1)}), bf16[64,8,512]{2,1,0:T(8,128)(2,1)S(1)}, u32[]{:S(2)}, u32[]{:S(2)}) async-start(bf16[64,8,512]{2,1,0:T(8,128)(2,1)} %bitcast.54), calls=%async_computation | async-start | bytes 1048576 | tf_op jit(solution)/shard_map/all_to_all | solution.py:295
  14.6 0.0 copy-start.3
  14.6 0.0 copy-done.5
  14.7 1.6 %collective-permute-start.1 = (bf16[3,16,128]{2,1,0:T(8,128)(2,1)S(1)}, bf16[3,16,128]{2,1,0:T(8,128)(2,1)S(1)}, u32[]{:S(2)}, u32[]{:S(2)}) collective-permute-start(bf16[3,16,128]{2,1,0:T(8,128)(2,1)S(1)} %get-tuple-element.41), channel_id=1, source_target_pairs={{0,1},{2,3},{4,5},{6,7},{8,9},{10,11},{12,13},{14,15},{16,17},{18,... | collective-permute-start | bytes 36872 | tf_op jit(solution)/shard_map/ppermute | solution.py:287
  16.3 0.7 %collective-permute-start = (bf16[3,16,128]{2,1,0:T(8,128)(2,1)S(1)}, bf16[3,16,128]{2,1,0:T(8,128)(2,1)S(1)}, u32[]{:S(2)}, u32[]{:S(2)}) collective-permute-start(bf16[3,16,128]{2,1,0:T(8,128)(2,1)S(1)} %get-tuple-element.42), channel_id=1, source_target_pairs={{1,2},{3,4},{5,6},{7,8},{9,10},{11,12},{13,14},{15,16},{17,18},{19... | collective-permute-start | bytes 36872 | tf_op jit(solution)/shard_map/ppermute | solution.py:287
  17.0 0.0 copy-start.6
  17.0 0.0 copy-start.7
  17.0 0.0 copy-done
  17.0 0.0 copy-done.1
  17.0 0.0 copy-done.2
  17.0 0.0 copy-done.4
  17.0 0.0 copy-done.3
  17.1 0.6 %copy-done.6 = s32[2,128]{1,0:T(2,128)S(1)} copy-done((s32[2,128]{1,0:T(2,128)S(1)}, s32[2,128]{1,0:T(2,128)}, u32[]{:S(2)}) %copy-start.6) | copy-done | bytes 1048
  17.7 0.0 copy-done.7
  17.7 0.0 copy-start.8
  17.7 0.0 copy-start.9
  17.7 0.0 copy-start.10
  17.7 0.0 copy-start.11
  17.8 0.1 collective-permute-start.4
  17.8 1.7 %shard_map.166.part = f32[3,256,128]{2,1,0:T(8,128)S(1)} custom-call(f32[3,32,128]{2,1,0:T(8,128)S(1)} %bitcast.47, s32[256,128]{1,0:T(8,128)S(1)} %bitcast.42), custom_call_target="tpu_custom_call" | custom-call | flops 1073741824 | bytes 1048576 | tf_op jit(solution)/shard_map/pallas_call | solution.py:353
  19.5 0.0 collective-permute-done.1.near
  19.5 0.0 collective-permute-done.far
  19.6 0.0 copy-done.8
  19.6 0.0 copy-done.9
  19.6 0.0 copy-done.10
  19.6 0.0 copy-done.11
  19.6 3.9 %shard_map.167 = (bf16[3,16,128]{2,1,0:T(8,128)(2,1)S(1)}, bf16[3,16,128]{2,1,0:T(8,128)(2,1)S(1)}, f32[3,32,128]{2,1,0:T(8,128)S(1)}) custom-call(s32[8,128]{1,0:T(8,128)S(1)} %broadcast_in_dim.9.parity, bf16[3,16,128]{2,1,0:T(8,128)(2,1)S(1)} %collective-permute-done.far, bf16[3,16,128]{2,1,0:T(8,128)(2,1)S(1)} %collective-permute-done.1.near, ...), custom_call_target="tpu_custom_call" | custom-call | flops 4294967296 | bytes 1048576 | tf_op jit(solution)/shard_map/pallas_call | solution.py:356
  23.5 4.4 %all-to-all-done = bf16[64,8,512]{2,1,0:T(8,128)(2,1)S(1)} async-done(((bf16[64,8,512]{2,1,0:T(8,128)(2,1)}), bf16[64,8,512]{2,1,0:T(8,128)(2,1)S(1)}, u32[]{:S(2)}, u32[]{:S(2)}) %all-to-all-start) | async-done | bytes 524320 | tf_op jit(solution)/shard_map/all_to_all | solution.py:295
  27.9 0.0 collective-permute-done.4.rows
  27.9 1.2 %shard_map.170 = (bf16[512,384]{1,0:T(8,128)(2,1)}, f32[3,128,128]{2,1,0:T(8,128)S(1)}) custom-call(bf16[512,512]{1,0:T(8,128)(2,1)S(1)} %bitcast.39, f32[4,128,128]{2,1,0:T(8,128)S(1)} %collective-permute-done.4.rows, bf16[128,128]{1,0:T(8,128)(2,1)S(1)} %get-tuple-element.28.mortar_ref, f32[8,128]{1,0:T(8,128)S(1)} %get-tuple-element.29.weight), custom_call_target="tpu_custom_call" | custom-call | flops 268435456 | bytes 1048576 | tf_op jit(solution)/shard_map/pallas_call | solution.py:387
  29.1 11.2 %all-to-all-start.1 = ((bf16[64,8,384]{2,1,0:T(8,128)(2,1)}), bf16[64,8,384]{2,1,0:T(8,128)(2,1)S(1)}, u32[]{:S(2)}, u32[]{:S(2)}) async-start(bf16[64,8,384]{2,1,0:T(8,128)(2,1)} %bitcast.25), calls=%async_computation.1 | async-start | bytes 786432 | tf_op jit(solution)/shard_map/all_to_all | solution.py:295
  40.4 0.1 collective-permute-start.5
  40.5 0.7 %collective-permute-start.2 = (bf16[3,16,128]{2,1,0:T(8,128)(2,1)S(1)}, bf16[3,16,128]{2,1,0:T(8,128)(2,1)S(1)}, u32[]{:S(2)}, u32[]{:S(2)}) collective-permute-start(bf16[3,16,128]{2,1,0:T(8,128)(2,1)S(1)} %get-tuple-element.23), channel_id=1, source_target_pairs={{1,2},{3,4},{5,6},{7,8},{9,10},{11,12},{13,14},{15,16},{17,18},{19... | collective-permute-start | bytes 36872 | tf_op jit(solution)/shard_map/ppermute | solution.py:287
  41.1 4.4 %collective-permute-start.3 = (bf16[3,16,128]{2,1,0:T(8,128)(2,1)S(1)}, bf16[3,16,128]{2,1,0:T(8,128)(2,1)S(1)}, u32[]{:S(2)}, u32[]{:S(2)}) collective-permute-start(bf16[3,16,128]{2,1,0:T(8,128)(2,1)S(1)} %get-tuple-element.24), channel_id=1, source_target_pairs={{0,1},{2,3},{4,5},{6,7},{8,9},{10,11},{12,13},{14,15},{16,17},{18,... | collective-permute-start | bytes 36872 | tf_op jit(solution)/shard_map/ppermute | solution.py:287
  45.5 0.0 collective-permute-done.2.far
  45.5 1.8 %collective-permute-done.3.near = bf16[3,16,128]{2,1,0:T(8,128)(2,1)S(1)} collective-permute-done((bf16[3,16,128]{2,1,0:T(8,128)(2,1)S(1)}, bf16[3,16,128]{2,1,0:T(8,128)(2,1)S(1)}, u32[]{:S(2)}, u32[]{:S(2)}) %collective-permute-start.3) | collective-permute-done | bytes 12320 | tf_op jit(solution)/shard_map/ppermute | solution.py:287
  47.3 0.0 collective-permute-done.5.force
  47.3 0.7 %shard_map.171 = (f32[3,32,128]{2,1,0:T(8,128)}, f32[3,128,128]{2,1,0:T(8,128)}) custom-call(s32[8,128]{1,0:T(8,128)S(1)} %broadcast_in_dim.9.parity, f32[3,32,128]{2,1,0:T(8,128)S(1)} %get-tuple-element.19.own, bf16[3,16,128]{2,1,0:T(8,128)(2,1)S(1)} %collective-permute-done.2.far, bf16[3,16,128]{2,1,0:T(8,128)(2,1)S(1)} %collective-permute-done.3.near, ...), custom_call_target="tpu_custom_call" | custom-call | flops 1048576 | bytes 1048576 | tf_op jit(solution)/shard_map/pallas_call | solution.py:408
  48.0 3.6 %all-to-all-done.1 = bf16[64,8,384]{2,1,0:T(8,128)(2,1)S(1)} async-done(((bf16[64,8,384]{2,1,0:T(8,128)(2,1)}), bf16[64,8,384]{2,1,0:T(8,128)(2,1)S(1)}, u32[]{:S(2)}, u32[]{:S(2)}) %all-to-all-start.1) | async-done | bytes 393248 | tf_op jit(solution)/shard_map/all_to_all | solution.py:295
  51.6 1.1 %shard_map.172 = f32[3,128,128]{2,1,0:T(8,128)} custom-call(bf16[512,384]{1,0:T(8,128)(2,1)S(1)} %bitcast.38, s32[2,128]{1,0:T(2,128)S(1)} %get-tuple-element.33.slots, bf16[128,128]{1,0:T(8,128)(2,1)S(1)} %get-tuple-element.28.mortar_ref), custom_call_target="tpu_custom_call" | custom-call | flops 134217728 | bytes 1048576 | tf_op jit(solution)/shard_map/pallas_call | solution.py:400
  (3 shorter events, 0.1 us)
Async XLA Ops:
  2.9 11.7 %copy-start.5 = (f32[1,3,4096]{2,0,1:T(1,128)S(1)}, f32[1,3,4096]{2,0,1:T(1,128)}, u32[]{:S(2)}) copy-start(f32[1,3,4096]{2,0,1:T(1,128)} %param.15) | copy-start | bytes 147460
  2.9 14.1 %copy-start = (f32[1,128,3,128]{3,1,2,0:T(8,128)S(1)}, f32[1,128,3,128]{3,1,2,0:T(8,128)}, u32[]{:S(2)}) copy-start(f32[1,128,3,128]{3,1,2,0:T(8,128)} %param.26) | copy-start | bytes 589828
  2.9 14.1 %copy-start.1 = (s32[1,8,4096]{2,1,0:T(8,128)S(1)}, s32[1,8,4096]{2,1,0:T(8,128)}, u32[]{:S(2)}) copy-start(s32[1,8,4096]{2,1,0:T(8,128)} %param.16) | copy-start | bytes 393220
  2.9 14.1 %copy-start.2 = (bf16[1,128,3,128]{3,1,2,0:T(8,128)(2,1)S(1)}, bf16[1,128,3,128]{3,1,2,0:T(8,128)(2,1)}, u32[]{:S(2)}) copy-start(bf16[1,128,3,128]{3,1,2,0:T(8,128)(2,1)} %param.27) | copy-start | bytes 294916
  2.9 14.1 %copy-start.4 = (bf16[128,128]{1,0:T(8,128)(2,1)S(1)}, bf16[128,128]{1,0:T(8,128)(2,1)}, u32[]{:S(2)}) copy-start(bf16[128,128]{1,0:T(8,128)(2,1)} %coupling.1) | copy-start | bytes 98308
  3.0 24.9 %all-to-all-start = ((bf16[64,8,512]{2,1,0:T(8,128)(2,1)}), bf16[64,8,512]{2,1,0:T(8,128)(2,1)S(1)}, u32[]{:S(2)}, u32[]{:S(2)}) async-start(bf16[64,8,512]{2,1,0:T(8,128)(2,1)} %bitcast.54), calls=%async_computation | async-start | bytes 1048576 | tf_op jit(solution)/shard_map/all_to_all | solution.py:295
  14.6 2.4 %copy-start.3 = (f32[1,128,128]{2,1,0:T(8,128)S(1)}, f32[1,128,128]{2,1,0:T(8,128)}, u32[]{:S(2)}) copy-start(f32[1,128,128]{2,1,0:T(8,128)} %param.25) | copy-start | bytes 196612
  14.7 4.9 %collective-permute-start.1 = (bf16[3,16,128]{2,1,0:T(8,128)(2,1)S(1)}, bf16[3,16,128]{2,1,0:T(8,128)(2,1)S(1)}, u32[]{:S(2)}, u32[]{:S(2)}) collective-permute-start(bf16[3,16,128]{2,1,0:T(8,128)(2,1)S(1)} %get-tuple-element.41), channel_id=1, source_target_pairs={{0,1},{2,3},{4,5},{6,7},{8,9},{10,11},{12,13},{14,15},{16,17},{18,... | collective-permute-start | bytes 36872 | tf_op jit(solution)/shard_map/ppermute | solution.py:287
  16.3 3.2 %collective-permute-start = (bf16[3,16,128]{2,1,0:T(8,128)(2,1)S(1)}, bf16[3,16,128]{2,1,0:T(8,128)(2,1)S(1)}, u32[]{:S(2)}, u32[]{:S(2)}) collective-permute-start(bf16[3,16,128]{2,1,0:T(8,128)(2,1)S(1)} %get-tuple-element.42), channel_id=1, source_target_pairs={{1,2},{3,4},{5,6},{7,8},{9,10},{11,12},{13,14},{15,16},{17,18},{19... | collective-permute-start | bytes 36872 | tf_op jit(solution)/shard_map/ppermute | solution.py:287
  17.0 0.7 %copy-start.6 = (s32[2,128]{1,0:T(2,128)S(1)}, s32[2,128]{1,0:T(2,128)}, u32[]{:S(2)}) copy-start(s32[2,128]{1,0:T(2,128)} %get-tuple-element.26.slots) | copy-start | bytes 3076
  17.0 0.7 %copy-start.7 = (f32[128]{0:T(128)S(1)}, f32[128]{0:T(128)}, u32[]{:S(2)}) copy-start(f32[128]{0:T(128)} %param.29) | copy-start | bytes 1540
  17.7 1.9 %copy-start.8 = (f32[1,6,4096]{2,0,1:T(1,128)S(1)}, f32[1,6,4096]{2,0,1:T(1,128)}, u32[]{:S(2)}) copy-start(f32[1,6,4096]{2,0,1:T(1,128)} %param.17) | copy-start | bytes 294916
  17.7 1.9 %copy-start.9 = (f32[1,3,4096]{2,0,1:T(1,128)S(1)}, f32[1,3,4096]{2,0,1:T(1,128)}, u32[]{:S(2)}) copy-start(f32[1,3,4096]{2,0,1:T(1,128)} %param.20) | copy-start | bytes 147460
  17.7 1.8 %copy-start.10 = (f32[1,4096]{1,0:T(1,128)S(1)}, f32[1,4096]{1,0:T(1,128)}, u32[]{:S(2)}) copy-start(f32[1,4096]{1,0:T(1,128)} %param.18) | copy-start | bytes 49156
  17.7 1.8 %copy-start.11 = (f32[1,4096]{1,0:T(1,128)S(1)}, f32[1,4096]{1,0:T(1,128)}, u32[]{:S(2)}) copy-start(f32[1,4096]{1,0:T(1,128)} %param.19) | copy-start | bytes 49156
  17.8 10.1 %collective-permute-start.4 = (f32[4,128,128]{2,1,0:T(8,128)S(1)}, f32[4,128,128]{2,1,0:T(8,128)S(1)}, u32[]{:S(2)}, u32[]{:S(2)}) collective-permute-start(f32[4,128,128]{2,1,0:T(8,128)S(1)} %get-tuple-element.27), channel_id=1, source_target_pairs={{0,64},{64,0},{1,65},{65,1},{2,66},{66,2},{3,67},{67,3},{4,68},{68... | collective-permute-start | bytes 786440 | tf_op jit(solution)/shard_map/ppermute | solution.py:291
  29.1 22.5 %all-to-all-start.1 = ((bf16[64,8,384]{2,1,0:T(8,128)(2,1)}), bf16[64,8,384]{2,1,0:T(8,128)(2,1)S(1)}, u32[]{:S(2)}, u32[]{:S(2)}) async-start(bf16[64,8,384]{2,1,0:T(8,128)(2,1)} %bitcast.25), calls=%async_computation.1 | async-start | bytes 786432 | tf_op jit(solution)/shard_map/all_to_all | solution.py:295
  40.4 6.9 %collective-permute-start.5 = (f32[3,128,128]{2,1,0:T(8,128)S(1)}, f32[3,128,128]{2,1,0:T(8,128)S(1)}, u32[]{:S(2)}, u32[]{:S(2)}) collective-permute-start(f32[3,128,128]{2,1,0:T(8,128)S(1)} %get-tuple-element.30), channel_id=1, source_target_pairs={{0,64},{64,0},{1,65},{65,1},{2,66},{66,2},{3,67},{67,3},{4,68},{68... | collective-permute-start | bytes 589832 | tf_op jit(solution)/shard_map/ppermute | solution.py:291
  40.5 5.0 %collective-permute-start.2 = (bf16[3,16,128]{2,1,0:T(8,128)(2,1)S(1)}, bf16[3,16,128]{2,1,0:T(8,128)(2,1)S(1)}, u32[]{:S(2)}, u32[]{:S(2)}) collective-permute-start(bf16[3,16,128]{2,1,0:T(8,128)(2,1)S(1)} %get-tuple-element.23), channel_id=1, source_target_pairs={{1,2},{3,4},{5,6},{7,8},{9,10},{11,12},{13,14},{15,16},{17,18},{19... | collective-permute-start | bytes 36872 | tf_op jit(solution)/shard_map/ppermute | solution.py:287
  41.1 6.2 %collective-permute-start.3 = (bf16[3,16,128]{2,1,0:T(8,128)(2,1)S(1)}, bf16[3,16,128]{2,1,0:T(8,128)(2,1)S(1)}, u32[]{:S(2)}, u32[]{:S(2)}) collective-permute-start(bf16[3,16,128]{2,1,0:T(8,128)(2,1)S(1)} %get-tuple-element.24), channel_id=1, source_target_pairs={{0,1},{2,3},{4,5},{6,7},{8,9},{10,11},{12,13},{14,15},{16,17},{18,... | collective-permute-start | bytes 36872 | tf_op jit(solution)/shard_map/ppermute | solution.py:287

commit v10 on v9

--- a/solution.py
+++ b/solution.py
@@ -169,14 +169,21 @@
     out[:, HALO:BLOCKS, :] = own[:, HALO:BLOCKS, :] + jnp.where(odd, far_sum, near_sum)
 
 
-def pack_kernel(owner, where, active, disp, send, slots):
+def pack_kernel(owner_hbm, where_hbm, active_hbm, disp_hbm, send, slots, owner, where, active, disp, sem):
+    ends = ((owner_hbm, owner), (where_hbm, where), (active_hbm, active), (disp_hbm, disp))
+    copies = [pltpu.make_async_copy(source, target, sem.at[n]) for n, (source, target) in enumerate(ends)]
+    for copy in copies:
+        copy.start()
     names = iota((PEERS, SEG), 0)
     earlier = jnp.where(iota((SEG, SEG), 0) < iota((SEG, SEG), 1), 1.0, 0.0).astype(BF16)
     ones = jnp.ones((SEG, SEG), BF16)
+    copies[0].wait()
     hot = [owner[k : k + 1, :] == names for k in range(2)]
     hot16 = [jnp.where(h, 1.0, 0.0).astype(BF16) for h in hot]
     before = [dot(hot16[0], earlier), dot(hot16[1], earlier) + dot(hot16[0], ones)]
     rows = iota((PEERS * SLOTS, SEG), 0)
+    copies[1].wait()
+    copies[2].wait()
     sent = jnp.zeros((PEERS * SLOTS, SEG), F32)
     meta = jnp.zeros((PEERS * SLOTS, SEG), F32)
     for k in range(2):
@@ -188,6 +195,7 @@
         sent = jnp.where(here, 1.0, sent)
         meta = jnp.where(here, mark, meta)
     sent = sent.astype(BF16)
+    copies[3].wait()
     for c in range(3):
         send[:, c * LANES : (c + 1) * LANES] = dot(sent, disp[c]).astype(BF16)
     send[:, 3 * LANES :] = dot(meta.astype(BF16), ones).astype(BF16)
@@ -274,7 +282,7 @@
     return pl.pallas_call(
         kernel,
         out_shape=outs,
-        in_specs=[VMEM] * ins if ins > 0 else [pl.BlockSpec()] * -ins,
+        in_specs=[VMEM] * ins if ins > 0 else [HBM] * -ins,
         out_specs=jax.tree.map(lambda _: VMEM, outs) if places is None else places,
         scratch_shapes=scratch,
         compiler_params=pltpu.CompilerParams(vmem_limit_bytes=grant),
@@ -318,6 +326,13 @@
         -4,
         (shape(PEERS * SLOTS, 4 * LANES, dtype=BF16), shape(2, SEG, dtype=jnp.int32)),
         1 << 27,
+        (
+            pltpu.VMEM((2, SEG), jnp.int32),
+            pltpu.VMEM((2, SEG), jnp.int32),
+            pltpu.VMEM((1, SEG), jnp.int32),
+            pltpu.VMEM((3, SEG, LANES), BF16),
+            pltpu.SemaphoreType.DMA((4,)),
+        ),
         grant=60 << 20,
         places=(pl.BlockSpec(), pl.BlockSpec()),
     )(pair_owner[0].T, pair_local[0].T, active, seg_major(slave_disp))

time: 53 us -> 52.9 us (level)
  no operation moved by 1% of the time
where the time goes in v10:
time: 52.9 us; the launch traced here: 52.6 us
  starting transfers between devices  30.4 us (57%)
  Pallas kernels  10.8 us (20%)
  waiting for transfers between devices  9.8 us (19%)
  between operations  0.92 us (2%)
  local copies, waits for them, and re-layouts  0.69 us (1%)
    all_to_all x2, starting transfers between devices, exchanged(): return lax.all_to_all(block, 'dom', split_axis=0, concat_axis=0, tiled=True)  22.9 us
    all_to_all x2, waiting for transfers between devices, exchanged(): return lax.all_to_all(block, 'dom', split_axis=0, concat_axis=0, tiled=True)  7.98 us
    ppermute x4, starting transfers between devices, paired(): return lax.ppermute(block, 'dom', route + [(j, i) for i, j in route])  7.32 us
    pallas_call x1, Pallas kernels, local(): call(element_kernel, 10, (shape(3, HALO, LANES, dtype=BF16), shape(3, HAL...  3.9 us
    pallas_call x1, Pallas kernels, local(): call(pack_kernel, -4, (shape(PEERS * SLOTS, 4 * LANES, dtype=BF16), shape...  2.14 us
    ppermute x4, waiting for transfers between devices, paired(): return lax.ppermute(block, 'dom', route + [(j, i) for i, j in route])  1.81 us
    pallas_call x1, Pallas kernels, local(): call(gather_kernel, 2, shape(3, 8 * BLOCKS, LANES), 1 << 30, (pltpu.VMEM(...  1.67 us
    pallas_call x1, Pallas kernels, local(): call(master_kernel, 4, (shape(PEERS * SLOTS, 3 * LANES, dtype=BF16), shap...  1.22 us
  transfers between devices with their start and end apart: 8, of which 3 were waited for; matrix products, arithmetic and copies ran while one was open for 0% of the time, Pallas kernels for 12%

profile of v10, /device:TPU:0, one launch (start us, length us, event | category | flops | bytes accessed | tf_op | source)
XLA Modules:
  0.0 52.6 jit_solution(475470903379794148)
XLA Ops:
  0.6 2.1 %shard_map.168 = (bf16[512,512]{1,0:T(8,128)(2,1)}, s32[2,128]{1,0:T(2,128)}) custom-call(s32[2,128]{1,0:T(2,128)} %bitcast.59, s32[2,128]{1,0:T(2,128)} %bitcast.60, s32[1,128]{1,0:T(1,128)} %active_hbm.1, bf16[3,128,128]{2,1,0:T(8,128)(2,1)} %bitcast.57), custom_call_target="tpu_custom_call" | custom-call | flops 134217728 | bytes 1048576 | tf_op jit(solution)/shard_map/pallas_call | solution.py:324
  2.8 0.0 copy-start.5
  2.8 0.0 copy-start
  2.8 0.0 copy-start.1
  2.8 0.0 copy-start.2
  2.8 0.0 copy-start.4
  2.8 11.7 %all-to-all-start = ((bf16[64,8,512]{2,1,0:T(8,128)(2,1)}), bf16[64,8,512]{2,1,0:T(8,128)(2,1)S(1)}, u32[]{:S(2)}, u32[]{:S(2)}) async-start(bf16[64,8,512]{2,1,0:T(8,128)(2,1)} %bitcast.54), calls=%async_computation | async-start | bytes 1048576 | tf_op jit(solution)/shard_map/all_to_all | solution.py:303
  14.5 0.0 copy-start.3
  14.5 0.0 copy-done.5
  14.6 1.6 %collective-permute-start.1 = (bf16[3,16,128]{2,1,0:T(8,128)(2,1)S(1)}, bf16[3,16,128]{2,1,0:T(8,128)(2,1)S(1)}, u32[]{:S(2)}, u32[]{:S(2)}) collective-permute-start(bf16[3,16,128]{2,1,0:T(8,128)(2,1)S(1)} %get-tuple-element.41), channel_id=1, source_target_pairs={{0,1},{2,3},{4,5},{6,7},{8,9},{10,11},{12,13},{14,15},{16,17},{18,... | collective-permute-start | bytes 36872 | tf_op jit(solution)/shard_map/ppermute | solution.py:295
  16.2 0.7 %collective-permute-start = (bf16[3,16,128]{2,1,0:T(8,128)(2,1)S(1)}, bf16[3,16,128]{2,1,0:T(8,128)(2,1)S(1)}, u32[]{:S(2)}, u32[]{:S(2)}) collective-permute-start(bf16[3,16,128]{2,1,0:T(8,128)(2,1)S(1)} %get-tuple-element.42), channel_id=1, source_target_pairs={{1,2},{3,4},{5,6},{7,8},{9,10},{11,12},{13,14},{15,16},{17,18},{19... | collective-permute-start | bytes 36872 | tf_op jit(solution)/shard_map/ppermute | solution.py:295
  16.9 0.0 copy-start.6
  16.9 0.0 copy-start.7
  16.9 0.0 copy-done
  16.9 0.0 copy-done.1
  16.9 0.0 copy-done.2
  16.9 0.0 copy-done.4
  16.9 0.0 copy-done.3
  16.9 0.6 %copy-done.6 = s32[2,128]{1,0:T(2,128)S(1)} copy-done((s32[2,128]{1,0:T(2,128)S(1)}, s32[2,128]{1,0:T(2,128)}, u32[]{:S(2)}) %copy-start.6) | copy-done | bytes 1048
  17.5 0.0 copy-done.7
  17.6 0.0 copy-start.8
  17.6 0.0 copy-start.9
  17.6 0.0 copy-start.10
  17.6 0.0 copy-start.11
  17.6 0.1 collective-permute-start.4
  17.7 1.7 %shard_map.166.part = f32[3,256,128]{2,1,0:T(8,128)S(1)} custom-call(f32[3,32,128]{2,1,0:T(8,128)S(1)} %bitcast.47, s32[256,128]{1,0:T(8,128)S(1)} %bitcast.42), custom_call_target="tpu_custom_call" | custom-call | flops 1073741824 | bytes 1048576 | tf_op jit(solution)/shard_map/pallas_call | solution.py:368
  19.4 0.0 collective-permute-done.1.near
  19.4 0.0 collective-permute-done.far
  19.4 0.0 copy-done.8
  19.5 0.0 copy-done.9
  19.5 0.0 copy-done.10
  19.5 0.0 copy-done.11
  19.5 3.9 %shard_map.167 = (bf16[3,16,128]{2,1,0:T(8,128)(2,1)S(1)}, bf16[3,16,128]{2,1,0:T(8,128)(2,1)S(1)}, f32[3,32,128]{2,1,0:T(8,128)S(1)}) custom-call(s32[8,128]{1,0:T(8,128)S(1)} %broadcast_in_dim.9.parity, bf16[3,16,128]{2,1,0:T(8,128)(2,1)S(1)} %collective-permute-done.far, bf16[3,16,128]{2,1,0:T(8,128)(2,1)S(1)} %collective-permute-done.1.near, ...), custom_call_target="tpu_custom_call" | custom-call | flops 4294967296 | bytes 1048576 | tf_op jit(solution)/shard_map/pallas_call | solution.py:371
  23.4 4.4 %all-to-all-done = bf16[64,8,512]{2,1,0:T(8,128)(2,1)S(1)} async-done(((bf16[64,8,512]{2,1,0:T(8,128)(2,1)}), bf16[64,8,512]{2,1,0:T(8,128)(2,1)S(1)}, u32[]{:S(2)}, u32[]{:S(2)}) %all-to-all-start) | async-done | bytes 524320 | tf_op jit(solution)/shard_map/all_to_all | solution.py:303
  27.8 0.0 collective-permute-done.4.rows
  27.8 1.2 %shard_map.170 = (bf16[512,384]{1,0:T(8,128)(2,1)}, f32[3,128,128]{2,1,0:T(8,128)S(1)}) custom-call(bf16[512,512]{1,0:T(8,128)(2,1)S(1)} %bitcast.39, f32[4,128,128]{2,1,0:T(8,128)S(1)} %collective-permute-done.4.rows, bf16[128,128]{1,0:T(8,128)(2,1)S(1)} %get-tuple-element.28.mortar_ref, f32[8,128]{1,0:T(8,128)S(1)} %get-tuple-element.29.weight), custom_call_target="tpu_custom_call" | custom-call | flops 268435456 | bytes 1048576 | tf_op jit(solution)/shard_map/pallas_call | solution.py:402
  29.0 11.2 %all-to-all-start.1 = ((bf16[64,8,384]{2,1,0:T(8,128)(2,1)}), bf16[64,8,384]{2,1,0:T(8,128)(2,1)S(1)}, u32[]{:S(2)}, u32[]{:S(2)}) async-start(bf16[64,8,384]{2,1,0:T(8,128)(2,1)} %bitcast.25), calls=%async_computation.1 | async-start | bytes 786432 | tf_op jit(solution)/shard_map/all_to_all | solution.py:303
  40.3 0.1 collective-permute-start.5
  40.4 0.7 %collective-permute-start.2 = (bf16[3,16,128]{2,1,0:T(8,128)(2,1)S(1)}, bf16[3,16,128]{2,1,0:T(8,128)(2,1)S(1)}, u32[]{:S(2)}, u32[]{:S(2)}) collective-permute-start(bf16[3,16,128]{2,1,0:T(8,128)(2,1)S(1)} %get-tuple-element.23), channel_id=1, source_target_pairs={{1,2},{3,4},{5,6},{7,8},{9,10},{11,12},{13,14},{15,16},{17,18},{19... | collective-permute-start | bytes 36872 | tf_op jit(solution)/shard_map/ppermute | solution.py:295
  41.0 4.4 %collective-permute-start.3 = (bf16[3,16,128]{2,1,0:T(8,128)(2,1)S(1)}, bf16[3,16,128]{2,1,0:T(8,128)(2,1)S(1)}, u32[]{:S(2)}, u32[]{:S(2)}) collective-permute-start(bf16[3,16,128]{2,1,0:T(8,128)(2,1)S(1)} %get-tuple-element.24), channel_id=1, source_target_pairs={{0,1},{2,3},{4,5},{6,7},{8,9},{10,11},{12,13},{14,15},{16,17},{18,... | collective-permute-start | bytes 36872 | tf_op jit(solution)/shard_map/ppermute | solution.py:295
  45.4 0.0 collective-permute-done.2.far
  45.4 1.8 %collective-permute-done.3.near = bf16[3,16,128]{2,1,0:T(8,128)(2,1)S(1)} collective-permute-done((bf16[3,16,128]{2,1,0:T(8,128)(2,1)S(1)}, bf16[3,16,128]{2,1,0:T(8,128)(2,1)S(1)}, u32[]{:S(2)}, u32[]{:S(2)}) %collective-permute-start.3) | collective-permute-done | bytes 12320 | tf_op jit(solution)/shard_map/ppermute | solution.py:295
  47.2 0.0 collective-permute-done.5.force
  47.2 0.7 %shard_map.171 = (f32[3,32,128]{2,1,0:T(8,128)}, f32[3,128,128]{2,1,0:T(8,128)}) custom-call(s32[8,128]{1,0:T(8,128)S(1)} %broadcast_in_dim.9.parity, f32[3,32,128]{2,1,0:T(8,128)S(1)} %get-tuple-element.19.own, bf16[3,16,128]{2,1,0:T(8,128)(2,1)S(1)} %collective-permute-done.2.far, bf16[3,16,128]{2,1,0:T(8,128)(2,1)S(1)} %collective-permute-done.3.near, ...), custom_call_target="tpu_custom_call" | custom-call | flops 1048576 | bytes 1048576 | tf_op jit(solution)/shard_map/pallas_call | solution.py:423
  47.9 3.6 %all-to-all-done.1 = bf16[64,8,384]{2,1,0:T(8,128)(2,1)S(1)} async-done(((bf16[64,8,384]{2,1,0:T(8,128)(2,1)}), bf16[64,8,384]{2,1,0:T(8,128)(2,1)S(1)}, u32[]{:S(2)}, u32[]{:S(2)}) %all-to-all-start.1) | async-done | bytes 393248 | tf_op jit(solution)/shard_map/all_to_all | solution.py:303
  51.5 1.1 %shard_map.172 = f32[3,128,128]{2,1,0:T(8,128)} custom-call(bf16[512,384]{1,0:T(8,128)(2,1)S(1)} %bitcast.38, s32[2,128]{1,0:T(2,128)S(1)} %get-tuple-element.33.slots, bf16[128,128]{1,0:T(8,128)(2,1)S(1)} %get-tuple-element.28.mortar_ref), custom_call_target="tpu_custom_call" | custom-call | flops 134217728 | bytes 1048576 | tf_op jit(solution)/shard_map/pallas_call | solution.py:415
  (3 shorter events, 0.1 us)
Async XLA Ops:
  2.8 11.8 %copy-start.5 = (f32[1,3,4096]{2,0,1:T(1,128)S(1)}, f32[1,3,4096]{2,0,1:T(1,128)}, u32[]{:S(2)}) copy-start(f32[1,3,4096]{2,0,1:T(1,128)} %param.15) | copy-start | bytes 147460
  2.8 14.1 %copy-start = (f32[1,128,3,128]{3,1,2,0:T(8,128)S(1)}, f32[1,128,3,128]{3,1,2,0:T(8,128)}, u32[]{:S(2)}) copy-start(f32[1,128,3,128]{3,1,2,0:T(8,128)} %param.26) | copy-start | bytes 589828
  2.8 14.1 %copy-start.1 = (s32[1,8,4096]{2,1,0:T(8,128)S(1)}, s32[1,8,4096]{2,1,0:T(8,128)}, u32[]{:S(2)}) copy-start(s32[1,8,4096]{2,1,0:T(8,128)} %param.16) | copy-start | bytes 393220
  2.8 14.1 %copy-start.2 = (bf16[1,128,3,128]{3,1,2,0:T(8,128)(2,1)S(1)}, bf16[1,128,3,128]{3,1,2,0:T(8,128)(2,1)}, u32[]{:S(2)}) copy-start(bf16[1,128,3,128]{3,1,2,0:T(8,128)(2,1)} %param.27) | copy-start | bytes 294916
  2.8 14.1 %copy-start.4 = (bf16[128,128]{1,0:T(8,128)(2,1)S(1)}, bf16[128,128]{1,0:T(8,128)(2,1)}, u32[]{:S(2)}) copy-start(bf16[128,128]{1,0:T(8,128)(2,1)} %coupling.1) | copy-start | bytes 98308
  2.8 24.9 %all-to-all-start = ((bf16[64,8,512]{2,1,0:T(8,128)(2,1)}), bf16[64,8,512]{2,1,0:T(8,128)(2,1)S(1)}, u32[]{:S(2)}, u32[]{:S(2)}) async-start(bf16[64,8,512]{2,1,0:T(8,128)(2,1)} %bitcast.54), calls=%async_computation | async-start | bytes 1048576 | tf_op jit(solution)/shard_map/all_to_all | solution.py:303
  14.5 2.4 %copy-start.3 = (f32[1,128,128]{2,1,0:T(8,128)S(1)}, f32[1,128,128]{2,1,0:T(8,128)}, u32[]{:S(2)}) copy-start(f32[1,128,128]{2,1,0:T(8,128)} %param.25) | copy-start | bytes 196612
  14.6 4.9 %collective-permute-start.1 = (bf16[3,16,128]{2,1,0:T(8,128)(2,1)S(1)}, bf16[3,16,128]{2,1,0:T(8,128)(2,1)S(1)}, u32[]{:S(2)}, u32[]{:S(2)}) collective-permute-start(bf16[3,16,128]{2,1,0:T(8,128)(2,1)S(1)} %get-tuple-element.41), channel_id=1, source_target_pairs={{0,1},{2,3},{4,5},{6,7},{8,9},{10,11},{12,13},{14,15},{16,17},{18,... | collective-permute-start | bytes 36872 | tf_op jit(solution)/shard_map/ppermute | solution.py:295
  16.2 3.2 %collective-permute-start = (bf16[3,16,128]{2,1,0:T(8,128)(2,1)S(1)}, bf16[3,16,128]{2,1,0:T(8,128)(2,1)S(1)}, u32[]{:S(2)}, u32[]{:S(2)}) collective-permute-start(bf16[3,16,128]{2,1,0:T(8,128)(2,1)S(1)} %get-tuple-element.42), channel_id=1, source_target_pairs={{1,2},{3,4},{5,6},{7,8},{9,10},{11,12},{13,14},{15,16},{17,18},{19... | collective-permute-start | bytes 36872 | tf_op jit(solution)/shard_map/ppermute | solution.py:295
  16.9 0.7 %copy-start.6 = (s32[2,128]{1,0:T(2,128)S(1)}, s32[2,128]{1,0:T(2,128)}, u32[]{:S(2)}) copy-start(s32[2,128]{1,0:T(2,128)} %get-tuple-element.26.slots) | copy-start | bytes 3076
  16.9 0.7 %copy-start.7 = (f32[128]{0:T(128)S(1)}, f32[128]{0:T(128)}, u32[]{:S(2)}) copy-start(f32[128]{0:T(128)} %param.29) | copy-start | bytes 1540
  17.6 1.9 %copy-start.8 = (f32[1,6,4096]{2,0,1:T(1,128)S(1)}, f32[1,6,4096]{2,0,1:T(1,128)}, u32[]{:S(2)}) copy-start(f32[1,6,4096]{2,0,1:T(1,128)} %param.17) | copy-start | bytes 294916
  17.6 1.9 %copy-start.9 = (f32[1,3,4096]{2,0,1:T(1,128)S(1)}, f32[1,3,4096]{2,0,1:T(1,128)}, u32[]{:S(2)}) copy-start(f32[1,3,4096]{2,0,1:T(1,128)} %param.20) | copy-start | bytes 147460
  17.6 1.8 %copy-start.10 = (f32[1,4096]{1,0:T(1,128)S(1)}, f32[1,4096]{1,0:T(1,128)}, u32[]{:S(2)}) copy-start(f32[1,4096]{1,0:T(1,128)} %param.18) | copy-start | bytes 49156
  17.6 1.8 %copy-start.11 = (f32[1,4096]{1,0:T(1,128)S(1)}, f32[1,4096]{1,0:T(1,128)}, u32[]{:S(2)}) copy-start(f32[1,4096]{1,0:T(1,128)} %param.19) | copy-start | bytes 49156
  17.6 10.1 %collective-permute-start.4 = (f32[4,128,128]{2,1,0:T(8,128)S(1)}, f32[4,128,128]{2,1,0:T(8,128)S(1)}, u32[]{:S(2)}, u32[]{:S(2)}) collective-permute-start(f32[4,128,128]{2,1,0:T(8,128)S(1)} %get-tuple-element.27), channel_id=1, source_target_pairs={{0,64},{64,0},{1,65},{65,1},{2,66},{66,2},{3,67},{67,3},{4,68},{68... | collective-permute-start | bytes 786440 | tf_op jit(solution)/shard_map/ppermute | solution.py:299
  29.0 22.5 %all-to-all-start.1 = ((bf16[64,8,384]{2,1,0:T(8,128)(2,1)}), bf16[64,8,384]{2,1,0:T(8,128)(2,1)S(1)}, u32[]{:S(2)}, u32[]{:S(2)}) async-start(bf16[64,8,384]{2,1,0:T(8,128)(2,1)} %bitcast.25), calls=%async_computation.1 | async-start | bytes 786432 | tf_op jit(solution)/shard_map/all_to_all | solution.py:303
  40.3 6.9 %collective-permute-start.5 = (f32[3,128,128]{2,1,0:T(8,128)S(1)}, f32[3,128,128]{2,1,0:T(8,128)S(1)}, u32[]{:S(2)}, u32[]{:S(2)}) collective-permute-start(f32[3,128,128]{2,1,0:T(8,128)S(1)} %get-tuple-element.30), channel_id=1, source_target_pairs={{0,64},{64,0},{1,65},{65,1},{2,66},{66,2},{3,67},{67,3},{4,68},{68... | collective-permute-start | bytes 589832 | tf_op jit(solution)/shard_map/ppermute | solution.py:299
  40.4 5.0 %collective-permute-start.2 = (bf16[3,16,128]{2,1,0:T(8,128)(2,1)S(1)}, bf16[3,16,128]{2,1,0:T(8,128)(2,1)S(1)}, u32[]{:S(2)}, u32[]{:S(2)}) collective-permute-start(bf16[3,16,128]{2,1,0:T(8,128)(2,1)S(1)} %get-tuple-element.23), channel_id=1, source_target_pairs={{1,2},{3,4},{5,6},{7,8},{9,10},{11,12},{13,14},{15,16},{17,18},{19... | collective-permute-start | bytes 36872 | tf_op jit(solution)/shard_map/ppermute | solution.py:295
  41.0 6.2 %collective-permute-start.3 = (bf16[3,16,128]{2,1,0:T(8,128)(2,1)S(1)}, bf16[3,16,128]{2,1,0:T(8,128)(2,1)S(1)}, u32[]{:S(2)}, u32[]{:S(2)}) collective-permute-start(bf16[3,16,128]{2,1,0:T(8,128)(2,1)S(1)} %get-tuple-element.24), channel_id=1, source_target_pairs={{0,1},{2,3},{4,5},{6,7},{8,9},{10,11},{12,13},{14,15},{16,17},{18,... | collective-permute-start | bytes 36872 | tf_op jit(solution)/shard_map/ppermute | solution.py:295

commit v11 on v10

--- a/solution.py
+++ b/solution.py
@@ -13,6 +13,7 @@
 WINDOW = 48
 SLOTS = 8
 PEERS = 64
+STRIDE, INVERSE = 27, 19
 SEG = 128
 F32 = jnp.float32
 BF16 = jnp.bfloat16
@@ -188,7 +189,7 @@
     meta = jnp.zeros((PEERS * SLOTS, SEG), F32)
     for k in range(2):
         rank = jnp.sum(jnp.where(hot[k], before[k], 0.0), axis=0, keepdims=True)
-        slot = owner[k : k + 1, :] * SLOTS + rank.astype(jnp.int32)
+        slot = (owner[k : k + 1, :] * INVERSE & (PEERS - 1)) * SLOTS + rank.astype(jnp.int32)
         slots[k : k + 1, :] = slot
         mark = ((where[k : k + 1, :] + 1) * active[...]).astype(F32)
         here = slot == rows
@@ -300,7 +301,10 @@
 
 
 def exchanged(block):
-    return lax.all_to_all(block, "dom", split_axis=0, concat_axis=0, tiled=True)
+    order = [STRIDE * i % PEERS for i in range(PEERS)]
+    return lax.all_to_all(
+        block, "dom", split_axis=0, concat_axis=0, axis_index_groups=[order], tiled=True
+    )
 
 
 def local(

time: 52.9 us -> 52.6 us (level)
  the two profiles are of different devices: /device:TPU:0 before, /device:TPU:30 now
where the time goes in v11:
time: 52.6 us; the launch traced here: 51.6 us
  starting transfers between devices  29.7 us (56%)
  Pallas kernels  10.8 us (21%)
  waiting for transfers between devices  9.49 us (18%)
  between operations  0.91 us (2%)
  local copies, waits for them, and re-layouts  0.68 us (1%)
    all_to_all x2, starting transfers between devices, exchanged(): lax.all_to_all(block, 'dom', split_axis=0, concat_axis=0, axis_index_grou...  21.2 us
    ppermute x4, waiting for transfers between devices, paired(): return lax.ppermute(block, 'dom', route + [(j, i) for i, j in route])  9.48 us
    ppermute x4, starting transfers between devices, paired(): return lax.ppermute(block, 'dom', route + [(j, i) for i, j in route])  8.41 us
    pallas_call x1, Pallas kernels, local(): call(element_kernel, 10, (shape(3, HALO, LANES, dtype=BF16), shape(3, HAL...  3.9 us
    pallas_call x1, Pallas kernels, local(): call(pack_kernel, -4, (shape(PEERS * SLOTS, 4 * LANES, dtype=BF16), shape...  2.14 us
    pallas_call x1, Pallas kernels, local(): call(gather_kernel, 2, shape(3, 8 * BLOCKS, LANES), 1 << 30, (pltpu.VMEM(...  1.67 us
    pallas_call x1, Pallas kernels, local(): call(master_kernel, 4, (shape(PEERS * SLOTS, 3 * LANES, dtype=BF16), shap...  1.22 us
    pallas_call x1, Pallas kernels, local(): call(slave_kernel, 3, shape(3, SEG, LANES), 1 << 27, (pltpu.VMEM((3, SEG,...  1.08 us
  transfers between devices with their start and end apart: 8, of which 2 were waited for; matrix products, arithmetic and copies ran while one was open for 0% of the time, Pallas kernels for 12%

profile of v11, /device:TPU:30, one launch (start us, length us, event | category | flops | bytes accessed | tf_op | source)
XLA Modules:
  0.0 51.6 jit_solution(14716431044318506195)
XLA Ops:
  0.6 2.1 %shard_map.168 = (bf16[512,512]{1,0:T(8,128)(2,1)}, s32[2,128]{1,0:T(2,128)}) custom-call(s32[2,128]{1,0:T(2,128)} %bitcast.59, s32[2,128]{1,0:T(2,128)} %bitcast.60, s32[1,128]{1,0:T(1,128)} %active_hbm.1, bf16[3,128,128]{2,1,0:T(8,128)(2,1)} %bitcast.57), custom_call_target="tpu_custom_call" | custom-call | flops 134217728 | bytes 1048576 | tf_op jit(solution)/shard_map/pallas_call | solution.py:328
  2.8 0.0 copy-start.5
  2.8 0.0 copy-start
  2.8 0.0 copy-start.1
  2.8 0.0 copy-start.2
  2.8 0.0 copy-start.4
  2.8 11.3 %all-to-all-start = ((bf16[64,8,512]{2,1,0:T(8,128)(2,1)}), bf16[64,8,512]{2,1,0:T(8,128)(2,1)S(1)}, u32[]{:S(2)}, u32[]{:S(2)}) async-start(bf16[64,8,512]{2,1,0:T(8,128)(2,1)} %bitcast.54), calls=%async_computation | async-start | bytes 1048576 | tf_op jit(solution)/shard_map/all_to_all | solution.py:305
  14.2 0.0 copy-start.3
  14.2 0.0 copy-done.5
  14.2 0.9 %collective-permute-start.1 = (bf16[3,16,128]{2,1,0:T(8,128)(2,1)S(1)}, bf16[3,16,128]{2,1,0:T(8,128)(2,1)S(1)}, u32[]{:S(2)}, u32[]{:S(2)}) collective-permute-start(bf16[3,16,128]{2,1,0:T(8,128)(2,1)S(1)} %get-tuple-element.41), channel_id=1, source_target_pairs={{0,1},{2,3},{4,5},{6,7},{8,9},{10,11},{12,13},{14,15},{16,17},{18,... | collective-permute-start | bytes 36872 | tf_op jit(solution)/shard_map/ppermute | solution.py:296
  15.1 4.0 %collective-permute-start = (bf16[3,16,128]{2,1,0:T(8,128)(2,1)S(1)}, bf16[3,16,128]{2,1,0:T(8,128)(2,1)S(1)}, u32[]{:S(2)}, u32[]{:S(2)}) collective-permute-start(bf16[3,16,128]{2,1,0:T(8,128)(2,1)S(1)} %get-tuple-element.42), channel_id=1, source_target_pairs={{1,2},{3,4},{5,6},{7,8},{9,10},{11,12},{13,14},{15,16},{17,18},{19... | collective-permute-start | bytes 36872 | tf_op jit(solution)/shard_map/ppermute | solution.py:296
  19.0 0.0 copy-start.6
  19.0 0.0 copy-start.7
  19.1 0.0 copy-done
  19.1 0.0 copy-done.1
  19.1 0.0 copy-done.2
  19.1 0.0 copy-done.4
  19.1 0.0 copy-done.3
  19.1 0.6 %copy-done.6 = s32[2,128]{1,0:T(2,128)S(1)} copy-done((s32[2,128]{1,0:T(2,128)S(1)}, s32[2,128]{1,0:T(2,128)}, u32[]{:S(2)}) %copy-start.6) | copy-done | bytes 1048
  19.7 0.0 copy-done.7
  19.8 0.0 copy-start.8
  19.8 0.0 copy-start.9
  19.8 0.0 copy-start.10
  19.8 0.0 copy-start.11
  19.8 0.1 collective-permute-start.4
  19.9 1.7 %shard_map.166.part = f32[3,256,128]{2,1,0:T(8,128)S(1)} custom-call(f32[3,32,128]{2,1,0:T(8,128)S(1)} %bitcast.47, s32[256,128]{1,0:T(8,128)S(1)} %bitcast.42), custom_call_target="tpu_custom_call" | custom-call | flops 1073741824 | bytes 1048576 | tf_op jit(solution)/shard_map/pallas_call | solution.py:372
  21.6 0.0 collective-permute-done.1.near
  21.6 3.3 %collective-permute-done.far = bf16[3,16,128]{2,1,0:T(8,128)(2,1)S(1)} collective-permute-done((bf16[3,16,128]{2,1,0:T(8,128)(2,1)S(1)}, bf16[3,16,128]{2,1,0:T(8,128)(2,1)S(1)}, u32[]{:S(2)}, u32[]{:S(2)}) %collective-permute-start) | collective-permute-done | bytes 12320 | tf_op jit(solution)/shard_map/ppermute | solution.py:296
  24.9 0.0 copy-done.8
  24.9 0.0 copy-done.9
  24.9 0.0 copy-done.10
  24.9 0.0 copy-done.11
  24.9 3.9 %shard_map.167 = (bf16[3,16,128]{2,1,0:T(8,128)(2,1)S(1)}, bf16[3,16,128]{2,1,0:T(8,128)(2,1)S(1)}, f32[3,32,128]{2,1,0:T(8,128)S(1)}) custom-call(s32[8,128]{1,0:T(8,128)S(1)} %broadcast_in_dim.9.parity, bf16[3,16,128]{2,1,0:T(8,128)(2,1)S(1)} %collective-permute-done.far, bf16[3,16,128]{2,1,0:T(8,128)(2,1)S(1)} %collective-permute-done.1.near, ...), custom_call_target="tpu_custom_call" | custom-call | flops 4294967296 | bytes 1048576 | tf_op jit(solution)/shard_map/pallas_call | solution.py:375
  28.8 0.0 all-to-all-done
  28.8 0.0 collective-permute-done.4.rows
  28.8 1.2 %shard_map.170 = (bf16[512,384]{1,0:T(8,128)(2,1)}, f32[3,128,128]{2,1,0:T(8,128)S(1)}) custom-call(bf16[512,512]{1,0:T(8,128)(2,1)S(1)} %bitcast.39, f32[4,128,128]{2,1,0:T(8,128)S(1)} %collective-permute-done.4.rows, bf16[128,128]{1,0:T(8,128)(2,1)S(1)} %get-tuple-element.28.mortar_ref, f32[8,128]{1,0:T(8,128)S(1)} %get-tuple-element.29.weight), custom_call_target="tpu_custom_call" | custom-call | flops 268435456 | bytes 1048576 | tf_op jit(solution)/shard_map/pallas_call | solution.py:406
  30.0 9.8 %all-to-all-start.1 = ((bf16[64,8,384]{2,1,0:T(8,128)(2,1)}), bf16[64,8,384]{2,1,0:T(8,128)(2,1)S(1)}, u32[]{:S(2)}, u32[]{:S(2)}) async-start(bf16[64,8,384]{2,1,0:T(8,128)(2,1)} %bitcast.25), calls=%async_computation.1 | async-start | bytes 786432 | tf_op jit(solution)/shard_map/all_to_all | solution.py:305
  39.9 0.1 collective-permute-start.5
  40.0 3.5 %collective-permute-start.2 = (bf16[3,16,128]{2,1,0:T(8,128)(2,1)S(1)}, bf16[3,16,128]{2,1,0:T(8,128)(2,1)S(1)}, u32[]{:S(2)}, u32[]{:S(2)}) collective-permute-start(bf16[3,16,128]{2,1,0:T(8,128)(2,1)S(1)} %get-tuple-element.23), channel_id=1, source_target_pairs={{1,2},{3,4},{5,6},{7,8},{9,10},{11,12},{13,14},{15,16},{17,18},{19... | collective-permute-start | bytes 36872 | tf_op jit(solution)/shard_map/ppermute | solution.py:296
  43.5 0.1 collective-permute-start.3
  43.6 6.2 %collective-permute-done.2.far = bf16[3,16,128]{2,1,0:T(8,128)(2,1)S(1)} collective-permute-done((bf16[3,16,128]{2,1,0:T(8,128)(2,1)S(1)}, bf16[3,16,128]{2,1,0:T(8,128)(2,1)S(1)}, u32[]{:S(2)}, u32[]{:S(2)}) %collective-permute-start.2) | collective-permute-done | bytes 12320 | tf_op jit(solution)/shard_map/ppermute | solution.py:296
  49.8 0.0 collective-permute-done.3.near
  49.8 0.0 collective-permute-done.5.force
  49.8 0.7 %shard_map.171 = (f32[3,32,128]{2,1,0:T(8,128)}, f32[3,128,128]{2,1,0:T(8,128)}) custom-call(s32[8,128]{1,0:T(8,128)S(1)} %broadcast_in_dim.9.parity, f32[3,32,128]{2,1,0:T(8,128)S(1)} %get-tuple-element.19.own, bf16[3,16,128]{2,1,0:T(8,128)(2,1)S(1)} %collective-permute-done.2.far, bf16[3,16,128]{2,1,0:T(8,128)(2,1)S(1)} %collective-permute-done.3.near, ...), custom_call_target="tpu_custom_call" | custom-call | flops 1048576 | bytes 1048576 | tf_op jit(solution)/shard_map/pallas_call | solution.py:427
  50.5 0.0 all-to-all-done.1
  50.5 1.1 %shard_map.172 = f32[3,128,128]{2,1,0:T(8,128)} custom-call(bf16[512,384]{1,0:T(8,128)(2,1)S(1)} %bitcast.38, s32[2,128]{1,0:T(2,128)S(1)} %get-tuple-element.33.slots, bf16[128,128]{1,0:T(8,128)(2,1)S(1)} %get-tuple-element.28.mortar_ref), custom_call_target="tpu_custom_call" | custom-call | flops 134217728 | bytes 1048576 | tf_op jit(solution)/shard_map/pallas_call | solution.py:419
  (3 shorter events, 0.0 us)
Async XLA Ops:
  2.8 11.4 %copy-start.5 = (f32[1,3,4096]{2,0,1:T(1,128)S(1)}, f32[1,3,4096]{2,0,1:T(1,128)}, u32[]{:S(2)}) copy-start(f32[1,3,4096]{2,0,1:T(1,128)} %param.15) | copy-start | bytes 147460
  2.8 16.3 %copy-start = (f32[1,128,3,128]{3,1,2,0:T(8,128)S(1)}, f32[1,128,3,128]{3,1,2,0:T(8,128)}, u32[]{:S(2)}) copy-start(f32[1,128,3,128]{3,1,2,0:T(8,128)} %param.26) | copy-start | bytes 589828
  2.8 16.3 %copy-start.1 = (s32[1,8,4096]{2,1,0:T(8,128)S(1)}, s32[1,8,4096]{2,1,0:T(8,128)}, u32[]{:S(2)}) copy-start(s32[1,8,4096]{2,1,0:T(8,128)} %param.16) | copy-start | bytes 393220
  2.8 16.3 %copy-start.2 = (bf16[1,128,3,128]{3,1,2,0:T(8,128)(2,1)S(1)}, bf16[1,128,3,128]{3,1,2,0:T(8,128)(2,1)}, u32[]{:S(2)}) copy-start(bf16[1,128,3,128]{3,1,2,0:T(8,128)(2,1)} %param.27) | copy-start | bytes 294916
  2.8 16.3 %copy-start.4 = (bf16[128,128]{1,0:T(8,128)(2,1)S(1)}, bf16[128,128]{1,0:T(8,128)(2,1)}, u32[]{:S(2)}) copy-start(bf16[128,128]{1,0:T(8,128)(2,1)} %coupling.1) | copy-start | bytes 98308
  2.8 26.0 %all-to-all-start = ((bf16[64,8,512]{2,1,0:T(8,128)(2,1)}), bf16[64,8,512]{2,1,0:T(8,128)(2,1)S(1)}, u32[]{:S(2)}, u32[]{:S(2)}) async-start(bf16[64,8,512]{2,1,0:T(8,128)(2,1)} %bitcast.54), calls=%async_computation | async-start | bytes 1048576 | tf_op jit(solution)/shard_map/all_to_all | solution.py:305
  14.2 4.9 %copy-start.3 = (f32[1,128,128]{2,1,0:T(8,128)S(1)}, f32[1,128,128]{2,1,0:T(8,128)}, u32[]{:S(2)}) copy-start(f32[1,128,128]{2,1,0:T(8,128)} %param.25) | copy-start | bytes 196612
  14.2 7.4 %collective-permute-start.1 = (bf16[3,16,128]{2,1,0:T(8,128)(2,1)S(1)}, bf16[3,16,128]{2,1,0:T(8,128)(2,1)S(1)}, u32[]{:S(2)}, u32[]{:S(2)}) collective-permute-start(bf16[3,16,128]{2,1,0:T(8,128)(2,1)S(1)} %get-tuple-element.41), channel_id=1, source_target_pairs={{0,1},{2,3},{4,5},{6,7},{8,9},{10,11},{12,13},{14,15},{16,17},{18,... | collective-permute-start | bytes 36872 | tf_op jit(solution)/shard_map/ppermute | solution.py:296
  15.1 9.8 %collective-permute-start = (bf16[3,16,128]{2,1,0:T(8,128)(2,1)S(1)}, bf16[3,16,128]{2,1,0:T(8,128)(2,1)S(1)}, u32[]{:S(2)}, u32[]{:S(2)}) collective-permute-start(bf16[3,16,128]{2,1,0:T(8,128)(2,1)S(1)} %get-tuple-element.42), channel_id=1, source_target_pairs={{1,2},{3,4},{5,6},{7,8},{9,10},{11,12},{13,14},{15,16},{17,18},{19... | collective-permute-start | bytes 36872 | tf_op jit(solution)/shard_map/ppermute | solution.py:296
  19.0 0.7 %copy-start.6 = (s32[2,128]{1,0:T(2,128)S(1)}, s32[2,128]{1,0:T(2,128)}, u32[]{:S(2)}) copy-start(s32[2,128]{1,0:T(2,128)} %get-tuple-element.26.slots) | copy-start | bytes 3076
  19.0 0.7 %copy-start.7 = (f32[128]{0:T(128)S(1)}, f32[128]{0:T(128)}, u32[]{:S(2)}) copy-start(f32[128]{0:T(128)} %param.29) | copy-start | bytes 1540
  19.8 5.1 %copy-start.8 = (f32[1,6,4096]{2,0,1:T(1,128)S(1)}, f32[1,6,4096]{2,0,1:T(1,128)}, u32[]{:S(2)}) copy-start(f32[1,6,4096]{2,0,1:T(1,128)} %param.17) | copy-start | bytes 294916
  19.8 5.1 %copy-start.9 = (f32[1,3,4096]{2,0,1:T(1,128)S(1)}, f32[1,3,4096]{2,0,1:T(1,128)}, u32[]{:S(2)}) copy-start(f32[1,3,4096]{2,0,1:T(1,128)} %param.20) | copy-start | bytes 147460
  19.8 5.1 %copy-start.10 = (f32[1,4096]{1,0:T(1,128)S(1)}, f32[1,4096]{1,0:T(1,128)}, u32[]{:S(2)}) copy-start(f32[1,4096]{1,0:T(1,128)} %param.18) | copy-start | bytes 49156
  19.8 5.1 %copy-start.11 = (f32[1,4096]{1,0:T(1,128)S(1)}, f32[1,4096]{1,0:T(1,128)}, u32[]{:S(2)}) copy-start(f32[1,4096]{1,0:T(1,128)} %param.19) | copy-start | bytes 49156
  19.8 9.0 %collective-permute-start.4 = (f32[4,128,128]{2,1,0:T(8,128)S(1)}, f32[4,128,128]{2,1,0:T(8,128)S(1)}, u32[]{:S(2)}, u32[]{:S(2)}) collective-permute-start(f32[4,128,128]{2,1,0:T(8,128)S(1)} %get-tuple-element.27), channel_id=1, source_target_pairs={{0,64},{64,0},{1,65},{65,1},{2,66},{66,2},{3,67},{67,3},{4,68},{68... | collective-permute-start | bytes 786440 | tf_op jit(solution)/shard_map/ppermute | solution.py:300
  30.0 20.5 %all-to-all-start.1 = ((bf16[64,8,384]{2,1,0:T(8,128)(2,1)}), bf16[64,8,384]{2,1,0:T(8,128)(2,1)S(1)}, u32[]{:S(2)}, u32[]{:S(2)}) async-start(bf16[64,8,384]{2,1,0:T(8,128)(2,1)} %bitcast.25), calls=%async_computation.1 | async-start | bytes 786432 | tf_op jit(solution)/shard_map/all_to_all | solution.py:305
  39.9 9.9 %collective-permute-start.5 = (f32[3,128,128]{2,1,0:T(8,128)S(1)}, f32[3,128,128]{2,1,0:T(8,128)S(1)}, u32[]{:S(2)}, u32[]{:S(2)}) collective-permute-start(f32[3,128,128]{2,1,0:T(8,128)S(1)} %get-tuple-element.30), channel_id=1, source_target_pairs={{0,64},{64,0},{1,65},{65,1},{2,66},{66,2},{3,67},{67,3},{4,68},{68... | collective-permute-start | bytes 589832 | tf_op jit(solution)/shard_map/ppermute | solution.py:300
  40.0 9.8 %collective-permute-start.2 = (bf16[3,16,128]{2,1,0:T(8,128)(2,1)S(1)}, bf16[3,16,128]{2,1,0:T(8,128)(2,1)S(1)}, u32[]{:S(2)}, u32[]{:S(2)}) collective-permute-start(bf16[3,16,128]{2,1,0:T(8,128)(2,1)S(1)} %get-tuple-element.23), channel_id=1, source_target_pairs={{1,2},{3,4},{5,6},{7,8},{9,10},{11,12},{13,14},{15,16},{17,18},{19... | collective-permute-start | bytes 36872 | tf_op jit(solution)/shard_map/ppermute | solution.py:296
  43.5 6.3 %collective-permute-start.3 = (bf16[3,16,128]{2,1,0:T(8,128)(2,1)S(1)}, bf16[3,16,128]{2,1,0:T(8,128)(2,1)S(1)}, u32[]{:S(2)}, u32[]{:S(2)}) collective-permute-start(bf16[3,16,128]{2,1,0:T(8,128)(2,1)S(1)} %get-tuple-element.24), channel_id=1, source_target_pairs={{0,1},{2,3},{4,5},{6,7},{8,9},{10,11},{12,13},{14,15},{16,17},{18,... | collective-permute-start | bytes 36872 | tf_op jit(solution)/shard_map/ppermute | solution.py:296
